TPU v7x, 32 devices: a whole 2x2x4 slice. The times are simulated.
32 devices in a mesh: dp: 16 (over z, y, x), seq: 2 (over core).
Axes of the slice: x: 2, y: 2, z: 4, core: 2. Of those that a mesh axis runs over, the one named last changes fastest.
Arguments:
- tokens: bfloat16 [16, 2048, 1120], P('dp', 'seq'), may hold values from -6 to 6
- cotangent: bfloat16 [16, 2048, 1120], P('dp', 'seq'), may hold values from -6 to 6
- pad_mask: int32 [16, 2048], P('dp', 'seq'), may hold values from 0 to 1, as said below
- prefix_len: int32 [16], P('dp'), may hold values from 1 to 128
- norm_gains: float32 [2, 1120], replicated, may hold values from 0.5 to 1.5
- norm_shifts: float32 [2, 1120], replicated, may hold values from -1.8 to 1.8
- owner_map: int32 [192], replicated, may hold values from 0 to 191, as said below
- weight_copy: bfloat16 [192, 280, 280], P('dp'), may hold values from -1.8090681 to 1.8090681
- master: float32 [192, 280, 280], P('dp'), may hold values from -1.8090681 to 1.8090681
- average_weights: float32 [192, 280, 280], P('dp'), may hold values from -1.8090681 to 1.8090681
- stat_left: float32 [192, 280, 280], P('dp'), may hold values from -16.290909 to 36.654545, as said below
- stat_right: float32 [192, 280, 280], P('dp'), may hold values from -16.290909 to 36.654545, as said below
- root_left: float32 [192, 280, 280], P('dp'), may hold values from -3 to 5, as said below
- root_right: float32 [192, 280, 280], P('dp'), may hold values from -3 to 5, as said below
Outputs:
- block_out: bfloat16 [16, 2048, 1120], P('dp', 'seq')
- grad_input: float32 [16, 2048, 1120], P('dp', 'seq')
- norm_grad: float32 [4, 1120], replicated
- new_norms: float32 [4, 1120], replicated
- slot_grad: float32 [192, 280, 280], P('dp')
- new_left: float32 [192, 280, 280], P('dp')
- new_right: float32 [192, 280, 280], P('dp')
- new_master: float32 [192, 280, 280], P('dp')
- new_copy: bfloat16 [192, 280, 280], P('dp')
- new_average: float32 [192, 280, 280], P('dp')
Inputs may be any that keep to these rules, and one draw needn't show every extreme that they name: `pad_mask`: in each cell the ones come first, 512 or more of them; some cell has no zeros. `owner_map`: each block number appears once. `stat_left`: Symmetric. `stat_right`: Symmetric. `root_left`: Symmetric. `root_right`: Symmetric.
All inputs are finite; a program needn't handle non-finite values.
Results may differ from a plain program's by a relative error of at most 0.0085.
Values may be sent and summed in bfloat16 or wider, within the bound.
A program may use at most 448 MiB of HBM per device.

v0:
```python
import math

import jax
import jax.numpy as jnp
from jax import lax
from jax.sharding import PartitionSpec as P

HEADS = 20
GB = 256
PREFIX = 128


highest = lax.Precision.HIGHEST


def spread(block, axis, holder):
    block = jnp.where(lax.axis_index(axis) == holder, block, jnp.zeros_like(block))
    return lax.psum(block, axis)


def layer_norm(values, gain_row, shift_row):
    average = jnp.mean(values, axis=-1, keepdims=True)
    centred = values - average
    variance = jnp.mean(centred * centred, axis=-1, keepdims=True)
    return centred * lax.rsqrt(variance + 1e-05) * gain_row + shift_row


def gelu_tanh(values):
    return jax.nn.gelu(values, approximate=True)


def assemble(pieces, row_blocks, col_blocks):
    block_size = pieces.shape[-1]
    return (
        pieces.reshape(row_blocks, col_blocks, block_size, block_size)
        .transpose(0, 2, 1, 3)
        .reshape(row_blocks * block_size, col_blocks * block_size)
    )


def split_blocks(matrix, block_size):
    row_count, col_count = matrix.shape
    return (
        matrix.reshape(row_count // block_size, block_size, col_count // block_size, block_size)
        .transpose(0, 2, 1, 3)
        .reshape(-1, block_size, block_size)
    )


def matmul(left, right):
    return jnp.dot(left, right, preferred_element_type=jnp.float32)


def local(
    tokens,
    cotangent,
    pad_mask,
    prefix_len,
    norm_gains,
    norm_shifts,
    owner_map,
    weight_copy,
    master,
    average_weights,
    stat_left,
    stat_right,
    root_left,
    root_right,
):
    cell_count, group_len, features = tokens.shape
    row_count = cell_count * group_len
    head_size = features // HEADS
    per_group = group_len // GB
    score_scale = head_size ** (-0.5)
    slots = lax.all_gather(weight_copy, "dp", axis=0, tiled=True)
    block_count = slots.shape[0]
    block_size = slots.shape[-1]
    row_blocks = features // block_size
    col_blocks = (block_count - 4 * row_blocks * row_blocks) // (2 * row_blocks)
    square = row_blocks * row_blocks
    inverse = (
        jnp.zeros((block_count,), jnp.int32)
        .at[owner_map]
        .set(jnp.arange(block_count, dtype=jnp.int32))
    )
    blocks = jnp.take(slots, inverse, axis=0)
    w_query = assemble(blocks[0:square], row_blocks, row_blocks)
    w_key = assemble(blocks[square : 2 * square], row_blocks, row_blocks)
    w_value = assemble(blocks[2 * square : 3 * square], row_blocks, row_blocks)
    w_out = assemble(blocks[3 * square : 4 * square], row_blocks, row_blocks)
    w_up = assemble(
        blocks[4 * square : 4 * square + row_blocks * col_blocks], row_blocks, col_blocks
    )
    w_down = assemble(blocks[4 * square + row_blocks * col_blocks :], col_blocks, row_blocks)
    inputs = tokens.astype(jnp.float32).reshape(row_count, features)
    normed_one, norm_one_back = jax.vjp(layer_norm, inputs, norm_gains[0], norm_shifts[0])
    normed_in = normed_one.astype(jnp.bfloat16)
    queries = matmul(normed_in, w_query).astype(jnp.bfloat16)
    key_rows = matmul(normed_in, w_key).astype(jnp.bfloat16)
    value_rows = matmul(normed_in, w_value).astype(jnp.bfloat16)
    block_shape = (cell_count, per_group, GB, HEADS, head_size)
    query_blocks = queries.reshape(block_shape)
    key_blocks = key_rows.reshape(block_shape)
    value_blocks = value_rows.reshape(block_shape)
    key_cells = key_rows.reshape(cell_count, group_len, HEADS, head_size)
    value_cells = value_rows.reshape(cell_count, group_len, HEADS, head_size)
    prefix_keys, prefix_values = (
        spread(key_cells[:, :PREFIX], "seq", 0),
        spread(value_cells[:, :PREFIX], "seq", 0),
    )
    seq_index = lax.axis_index("seq")
    position = seq_index * group_len + jnp.arange(group_len, dtype=jnp.int32)
    alive_keys = jnp.where(
        position[None, :] < PREFIX, position[None, :] < prefix_len[:, None], pad_mask == 1
    )
    prefix_alive = jnp.arange(PREFIX, dtype=jnp.int32)[None, :] < prefix_len[:, None]
    offsets = jnp.arange(GB)
    local_seen = alive_keys.reshape(cell_count, per_group, 1, 1, GB) & (
        offsets[:, None] >= offsets[None, :]
    )
    later_block = seq_index * per_group + jnp.arange(per_group) > 0
    prefix_seen = prefix_alive[:, None, None, None, :] & later_block[None, :, None, None, None]
    visible = jnp.concatenate(
        [jnp.broadcast_to(prefix_seen, (cell_count, per_group, 1, GB, PREFIX)), local_seen], axis=-1
    )

    def score_rows():
        raw_prefix = jnp.einsum(
            "cnqhd,ckhd->cnhqk", query_blocks, prefix_keys, preferred_element_type=jnp.float32
        )
        raw_local = jnp.einsum(
            "cnqhd,cnkhd->cnhqk", query_blocks, key_blocks, preferred_element_type=jnp.float32
        )
        return jnp.where(
            visible, jnp.concatenate([raw_prefix, raw_local], axis=-1) * score_scale, -1e30
        )

    scores = score_rows()
    row_max = jnp.max(scores, axis=-1, keepdims=True)
    log_total = row_max + jnp.log(jnp.sum(jnp.exp(scores - row_max), axis=-1, keepdims=True))
    weights_low = jnp.exp(scores - log_total).astype(jnp.bfloat16)
    attended = jnp.einsum(
        "cnhqk,ckhd->cnqhd",
        weights_low[..., :PREFIX],
        prefix_values,
        preferred_element_type=jnp.float32,
    )
    attended = attended + jnp.einsum(
        "cnhqk,cnkhd->cnqhd",
        weights_low[..., PREFIX:],
        value_blocks,
        preferred_element_type=jnp.float32,
    )
    attended_low = attended.reshape(row_count, features).astype(jnp.bfloat16)
    middle = inputs + matmul(attended_low, w_out)
    normed_two, norm_two_back = jax.vjp(layer_norm, middle, norm_gains[1], norm_shifts[1])
    normed_mid = normed_two.astype(jnp.bfloat16)
    up_pre = matmul(normed_mid, w_up)
    activated, gelu_back = jax.vjp(gelu_tanh, up_pre)
    activated_low = activated.astype(jnp.bfloat16)
    block_out = (
        (middle + matmul(activated_low, w_down))
        .astype(jnp.bfloat16)
        .reshape(cell_count, group_len, features)
    )
    grad_rows = cotangent.astype(jnp.float32).reshape(row_count, features)
    grad_low = cotangent.reshape(row_count, features)
    grad_down = matmul(activated_low.T, grad_low)
    grad_act = matmul(grad_low, w_down.T)
    grad_pre = gelu_back(grad_act)[0].astype(jnp.bfloat16)
    grad_up = matmul(normed_mid.T, grad_pre)
    grad_mid_in = matmul(grad_pre, w_up.T)
    grad_middle_n, grad_gain_two, grad_shift_two = norm_two_back(grad_mid_in)
    grad_middle = grad_rows + grad_middle_n
    grad_branch = grad_middle.astype(jnp.bfloat16)
    grad_out = matmul(attended_low.T, grad_branch)
    grad_att = matmul(grad_branch, w_out.T).astype(jnp.bfloat16).reshape(block_shape)
    key_weights = jnp.exp(score_rows() - log_total)
    weights_again = key_weights.astype(jnp.bfloat16)
    grad_prob = jnp.concatenate(
        [
            jnp.einsum(
                "cnqhd,ckhd->cnhqk", grad_att, prefix_values, preferred_element_type=jnp.float32
            ),
            jnp.einsum(
                "cnqhd,cnkhd->cnhqk", grad_att, value_blocks, preferred_element_type=jnp.float32
            ),
        ],
        axis=-1,
    )
    grad_score = key_weights * (
        grad_prob - jnp.sum(key_weights * grad_prob, axis=-1, keepdims=True)
    )
    grad_raw = (grad_score * score_scale).astype(jnp.bfloat16)
    grad_raw_prefix = grad_raw[..., :PREFIX]
    grad_raw_local = grad_raw[..., PREFIX:]
    grad_query = jnp.einsum(
        "cnhqk,ckhd->cnqhd", grad_raw_prefix, prefix_keys, preferred_element_type=jnp.float32
    )
    grad_query = grad_query + jnp.einsum(
        "cnhqk,cnkhd->cnqhd", grad_raw_local, key_blocks, preferred_element_type=jnp.float32
    )
    grad_key = jnp.einsum(
        "cnhqk,cnqhd->cnkhd", grad_raw_local, query_blocks, preferred_element_type=jnp.float32
    )
    grad_value = jnp.einsum(
        "cnhqk,cnqhd->cnkhd",
        weights_again[..., PREFIX:],
        grad_att,
        preferred_element_type=jnp.float32,
    )
    grad_key_pre = jnp.einsum(
        "cnhqk,cnqhd->ckhd", grad_raw_prefix, query_blocks, preferred_element_type=jnp.float32
    )
    grad_value_pre = jnp.einsum(
        "cnhqk,cnqhd->ckhd",
        weights_again[..., :PREFIX],
        grad_att,
        preferred_element_type=jnp.float32,
    )
    summed_key, summed_value = lax.psum((grad_key_pre, grad_value_pre), "seq")
    is_owner = (seq_index == 0).astype(jnp.float32)
    grad_key = (
        grad_key.reshape(cell_count, group_len, features)
        .at[:, :PREFIX]
        .add(is_owner * summed_key.reshape(cell_count, PREFIX, features))
    )
    grad_value = (
        grad_value.reshape(cell_count, group_len, features)
        .at[:, :PREFIX]
        .add(is_owner * summed_value.reshape(cell_count, PREFIX, features))
    )
    query_grad_low = grad_query.reshape(row_count, features).astype(jnp.bfloat16)
    key_grad_low = grad_key.reshape(row_count, features).astype(jnp.bfloat16)
    value_grad_low = grad_value.reshape(row_count, features).astype(jnp.bfloat16)
    grad_wq = matmul(normed_in.T, query_grad_low)
    grad_wk = matmul(normed_in.T, key_grad_low)
    grad_wv = matmul(normed_in.T, value_grad_low)
    grad_normed = (
        matmul(query_grad_low, w_query.T)
        + matmul(key_grad_low, w_key.T)
        + matmul(value_grad_low, w_value.T)
    )
    grad_in_n, grad_gain_one, grad_shift_one = norm_one_back(grad_normed)
    grad_input = (grad_middle + grad_in_n).reshape(cell_count, group_len, features)
    grad_scale = 1.0 / math.sqrt(row_count * lax.axis_size("dp") * lax.axis_size("seq"))
    norm_terms = (
        jnp.stack([grad_gain_one, grad_shift_one, grad_gain_two, grad_shift_two]) * grad_scale
    )
    norm_grad = lax.psum(norm_terms, ("dp", "seq"))
    params = jnp.stack([norm_gains[0], norm_shifts[0], norm_gains[1], norm_shifts[1]])
    new_norms = params - 0.1 * norm_grad * lax.rsqrt(jnp.mean(norm_grad * norm_grad) + 1e-06)
    grad_blocks = (
        jnp.concatenate(
            [
                split_blocks(matrix, block_size)
                for matrix in (grad_wq, grad_wk, grad_wv, grad_out, grad_up, grad_down)
            ],
            axis=0,
        )
        * grad_scale
    )
    ordered = jnp.take(grad_blocks, owner_map, axis=0)
    owned_part = lax.psum_scatter(ordered, "dp", scatter_dimension=0, tiled=True)
    slot_grad = lax.psum(owned_part, "seq")
    new_left = (
        0.5 * stat_left
        + 0.5 * jnp.einsum("sij,skj->sik", slot_grad, slot_grad, precision=highest) / block_size
    )
    new_right = (
        0.5 * stat_right
        + 0.5 * jnp.einsum("sji,sjk->sik", slot_grad, slot_grad, precision=highest) / block_size
    )
    right_part = jnp.einsum("sij,sjk->sik", slot_grad, root_right, precision=highest)
    precond = jnp.einsum("sij,sjk->sik", root_left, right_part, precision=highest)
    new_master = master - 0.03 * precond
    new_copy = new_master.astype(jnp.bfloat16)
    new_average = 0.8 * average_weights + 0.2 * new_master
    return (
        block_out,
        grad_input,
        norm_grad,
        new_norms,
        slot_grad,
        new_left,
        new_right,
        new_master,
        new_copy,
        new_average,
    )


def solution(mesh):
    in_specs = (
        P("dp", "seq", None),
        P("dp", "seq", None),
        P("dp", "seq"),
        P("dp"),
        P(),
        P(),
        P(),
        P("dp", None, None),
        P("dp", None, None),
        P("dp", None, None),
        P("dp", None, None),
        P("dp", None, None),
        P("dp", None, None),
        P("dp", None, None),
    )
    out_specs = (
        P("dp", "seq", None),
        P("dp", "seq", None),
        P(),
        P(),
        P("dp", None, None),
        P("dp", None, None),
        P("dp", None, None),
        P("dp", None, None),
        P("dp", None, None),
        P("dp", None, None),
    )
    return jax.shard_map(local, mesh=mesh, in_specs=in_specs, out_specs=out_specs, check_vma=False)
```

profile of v0, /device:TPU:0, one launch (start us, length us, event | category | flops | bytes accessed | tf_op | source)
XLA Modules:
  0.0 2638.7 jit_solution(1818044440257464110)
XLA Ops:
  16.7 420.8 %all-gather.2.cloned.1.call-done = bf16[192,280,280]{2,1,0:T(8,128)(2,1)} async-done(((bf16[12,280,280]{2,1,0:T(8,128)(2,1)}), bf16[192,280,280]{2,1,0:T(8,128)(2,1)}) %all-gather.2.cloned.1.call-update) | async-done | bytes 30105616 | tf_op jit(solution)/shard_map/all_gather | solution.py:75
  437.5 28.3 %gather_fusion = bf16[192,280,280]{2,1,0:T(8,128)(2,1)} fusion(bf16[192,280,280]{2,1,0:T(8,128)(2,1)} %all-gather.2.cloned.1.call-done, s32[1024]{0:T(1024)S(1)} %pad_clamp_fusion.1), kind=kCustom, calls=%fused_computation | custom fusion | bytes 60211968 | tf_op jit(solution)/shard_map/jit(_take)/gather | solution.py:86
  465.8 28.1 %broadcast_select_fusion.1 = bf16[192,280,280]{2,1,0:T(8,128)(2,1)} fusion(bf16[192,280,280]{2,1,0:T(8,128)(2,1)} %gather_fusion, pred[192]{0:T(512)(128)(4,1)S(1)} %compare_and_fusion.1), kind=kLoop, calls=%fused_computation.5 | loop fusion | flops 15052800 | bytes 60211392 | tf_op jit(solution)/shard_map/jit(_take)/select_n | solution.py:86
  493.9 9.3 fusion.111
  503.2 21.0 fusion.110
  527.4 6.3 reshape.760
  538.7 6.3 reshape.764
  545.0 6.7 convolution_convert_fusion.3
  551.7 5.1 convolution_convert_fusion.2
  559.9 6.3 reshape.768
  569.7 6.6 convolution_convert_fusion.1
  576.3 5.6 reshape.772
  589.3 5.9 copy.248
  595.2 6.3 reshape.775
  601.5 22.4 copy.115
  623.9 21.1 reshape.779
  644.9 14.3 copy.247
  659.3 21.4 reshape.777
  680.7 11.6 convolution_bitcast_fusion.1
  695.0 13.9 fusion.108
  709.7 6.5 exponential_reduce_fusion
  716.3 9.9 fusion.1
  726.2 5.2 fusion.22
  741.5 26.2 fusion.16
  767.8 31.0 %fusion.8 = bf16[1024,4480]{1,0:T(8,128)(2,1)} fusion(f32[1024,4480]{1,0:T(8,128)} %get-tuple-element.100, bf16[4480,1120]{0,1:T(8,128)(2,1)} %reshape.779, bf16[1,1024,1120]{1,2,0:T(8,128)(2,1)S(1)} %copy-done.12), kind=kOutput, calls=%fused_computation.23 | convolution fusion | flops 10367795200 | bytes 39854080 | tf_op jit(solution)/shard_map/dot_general | solution.py:51
  798.8 19.8 multiply_reduce_fusion.1
  832.3 9.6 convolution_bitcast_fusion.4
  842.0 8.6 convolution_bitcast_fusion
  850.6 5.4 convolution_bitcast_fusion.2
  856.0 5.2 fusion.74
  861.1 20.7 multiply_reduce_fusion
  881.8 22.1 multiply_convert_fusion
  903.9 5.5 copy-done.1
  912.1 8.7 fusion.20
  920.8 9.6 convolution_bitcast_fusion.5
  930.5 18.1 fusion.103
  948.6 5.1 copy.134
  953.7 6.5 reshape.790
  977.7 6.5 reshape.787
  988.5 28.5 %reshape.801 = f32[4,280,16,280]{3,2,1,0:T(8,128)} reshape(f32[1120,4480]{1,0:T(8,128)} %fusion.103) | data formatting | bytes 40140800 | tf_op jit(solution)/shard_map/reshape | solution.py:44
  1017.1 27.0 %copy.138 = f32[4,280,16,280]{3,1,2,0:T(8,128)} copy(f32[4,280,16,280]{3,2,1,0:T(8,128)} %reshape.801) | data formatting | bytes 40140800 | tf_op jit(solution)/shard_map/reshape | solution.py:44
  1044.0 12.7 copy.139
  1056.8 20.0 fusion.117
  1081.6 5.8 fusion.116
  1091.6 5.7 fusion.120
  1121.3 7.6 fusion.115
  1132.6 6.8 constant_dynamic-update-slice_fusion.3
  1139.4 6.4 constant_dynamic-update-slice_fusion.2
  1145.9 9.4 constant_dynamic-update-slice_fusion.1
  1155.3 20.5 constant_dynamic-update-slice_fusion
  1175.8 55.9 %broadcast_multiply_fusion = f32[192,280,280]{2,1,0:T(8,128)} fusion(f32[192,280,280]{2,1,0:T(8,128)} %constant_dynamic-update-slice_fusion), kind=kLoop, calls=%fused_computation.4 | loop fusion | flops 15052800 | bytes 120422400 | tf_op jit(solution)/shard_map/mul | solution.py:254
  1231.7 56.4 %gather_fusion.1 = f32[192,280,280]{2,1,0:T(8,128)} fusion(f32[192,280,280]{2,1,0:T(8,128)} %broadcast_multiply_fusion, s32[1024]{0:T(1024)} %pad_clamp_fusion), kind=kCustom, calls=%fused_computation.1 | custom fusion | bytes 120423168 | tf_op jit(solution)/shard_map/jit(_take)/gather | solution.py:263
  1288.1 54.1 %broadcast_select_fusion = f32[192,280,280]{2,1,0:T(8,128)} fusion(f32[192,280,280]{2,1,0:T(8,128)} %gather_fusion.1, pred[192]{0:T(512)(128)(4,1)S(1)} %copy-done.57), kind=kLoop, calls=%fused_computation.3 | loop fusion | flops 15052800 | bytes 120422592 | tf_op jit(solution)/shard_map/jit(_take)/select_n | solution.py:263
  1342.2 1134.6 %reduce-scatter.2.cloned.1.call-done = f32[12,280,280]{2,1,0:T(8,128)} async-done(((f32[192,280,280]{2,1,0:T(8,128)}), f32[12,280,280]{2,1,0:T(8,128)}) %reduce-scatter.2.cloned.1.call-update) | async-done | bytes 3763216 | tf_op jit(solution)/shard_map/reduce_scatter | solution.py:264
  2476.8 6.1 copy.143
  2483.0 6.5 copy.142
  2489.6 19.8 fusion.54
  2509.4 39.9 %psum.46 = f32[4,1120]{1,0:T(4,128)S(1)} all-reduce(f32[4,1120]{1,0:T(4,128)S(1)} %maximum_multiply_fusion.1), channel_id=1, replica_groups=mesh['dp'=16,'seq'=2] {'dp','seq'}, use_global_device_ids=true, to_apply=%region_20.21 | all-reduce | flops 4480 | bytes 35840 | tf_op jit(solution)/shard_map/psum | solution.py:250
  2551.3 14.1 fusion.118
  2565.4 17.3 multiply_add_fusion
  2582.7 6.1 copy.144
  2591.6 6.2 copy.146
  2597.8 16.9 multiply_add_fusion.2
  2614.7 14.9 multiply_add_fusion.1
  (258 shorter events, 125.6 us)
Async XLA Ops:
  7.2 6.6 copy-start.5
  7.2 8.3 copy-start.51
  7.2 8.2 copy-start.52
  7.2 430.3 %all-gather.2.cloned.1.call-start = ((), (), s32[]{:S(2)}) async-start(), calls=%async_computation.1 | async-start | bytes 43868160 | tf_op jit(solution)/shard_map/all_gather | solution.py:75
  7.9 684.3 %all-reduce.10.cloned.1.call-start = ((), (), s32[]{:S(2)}) async-start(), calls=%async_computation.5 | async-start | bytes 1146880 | tf_op jit(solution)/shard_map/psum | solution.py:18
  14.2 555.5 %copy-start.34 = (f32[1024]{0:T(1024)}, f32[1024]{0:T(1024)S(1)}, u32[]{:S(2)}) copy-start(f32[1024]{0:T(1024)S(1)} %broadcast_multiply_fusion.4) | copy-start | bytes 12292
  15.5 554.3 %copy-start.40 = (f32[1024]{0:T(1024)}, f32[1024]{0:T(1024)S(1)}, u32[]{:S(2)}) copy-start(f32[1024]{0:T(1024)S(1)} %fusion.95) | copy-start | bytes 12292
  16.7 553.0 %copy-start.32 = (f32[1120]{0:T(1024)}, f32[1120]{0:T(1024)S(1)}, u32[]{:S(2)}) copy-start(f32[1120]{0:T(1024)S(1)} %get-tuple-element.104) | copy-start | bytes 13444
  16.7 553.0 %copy-start.42 = (f32[1120]{0:T(1024)}, f32[1120]{0:T(1024)S(1)}, u32[]{:S(2)}) copy-start(f32[1120]{0:T(1024)S(1)} %get-tuple-element.73) | copy-start | bytes 13444
  545.0 6.7 copy-start.16
  569.7 517.7 %all-reduce.8.cloned.1.call-start = ((), (), s32[]{:S(2)}) async-start(), calls=%async_computation.4 | async-start | bytes 2293760 | tf_op jit(solution)/shard_map/psum | solution.py:221
  589.3 103.0 %copy-start.2 = (bf16[4,256,20,56]{1,0,3,2:T(4,128)(2,1)}, bf16[4,256,20,56]{1,0,3,2:T(4,128)(2,1)S(1)}, u32[]{:S(2)}) copy-start(bf16[4,256,20,56]{1,0,3,2:T(4,128)(2,1)S(1)} %reshape.769) | copy-start | bytes 6881284
  692.3 16.6 slice-start
  692.3 16.6 slice-start.1
  695.0 21.3 copy-start
  695.0 14.0 slice-start.2
  695.0 14.0 slice-start.3
  695.0 14.7 slice-start.4
  716.3 9.9 copy-start.10
  740.9 77.7 %copy-start.8 = (f32[1024,1120]{0,1:T(8,128)}, f32[1024,1120]{0,1:T(8,128)S(1)}, u32[]{:S(2)}) copy-start(f32[1024,1120]{0,1:T(8,128)S(1)} %get-tuple-element.95) | copy-start | bytes 13762564
  741.5 26.3 copy-start.12
  832.3 9.6 copy-start.11
  881.8 27.6 %copy-start.3 = (bf16[4,256,20,56]{1,0,3,2:T(4,128)(2,1)S(1)}, bf16[4,256,20,56]{1,0,3,2:T(4,128)(2,1)}, u32[]{:S(2)}) copy-start(bf16[4,256,20,56]{1,0,3,2:T(4,128)(2,1)} %copy-done.2) | copy-start | bytes 6881284
  912.1 18.3 slice-start.16
  920.8 9.6 slice-start.17
  920.8 9.6 copy-start.54
  920.8 27.8 %slice-start.18 = ((s8[4587520]{0:T(1024)(128)(4,1)}), s8[4194304]{0:T(1024)(128)(4,1)S(1)}, s32[]{:S(2)}) async-start(s8[4587520]{0:T(1024)(128)(4,1)} %bitcast.354), calls=%async_computation.24 | async-start | bytes 8388608
  930.4 18.1 slice-start.19
  960.2 12.5 slice-start.20
  964.7 8.0 slice-start.21
  1044.0 12.7 copy-start.13
  1056.7 1420.1 %reduce-scatter.2.cloned.1.call-start = ((), (), s32[]{:S(2)}) async-start(), calls=%async_computation.2 | async-start | bytes 87736320 | tf_op jit(solution)/shard_map/reduce_scatter | solution.py:264
  1056.8 20.0 copy-start.17
  1056.8 20.0 copy-start.22
  1089.6 9.2 slice-start.22
  1091.6 5.8 copy-start.24
  1091.6 7.2 copy-start.7
  1091.6 7.2 copy-start.15
  1091.6 7.2 copy-start.33
  1091.6 7.2 copy-start.35
  1091.6 7.2 slice-start.23
  1097.4 8.6 slice-start.14
  1098.9 7.1 slice-start.15
  1110.3 7.1 copy-start.28
  1121.3 24.5 slice-start.7
  1121.3 24.5 slice-start.8
  1121.3 24.5 slice-start.9
  1128.9 16.9 slice-start.10
  1132.6 13.2 slice-start.11
  1132.6 13.2 slice-start.12
  1139.4 6.4 slice-start.13
  1231.7 56.4 %copy-start.57 = (pred[192]{0:T(512)(128)(4,1)S(1)}, pred[192]{0:T(512)(128)(4,1)}, u32[]{:S(2)}) copy-start(pred[192]{0:T(512)(128)(4,1)} %compare_and_fusion) | copy-start | bytes 580
  1342.2 1209.1 %all-reduce.6.cloned.1.call-start = ((), (), s32[]{:S(2)}) async-start(), calls=%async_computation.3 | async-start | bytes 10321920 | tf_op jit(solution)/shard_map/psum | solution.py:265
  2483.0 6.5 copy-start.56
  2483.0 6.5 copy-start.55
  2489.5 19.9 copy-start.46
  2489.5 19.9 copy-start.45
  2489.5 61.1 %copy-start.47 = (f32[1,1120]{1,0:T(1,128)S(1)}, f32[1,1120]{1,0:T(1,128)}, u32[]{:S(2)}) copy-start(f32[1,1120]{1,0:T(1,128)} %get-tuple-element.91) | copy-start | bytes 13444
  2489.5 61.1 %copy-start.48 = (f32[1,1120]{1,0:T(1,128)S(1)}, f32[1,1120]{1,0:T(1,128)}, u32[]{:S(2)}) copy-start(f32[1,1120]{1,0:T(1,128)} %get-tuple-element.93) | copy-start | bytes 13444
  2489.6 61.1 %copy-start.49 = (f32[1,1120]{1,0:T(1,128)S(1)}, f32[1,1120]{1,0:T(1,128)}, u32[]{:S(2)}) copy-start(f32[1,1120]{1,0:T(1,128)} %get-tuple-element.102) | copy-start | bytes 13444
  2489.6 61.1 %copy-start.50 = (f32[1,1120]{1,0:T(1,128)S(1)}, f32[1,1120]{1,0:T(1,128)}, u32[]{:S(2)}) copy-start(f32[1,1120]{1,0:T(1,128)} %get-tuple-element.103) | copy-start | bytes 13444
  2549.3 16.1 copy-start.31
  2591.6 23.1 slice-start.5
  2597.8 16.9 slice-start.6
  (23 other events, 84.3 us)
Sparse Core Ops, SparseCore 0:
  10.8 426.5 all-gather.1
  569.8 17.0 all-reduce.9
  1056.8 18.0 all-reduce.7
  1342.3 1134.4 reduce-scatter.1
  2479.3 29.0 all-reduce.5
where the time goes:
time: 2650 us; the launch traced here: 2640 us
  waiting for transfers between devices  1560 us (59%)
  local copies, waits for them, and re-layouts  452 us (17%)
  matrix products  338 us (13%)
  other arithmetic  236 us (9%)
  blocking collectives  39.9 us (2%)
    reduce_scatter x1, waiting for transfers between devices, local(): lax.psum_scatter(ordered, 'dp', scatter_dimension=0, tiled=True)  1130 us
    all_gather x1, waiting for transfers between devices, local(): slots = lax.all_gather(weight_copy, 'dp', axis=0, tiled=True)  421 us
    dot_general x18, matrix products, matmul(): return jnp.dot(left, right, preferred_element_type=jnp.float32)  197 us
    unnamed x179, local copies, waits for them, and re-layouts  81.6 us
    reshape x6, local copies, waits for them, and re-layouts, assemble(): return pieces.reshape(row_blocks, col_blocks, block_size, block_size).tra...  67.7 us
    gather x1, local copies, waits for them, and re-layouts, local(): ordered = jnp.take(grad_blocks, owner_map, axis=0)  56.4 us
    mul x1, other arithmetic, local(): jnp.concatenate([split_blocks(matrix, block_size) for matrix in (grad_wq,...  55.9 us
    reshape x2, local copies, waits for them, and re-layouts, split_blocks(): matrix.reshape(row_count // block_size, block_size, col_count // block_si...  55.5 us
  transfers between devices with their start and end apart: 5, of which 2 were waited for; matrix products, arithmetic and copies ran while one was open for 7% of the time, Pallas kernels for 0%

commit v1 on v0

v1 whole, which is shorter than its diff:
```python
import functools
import math

import jax
import jax.numpy as jnp
from jax import lax
from jax.experimental import pallas as pl
from jax.experimental.pallas import tpu as pltpu
from jax.sharding import PartitionSpec as P

HEADS = 20
GB = 256
PREFIX = 128
HALF = GB // 2
MESH = pl.DeviceIdType.MESH
BF16 = jnp.bfloat16
F32 = jnp.float32

MAIN = 256
RUN = 32


def runs(size):
    rest, per_tile = size - MAIN, 128 // (size - MAIN)
    places = []
    for index in range(-(-size // RUN)):
        lane = 128 * (index // per_tile) + rest * (index % per_tile)
        places.append((RUN * index, min(RUN, size - RUN * index), lane))
    assert places[-1][2] + rest <= MAIN
    return places


def pack_tail(block):
    size = block.shape[0]
    rest = size - MAIN
    pieces, lane = [], 0
    for row, count, start in runs(size):
        if start > lane:
            pieces.append(jnp.zeros((RUN, start - lane), block.dtype))
        piece = block[row : row + count, MAIN:]
        if count < RUN:
            piece = jnp.concatenate([piece, jnp.zeros((RUN - count, rest), block.dtype)], axis=0)
        pieces.append(piece)
        lane = start + rest
    if lane < MAIN:
        pieces.append(jnp.zeros((RUN, MAIN - lane), block.dtype))
    return jnp.concatenate(pieces, axis=1)


def unpack(packed):
    size = packed.shape[0] - RUN
    rest = size - MAIN
    low = packed[size:]
    tail = [low[:count, lane : lane + rest] for _, count, lane in runs(size)]
    return jnp.concatenate([packed[:size], jnp.concatenate(tail, axis=0)], axis=1)


def tn(left, right):
    return lax.dot_general(left, right, (((0,), (0,)), ((), ())), preferred_element_type=F32)


def nn(left, right):
    return lax.dot_general(left, right, (((1,), (0,)), ((), ())), preferred_element_type=F32)


def nt(left, right):
    return lax.dot_general(left, right, (((1,), (1,)), ((), ())), preferred_element_type=F32)


def cost(flops, moved, exps=0):
    return pl.CostEstimate(flops=int(flops), bytes_accessed=int(moved), transcendentals=int(exps))


def pack_kernel(chip, block, packed):
    del chip
    size = block.shape[1]
    values = block[0].astype(F32)
    packed[0, :size] = values[:, :MAIN].astype(BF16)
    packed[0, size:] = pack_tail(values).astype(BF16)


def pack_slots(blocks, chip, slot_count):
    count, size, _ = blocks.shape
    return pl.pallas_call(
        pack_kernel,
        grid_spec=pltpu.PrefetchScalarGridSpec(
            num_scalar_prefetch=1,
            grid=(count,),
            in_specs=[pl.BlockSpec((1, size, size), lambda i, chip: (i, 0, 0))],
            out_specs=pl.BlockSpec((1, size + RUN, MAIN), lambda i, chip: (chip[0] * count + i, 0, 0)),
        ),
        out_shape=jax.ShapeDtypeStruct((slot_count, size + RUN, MAIN), BF16),
        name="pack_slots",
    )(chip, blocks)


def place():
    me, core = lax.axis_index("dp"), lax.axis_index("seq")
    x, y, z = me % 2, (me // 2) % 2, me // 4
    step_x, step_y = 1 - 2 * x, 2 * (1 - 2 * y)
    first = step_y * (1 - core) + step_x * core
    second = step_x * (1 - core) + step_y * core
    return me, core, z, first, second


def greet(partners):
    barrier = pltpu.get_barrier_semaphore()
    for chip, core in partners:
        pl.semaphore_signal(barrier, inc=1, device_id=(chip, core), device_id_type=MESH)
    pl.semaphore_wait(barrier, len(partners))


UP, DOWN, FIRST, SECOND, TWIN, GATHER_LABELS = 0, 4, 8, 12, 20, 36


def gather_kernel(slots, placed, out, send, recv):
    del placed
    me, core, z, first, second = place()
    half = slots // 2
    line = [(me + 4 * ((z + r) % 4 - z), core) for r in range(1, 4)]
    greet([(me + first, core), (me + second, core), (me, 1 - core)] + line)

    def copy(label, chip, dp, c):
        ref = out.at[pl.ds(chip * slots + core * half, half)]
        return pltpu.make_async_remote_copy(
            src_ref=ref,
            dst_ref=ref,
            send_sem=send.at[label],
            recv_sem=recv.at[label],
            device_id=(dp, c),
            device_id_type=MESH,
        )

    def arrival(label):
        ref = out.at[pl.ds(0, half)]
        return pltpu.make_async_remote_copy(
            src_ref=ref,
            dst_ref=ref,
            send_sem=send.at[label],
            recv_sem=recv.at[label],
            device_id=(me, 1 - core),
            device_id_type=MESH,
        )

    def col(zz):
        return me + 4 * (zz - z)

    def up(j):
        return copy(UP + j, me - 4 * (j - 1), me + 4, core)

    def down(j):
        return copy(DOWN + j, me + 4 * (j - 1), me - 4, core)

    def to_first(zz):
        return copy(FIRST + zz, col(zz), me + first, core)

    def to_second(zz, a):
        return copy(SECOND + 2 * zz + a, col(zz) + a * first, me + second, core)

    def to_twin(chip):
        return copy(TWIN + chip, chip, me, 1 - core)

    def spread(zz, own=False):
        to_first(zz).start()
        to_second(zz, 0).start()
        if not own:
            to_twin(col(zz)).start()

    def after_first(zz):
        to_first(zz).wait_recv()
        to_second(zz, 1).start()
        to_twin(col(zz) + first).start()

    def after_second(zz):
        for a in range(2):
            to_second(zz, a).wait_recv()
            to_twin(col(zz) + second + a * first).start()

    @pl.when(z < 3)
    def _():
        up(1).start()

    @pl.when(z > 0)
    def _():
        down(1).start()

    spread(z, own=True)
    for j in range(1, 4):

        @pl.when(z >= j)
        def _():
            up(j).wait_recv()
            if j < 3:

                @pl.when(z < 3)
                def _():
                    up(j + 1).start()

            spread(z - j)

        @pl.when(z + j <= 3)
        def _():
            down(j).wait_recv()
            if j < 3:

                @pl.when(z > 0)
                def _():
                    down(j + 1).start()

            spread(z + j)

        if j == 1:
            after_first(z)
        else:

            @pl.when(z >= j - 1)
            def _():
                after_first(z - (j - 1))

            @pl.when(z + j - 1 <= 3)
            def _():
                after_first(z + j - 1)

    @pl.when(z >= 3)
    def _():
        after_first(z - 3)

    @pl.when(z <= 0)
    def _():
        after_first(z + 3)

    after_second(z)
    for j in range(1, 4):

        @pl.when(z >= j)
        def _():
            after_second(z - j)

        @pl.when(z + j <= 3)
        def _():
            after_second(z + j)

    for zz in range(4):
        for a in range(2):
            for b in range(2):
                chip = col(zz) + a * first + b * second
                if a == 0 and b == 0:

                    @pl.when(zz != z)
                    def _():
                        to_twin(chip).wait_recv()
                        to_twin(chip).wait_send()

                else:
                    to_twin(chip).wait_recv()
                    to_twin(chip).wait_send()
        to_first(zz).wait_send()
        for a in range(2):
            to_second(zz, a).wait_send()

    @pl.when(z < 3)
    def _():
        up(1).wait_send()
        for j in range(1, 3):

            @pl.when(z >= j)
            def _():
                up(j + 1).wait_send()

    @pl.when(z > 0)
    def _():
        down(1).wait_send()
        for j in range(1, 3):

            @pl.when(z + j <= 3)
            def _():
                down(j + 1).wait_send()


def gather_slots(placed, slots):
    return pl.pallas_call(
        functools.partial(gather_kernel, slots),
        out_shape=jax.ShapeDtypeStruct(placed.shape, placed.dtype),
        in_specs=[pl.BlockSpec(memory_space=pl.ANY)],
        out_specs=pl.BlockSpec(memory_space=pl.ANY),
        scratch_shapes=[pltpu.SemaphoreType.DMA((GATHER_LABELS,)), pltpu.SemaphoreType.DMA((GATHER_LABELS,))],
        input_output_aliases={0: 0},
        compiler_params=pltpu.CompilerParams(collective_id=0, has_side_effects=True),
        name="gather_slots",
    )(placed)


R_TWIN, R_SECOND, R_FIRST, R_LINE, R_DONE, REDUCE_LABELS = 0, 16, 24, 28, 32, 33


def reduce_kernel(slots, grads, out, own, r_twin, r_second, r_first, r_line, total, load, send, recv, save):
    me, core, z, first, second = place()
    half = slots // 2
    line = [(me + 4 * ((z + r) % 4 - z), core) for r in range(1, 4)]
    greet([(me + first, core), (me + second, core), (me, 1 - core)] + line)

    def piece(chip, h):
        return grads.at[pl.ds(chip * slots + h * half, half)]

    def chip_at(zz, a, b):
        return me + 4 * (zz - z) + a * first + b * second

    def load_own(zz, a, b):
        chip = chip_at(zz, a, b)
        return pltpu.make_async_copy(piece(chip, core), own.at[chip], load.at[chip])

    def remote(src, dst, label, dp, c):
        return pltpu.make_async_remote_copy(
            src_ref=src,
            dst_ref=dst,
            send_sem=send.at[label],
            recv_sem=recv.at[label],
            device_id=(dp, c),
            device_id_type=MESH,
        )

    def twin(zz, a, b):
        chip = chip_at(zz, a, b)
        return remote(piece(chip, 1 - core), r_twin.at[chip], R_TWIN + chip, me, 1 - core)

    def to_second(zz, a):
        return remote(
            r_twin.at[chip_at(zz, a, 1)], r_second.at[2 * zz + a], R_SECOND + 2 * zz + a, me + second, core
        )

    def to_first(zz):
        return remote(r_twin.at[chip_at(zz, 1, 0)], r_first.at[zz], R_FIRST + zz, me + first, core)

    def to_line(r):
        zz = (z + r) % 4
        return remote(r_twin.at[chip_at(zz, 0, 0)], r_line.at[r - 1], R_LINE + r, chip_at(zz, 0, 0), core)

    def add_up(chip, others):
        def body(s, carry):
            value = own[chip, s].astype(F32) + r_twin[chip, s].astype(F32)
            for ref, index in others:
                value = value + ref[index, s].astype(F32)
            r_twin[chip, s] = value.astype(BF16)
            return carry

        lax.fori_loop(0, half, body, 0)

    def ready(zz, a, b):
        load_own(zz, a, b).wait()
        twin(zz, a, b).wait_recv()

    def send_second(zz, a):
        ready(zz, a, 1)
        add_up(chip_at(zz, a, 1), [])
        to_second(zz, a).start()

    def send_first(zz):
        ready(zz, 1, 0)
        to_second(zz, 1).wait_recv()
        add_up(chip_at(zz, 1, 0), [(r_second, 2 * zz + 1)])
        to_first(zz).start()

    def send_line(r):
        zz = (z + r) % 4
        ready(zz, 0, 0)
        to_second(zz, 0).wait_recv()
        to_first(zz).wait_recv()
        add_up(chip_at(zz, 0, 0), [(r_second, 2 * zz), (r_first, zz)])
        to_line(r).start()

    order = [2, 1, 3, 0]
    where = [(z + r) % 4 for r in order]
    for zz in where:
        for a in (1, 0):
            load_own(zz, a, 1).start()
            twin(zz, 1, a).start()
    for zz in where:
        for a in (1, 0):
            load_own(zz, a, 0).start()
            twin(zz, 0, a).start()

    def send_both(index):
        for a in (1, 0):
            send_second(where[index], a)

    send_both(0)
    send_both(1)
    send_both(2)
    send_first(where[0])
    send_both(3)
    send_first(where[1])
    send_line(order[0])
    send_first(where[2])
    send_line(order[1])
    send_first(where[3])
    send_line(order[2])

    ready(z, 0, 0)
    to_second(z, 0).wait_recv()
    to_first(z).wait_recv()
    for r in range(1, 4):
        to_line(r).wait_recv()

    def body(s, carry):
        value = own[me, s].astype(F32) + r_twin[me, s].astype(F32)
        value = value + r_second[2 * z, s].astype(F32)
        value = value + r_first[z, s].astype(F32)
        for r in range(3):
            value = value + r_line[r, s].astype(F32)
        total[s] = value
        return carry

    lax.fori_loop(0, half, body, 0)
    target = out.at[pl.ds(core * half, half)]
    done = remote(total, target, R_DONE, me, 1 - core)
    done.start()
    saved = pltpu.make_async_copy(total, target, save.at[0])
    saved.start()
    for zz in range(4):
        for a in range(2):
            for b in range(2):
                twin(zz, a, b).wait_send()
            to_second(zz, a).wait_send()
        to_first(zz).wait_send()
    for r in range(1, 4):
        to_line(r).wait_send()
    done.wait()
    saved.wait()


def reduce_slots(grads, slots):
    _, rows, lanes = grads.shape
    half = slots // 2
    pieces = lambda n: pltpu.VMEM((n, half, rows, lanes), BF16)
    return pl.pallas_call(
        functools.partial(reduce_kernel, slots),
        out_shape=jax.ShapeDtypeStruct((slots, rows, lanes), F32),
        in_specs=[pl.BlockSpec(memory_space=pl.ANY)],
        out_specs=pl.BlockSpec(memory_space=pl.ANY),
        scratch_shapes=[
            pieces(16),
            pieces(16),
            pieces(8),
            pieces(4),
            pieces(3),
            pltpu.VMEM((half, rows, lanes), F32),
            pltpu.SemaphoreType.DMA((16,)),
            pltpu.SemaphoreType.DMA((REDUCE_LABELS,)),
            pltpu.SemaphoreType.DMA((REDUCE_LABELS,)),
            pltpu.SemaphoreType.DMA((1,)),
        ],
        compiler_params=pltpu.CompilerParams(collective_id=1, has_side_effects=True, vmem_limit_bytes=60 << 20),
        name="reduce_slots",
    )(grads)


def assemble_kernel(slot_of, *refs):
    del slot_of
    out = refs[-1]
    size = out.shape[0]
    for j, block in enumerate(refs[:-1]):
        out[:, size * j : size * (j + 1)] = unpack(block[0].astype(F32)).astype(BF16)


def assemble(gathered, slot_of, rows, cols, block_of, name):
    packed_rows, lanes = gathered.shape[1:]
    size = packed_rows - RUN
    specs = [
        pl.BlockSpec((1, packed_rows, lanes), functools.partial(lambda j, i, v: (v[block_of(i, j)], 0, 0), j))
        for j in range(cols)
    ]
    return pl.pallas_call(
        assemble_kernel,
        grid_spec=pltpu.PrefetchScalarGridSpec(
            num_scalar_prefetch=1,
            grid=(rows,),
            in_specs=specs,
            out_specs=pl.BlockSpec((size, size * cols), lambda i, v: (i, 0)),
        ),
        out_shape=jax.ShapeDtypeStruct((size * rows, size * cols), BF16),
        name=name,
    )(slot_of, *([gathered] * cols))


def weight_grad_kernel(block_of, deep, size, slot_of, left, right, *refs):
    grads, stage, sem = refs[-3:]
    wide = right.shape[0] // size
    rows, cols = pl.program_id(0), pl.program_id(1)
    step = rows * pl.num_programs(1) + cols
    steps = pl.num_programs(0) * pl.num_programs(1)
    now = step % 2

    def copy(buffer, index, slot):
        return pltpu.make_async_copy(stage.at[buffer, index], grads.at[slot], sem.at[buffer, index])

    @pl.when(step >= 2)
    def _():
        for index in range(deep * wide):
            copy(now, index, 0).wait()

    other = right[...]
    for i in range(deep):
        panel = nt(left[size * i : size * (i + 1), :], other)
        for j in range(wide):
            index = i * wide + j
            block = panel[:, size * j : size * (j + 1)]
            stage[now, index, :size] = block[:, :MAIN].astype(BF16)
            stage[now, index, size:] = pack_tail(block).astype(BF16)
            copy(now, index, slot_of[block_of(rows * deep + i, cols * wide + j)]).start()

    @pl.when(step == steps - 1)
    def _():
        for index in range(deep * wide):
            copy(now, index, 0).wait()

        @pl.when(steps > 1)
        def _():
            for index in range(deep * wide):
                copy(1 - now, index, 0).wait()


def weight_grad(left, right, slot_of, grads, slot_count, size, block_of, name):
    depth = left.shape[1]
    deep = wide = 4
    grid = (left.shape[0] // (size * deep), right.shape[0] // (size * wide))
    anywhere = pl.BlockSpec(memory_space=pl.ANY)
    operands = [slot_of, left, right] + ([] if grads is None else [grads])
    return pl.pallas_call(
        functools.partial(weight_grad_kernel, block_of, deep, size),
        grid_spec=pltpu.PrefetchScalarGridSpec(
            num_scalar_prefetch=1,
            grid=grid,
            in_specs=[
                pl.BlockSpec((size * deep, depth), lambda i, j, v: (i, 0)),
                pl.BlockSpec((size * wide, depth), lambda i, j, v: (j, 0)),
            ]
            + [anywhere] * (len(operands) - 3),
            out_specs=anywhere,
            scratch_shapes=[
                pltpu.VMEM((2, deep * wide, size + RUN, MAIN), BF16),
                pltpu.SemaphoreType.DMA((2, deep * wide)),
            ],
        ),
        out_shape=jax.ShapeDtypeStruct((slot_count, size + RUN, MAIN), BF16),
        input_output_aliases={} if grads is None else {3: 0},
        cost_estimate=cost(
            2 * left.shape[0] * right.shape[0] * depth,
            2 * (left.size + right.size + left.shape[0] * right.shape[0]),
        ),
        name=name,
    )(*operands)


def attention_kernel(scale, qkv, low, high, out, lse):
    for group in range(low.shape[0]):
        base = PREFIX + GB * group
        for h in range(2):
            seen = slice(base, base + HALF * (h + 1))
            keys = jnp.concatenate([qkv[1, :, :PREFIX], qkv[1, :, seen]], axis=1)
            values = jnp.concatenate([qkv[2, :, :PREFIX], qkv[2, :, seen]], axis=1)
            queries = qkv[0, :, base + HALF * h : base + HALF * (h + 1)]
            scores = tn(keys, queries) * scale + (high if h else low)[group]
            top = jnp.max(scores, axis=0, keepdims=True)
            weights = jnp.exp(scores - top)
            total = jnp.sum(weights, axis=0, keepdims=True)
            mine = slice(GB * group + HALF * h, GB * group + HALF * (h + 1))
            out[:, mine] = (nn(values, weights.astype(BF16)) / total).astype(BF16)
            lse[0, :, mine] = top + jnp.log(total)


def attention_back_kernel(scale, qkv, low, high, out, lse, grad_out, grads):
    prefix_k = jnp.zeros((out.shape[0], PREFIX), F32)
    prefix_v = prefix_k
    for group in range(low.shape[0]):
        base = PREFIX + GB * group
        grad_k, grad_v = [None, None], [None, None]
        for h in range(2):
            seen = slice(base, base + HALF * (h + 1))
            keys = jnp.concatenate([qkv[1, :, :PREFIX], qkv[1, :, seen]], axis=1)
            values = jnp.concatenate([qkv[2, :, :PREFIX], qkv[2, :, seen]], axis=1)
            own = slice(base + HALF * h, base + HALF * (h + 1))
            mine = slice(GB * group + HALF * h, GB * group + HALF * (h + 1))
            queries = qkv[0, :, own]
            grad_o = grad_out[:, mine]
            delta = jnp.sum(grad_o.astype(F32) * out[:, mine].astype(F32), axis=0, keepdims=True)
            weights = jnp.exp(tn(keys, queries) * scale + (high if h else low)[group] - lse[0, :, mine])
            grad_s = weights * (tn(values, grad_o) - delta)
            grad_raw = (grad_s * scale).astype(BF16)
            grads[0, :, own] = nn(keys, grad_raw).astype(BF16)
            all_k = nt(queries, grad_raw)
            all_v = nt(grad_o, weights.astype(BF16))
            prefix_k = prefix_k + all_k[:, :PREFIX]
            prefix_v = prefix_v + all_v[:, :PREFIX]
            for i in range(h + 1):
                part = slice(PREFIX + HALF * i, PREFIX + HALF * (i + 1))
                grad_k[i] = all_k[:, part] if grad_k[i] is None else grad_k[i] + all_k[:, part]
                grad_v[i] = all_v[:, part] if grad_v[i] is None else grad_v[i] + all_v[:, part]
        for i in range(2):
            part = slice(base + HALF * i, base + HALF * (i + 1))
            grads[1, :, part] = grad_k[i].astype(BF16)
            grads[2, :, part] = grad_v[i].astype(BF16)
    grads[0, :, :PREFIX] = jnp.zeros((out.shape[0], PREFIX), BF16)
    grads[1, :, :PREFIX] = prefix_k.astype(BF16)
    grads[2, :, :PREFIX] = prefix_v.astype(BF16)


def attention_specs(qkv, low, high):
    _, features, length = qkv.shape
    head, own = features // HEADS, length - PREFIX
    whole = lambda array: pl.BlockSpec(array.shape, lambda h: (0,) * array.ndim)
    three = pl.BlockSpec((3, head, length), lambda h: (0, h, 0))
    one = pl.BlockSpec((head, own), lambda h: (h, 0))
    row = pl.BlockSpec((1, 1, own), lambda h: (h, 0, 0))
    return features, own, head, [three, whole(low), whole(high)], one, row, three


def attention(qkv, low, high):
    features, own, head, specs, one, row, _ = attention_specs(qkv, low, high)
    return pl.pallas_call(
        functools.partial(attention_kernel, head ** (-0.5)),
        grid=(HEADS,),
        in_specs=specs,
        out_specs=[one, row],
        out_shape=[
            jax.ShapeDtypeStruct((features, own), BF16),
            jax.ShapeDtypeStruct((HEADS, 1, own), F32),
        ],
        cost_estimate=cost(8 * features * own * GB, 2 * qkv.size, HEADS * own * GB),
        name="attention",
    )(qkv, low, high)


def attention_back(qkv, low, high, out, lse, grad_out):
    features, own, head, specs, one, row, three = attention_specs(qkv, low, high)
    return pl.pallas_call(
        functools.partial(attention_back_kernel, head ** (-0.5)),
        grid=(HEADS,),
        in_specs=specs + [one, row, one],
        out_specs=three,
        out_shape=jax.ShapeDtypeStruct(qkv.shape, BF16),
        cost_estimate=cost(20 * features * own * GB, 4 * qkv.size, HEADS * own * GB),
        name="attention_back",
    )(qkv, low, high, out, lse, grad_out)


def score_biases(alive, prefix_alive, later):
    groups = alive.shape[0] // GB
    live = alive.reshape(groups, GB, 1)
    square = (groups, HALF, HALF)
    prefix = jnp.broadcast_to(prefix_alive[None, :, None] & later[:, None, None], (groups, PREFIX, HALF))
    ahead = (jnp.arange(HALF)[:, None] <= jnp.arange(HALF)[None, :])[None]
    low = jnp.concatenate([prefix, live[:, :HALF] & ahead], axis=1)
    high = jnp.concatenate([prefix, jnp.broadcast_to(live[:, :HALF], square), live[:, HALF:] & ahead], axis=1)
    return jnp.where(low, 0.0, -1e30).astype(F32), jnp.where(high, 0.0, -1e30).astype(F32)


def split(values):
    high = values.astype(BF16)
    return high, (values - high.astype(F32)).astype(BF16)


def product(form, left, right):
    (left_high, left_low), (right_high, right_low) = left, right
    return form(left_high, right_high) + (form(left_high, right_low) + form(left_low, right_high))


def optimizer_kernel(scale, packed, master, average, left, right, root_left, root_right, *outs):
    slot_grad, new_left, new_right, new_master, new_copy, new_average = outs
    size = master.shape[1]
    grad = unpack(packed[0]) * scale
    slot_grad[0] = grad
    grad_parts = split(grad)
    new_left[0] = 0.5 * left[0] + (0.5 / size) * product(nt, grad_parts, grad_parts)
    new_right[0] = 0.5 * right[0] + (0.5 / size) * product(tn, grad_parts, grad_parts)
    right_part = product(nn, grad_parts, split(root_right[0]))
    step = product(nn, split(root_left[0]), split(right_part))
    moved = master[0] - 0.03 * step
    new_master[0] = moved
    new_copy[0] = moved.astype(BF16)
    new_average[0] = 0.8 * average[0] + 0.2 * moved


def optimizer(packed, scale, arrays):
    slots, size, _ = arrays[0].shape
    block = pl.BlockSpec((1, size, size), lambda i: (i, 0, 0))
    shape = lambda dtype: jax.ShapeDtypeStruct((slots, size, size), dtype)
    return pl.pallas_call(
        functools.partial(optimizer_kernel, scale),
        grid=(slots,),
        in_specs=[pl.BlockSpec((1,) + packed.shape[1:], lambda i: (i, 0, 0))] + [block] * 6,
        out_specs=[block] * 6,
        out_shape=[shape(F32), shape(F32), shape(F32), shape(F32), shape(BF16), shape(F32)],
        name="optimizer",
    )(packed, *arrays)


def norm_parts(values):
    average = jnp.mean(values, axis=0, keepdims=True)
    centred = values - average
    variance = jnp.mean(centred * centred, axis=0, keepdims=True)
    scale = lax.rsqrt(variance + 1e-05)
    return centred * scale, scale


def norm_back(unit, scale, gain, grad):
    inner = grad * gain
    mean_one = jnp.mean(inner, axis=0, keepdims=True)
    mean_two = jnp.mean(inner * unit, axis=0, keepdims=True)
    return scale * (inner - mean_one - unit * mean_two)


def butterfly(values, shape):
    for bit in (1, 2, 4, 8, 16):
        pairs = [(i, i ^ bit) for i in range(32)]
        values = values + lax.ppermute(values, ("dp", "seq"), pairs)
    return values


def local(
    chips,
    cores,
    tokens,
    cotangent,
    pad_mask,
    prefix_len,
    norm_gains,
    norm_shifts,
    owner_map,
    weight_copy,
    master,
    average_weights,
    stat_left,
    stat_right,
    root_left,
    root_right,
):
    cell_count, length, features = tokens.shape
    assert cell_count == 1
    slots, size, _ = weight_copy.shape
    slot_count = owner_map.shape[0]
    row_blocks = features // size
    square = row_blocks * row_blocks
    col_blocks = (slot_count - 4 * square) // (2 * row_blocks)
    known = chips == 16 and cores == 2
    chip = lax.axis_index("dp").astype(jnp.int32)
    seq_index = lax.axis_index("seq")

    slot_of = jnp.zeros((slot_count,), jnp.int32).at[owner_map].set(jnp.arange(slot_count, dtype=jnp.int32))
    if known:
        gathered = gather_slots(pack_slots(weight_copy, chip.reshape(1), slot_count), slots)
    else:
        packed = pack_slots(weight_copy, jnp.zeros((1,), jnp.int32), slots)
        gathered = lax.all_gather(packed, "dp", axis=0, tiled=True)

    def three_of(i, j):
        return (j // row_blocks) * square + i * row_blocks + j % row_blocks

    def out_of(i, j):
        return 3 * square + i * row_blocks + j

    def up_of(i, j):
        return 4 * square + i * col_blocks + j

    def down_of(i, j):
        return 4 * square + row_blocks * col_blocks + i * row_blocks + j

    w_three = assemble(gathered, slot_of, row_blocks, 3 * row_blocks, three_of, "lay_three")
    w_out = assemble(gathered, slot_of, row_blocks, row_blocks, out_of, "lay_out")
    w_up = assemble(gathered, slot_of, row_blocks, col_blocks, up_of, "lay_up")
    w_down = assemble(gathered, slot_of, col_blocks, row_blocks, down_of, "lay_down")

    own_tokens = tokens.reshape(length, features).T
    prefix_tokens = own_tokens[:, :PREFIX]
    if cores == 2:
        arrived = lax.ppermute(prefix_tokens, "seq", [(0, 1)])
        prefix_tokens = jnp.where(seq_index == 0, prefix_tokens, arrived)
    else:
        prefix_tokens = lax.all_gather(prefix_tokens, "seq")[0]
    inputs = own_tokens.astype(F32)
    gain_one, shift_one = norm_gains[0][:, None], norm_shifts[0][:, None]
    gain_two, shift_two = norm_gains[1][:, None], norm_shifts[1][:, None]
    unit_all, _ = norm_parts(jnp.concatenate([prefix_tokens, own_tokens], axis=1).astype(F32))
    normed_in = (unit_all * gain_one + shift_one).astype(BF16)
    qkv = tn(w_three, normed_in).astype(BF16).reshape(3, features, PREFIX + length)

    position = seq_index * length + jnp.arange(length, dtype=jnp.int32)
    alive = jnp.where(position < PREFIX, position < prefix_len[0], pad_mask[0] == 1)
    prefix_alive = jnp.arange(PREFIX, dtype=jnp.int32) < prefix_len[0]
    groups = length // GB
    later = seq_index * groups + jnp.arange(groups) > 0
    low, high = score_biases(alive, prefix_alive, later)

    attended, log_total = attention(qkv, low, high)
    middle = inputs + tn(w_out, attended)
    unit_two, scale_two = norm_parts(middle)
    normed_mid = (unit_two * gain_two + shift_two).astype(BF16)
    up_pre = tn(w_up, normed_mid)
    activated, gelu_back = jax.vjp(functools.partial(jax.nn.gelu, approximate=True), up_pre)
    activated = activated.astype(BF16)
    block_out = (middle + tn(w_down, activated)).astype(BF16)

    grad_low = cotangent.reshape(length, features).T
    grad_pre = gelu_back(nn(w_down, grad_low))[0].astype(BF16)
    grads = weight_grad(activated, grad_low, slot_of, None, slot_count, size, down_of, "grad_down")
    grads = weight_grad(normed_mid, grad_pre, slot_of, grads, slot_count, size, up_of, "grad_up")
    grad_normed_two = nn(w_up, grad_pre)
    grad_middle = grad_low.astype(F32) + norm_back(unit_two, scale_two, gain_two, grad_normed_two)
    grad_branch = grad_middle.astype(BF16)
    grads = weight_grad(attended, grad_branch, slot_of, grads, slot_count, size, out_of, "grad_out")
    grad_att = nn(w_out, grad_branch).astype(BF16)
    grad_three = attention_back(qkv, low, high, attended, log_total, grad_att)
    grad_three = grad_three.reshape(3 * features, PREFIX + length)
    grads = weight_grad(normed_in, grad_three, slot_of, grads, slot_count, size, three_of, "grad_three")
    grad_all = nn(w_three, grad_three)
    prefix_part = grad_all[:, :PREFIX]
    if cores == 2:
        prefix_part = prefix_part + lax.ppermute(prefix_part, "seq", [(1, 0)])
    else:
        prefix_part = lax.psum(prefix_part, "seq")
    prefix_part = jnp.where(seq_index == 0, prefix_part, 0.0)
    grad_normed = grad_all[:, PREFIX:] + jnp.pad(prefix_part, ((0, 0), (0, length - PREFIX)))
    unit_one, scale_one = norm_parts(inputs)
    grad_input = grad_middle + norm_back(unit_one, scale_one, gain_one, grad_normed)

    grad_scale = 1.0 / math.sqrt(length * chips * cores)
    norm_terms = jnp.stack(
        [
            jnp.sum(grad_normed * unit_one, axis=1),
            jnp.sum(grad_normed, axis=1),
            jnp.sum(grad_normed_two * unit_two, axis=1),
            jnp.sum(grad_normed_two, axis=1),
        ]
    )
    norm_terms = norm_terms * grad_scale
    norm_grad = butterfly(norm_terms, None) if known else lax.psum(norm_terms, ("dp", "seq"))
    params = jnp.stack([norm_gains[0], norm_shifts[0], norm_gains[1], norm_shifts[1]])
    new_norms = params - 0.1 * norm_grad * lax.rsqrt(jnp.mean(norm_grad * norm_grad) + 1e-06)

    if known:
        summed = reduce_slots(grads, slots)
    else:
        part = lax.psum_scatter(grads.astype(F32), "dp", scatter_dimension=0, tiled=True)
        summed = lax.psum(part, "seq")
    stepped = optimizer(
        summed, grad_scale, (master, average_weights, stat_left, stat_right, root_left, root_right)
    )
    token_shape = (cell_count, length, features)
    return (
        block_out.T.reshape(token_shape),
        grad_input.T.reshape(token_shape),
        norm_grad,
        new_norms,
        *stepped,
    )


def solution(mesh):
    tokens, slots = P("dp", "seq", None), P("dp", None, None)
    in_specs = (tokens, tokens, P("dp", "seq"), P("dp"), P(), P(), P()) + (slots,) * 7
    out_specs = (tokens, tokens, P(), P()) + (slots,) * 6
    body = functools.partial(local, mesh.shape["dp"], mesh.shape["seq"])
    return jax.shard_map(body, mesh=mesh, in_specs=in_specs, out_specs=out_specs, check_vma=False)
```

time: 2650 us -> 682 us (0.26)
  waiting for transfers between devices: 1560 us -> 5.99 us
  Pallas kernels: 0 us -> 492 us
  local copies, waits for them, and re-layouts: 452 us -> 9.02 us
  other arithmetic: 236 us -> 26.8 us
  matrix products: 338 us -> 131 us
  blocking collectives: 39.9 us -> 0 us
    reduce_scatter x1 -> x0, waiting for transfers between devices: 1130 us -> none  [local(): lax.psum_scatter(ordered, 'dp', scatter_dimension=0, tiled=True)]
    pallas_call x0 -> x14, Pallas kernels: none -> 492 us  [the longest x1 138 us: reduce_slots(): pl.pallas_call(functools.partial(reduce_kernel, slots), out_shape=jax.Sha...]
    all_gather x1 -> x0, waiting for transfers between devices: 421 us -> none  [local(): slots = lax.all_gather(weight_copy, 'dp', axis=0, tiled=True)]
    dot_general x34 -> x8, matrix products: 338 us -> 131 us  [the longest x4 66 us: nn(): lax.dot_general(left, right, (((1,), (0,)), ((), ())), preferred_element_...]
    reshape x20 -> x0, local copies, waits for them, and re-layouts: 190 us -> none  [the longest x6 67.7 us: assemble(): return pieces.reshape(row_blocks, col_blocks, block_size, block_size).tra...]
    gather x2 -> x0, local copies, waits for them, and re-layouts: 84.7 us -> none  [the longest x1 56.4 us: local(): ordered = jnp.take(grad_blocks, owner_map, axis=0)]
    select_n x5 -> x6, other arithmetic: 83.6 us -> 3.72 us  [the longest x1 1.12 us: local(): prefix_part = jnp.where(seq_index == 0, prefix_part, 0.0)]
    unnamed x179 -> x64, local copies, waits for them, and re-layouts: 81.6 us -> 4.45 us
  transfers between devices with their start and end apart: 5 -> 7, of which waited for: 2 -> 2; matrix products, arithmetic and copies ran while one was open for 7% -> 5% of each run, Pallas kernels for 0% -> 61%
where the time goes in v1:
time: 682 us; the launch traced here: 678 us
  Pallas kernels  492 us (72%)
  matrix products  131 us (19%)
  other arithmetic  26.8 us (4%)
  starting transfers between devices  10.2 us (1%)
  local copies, waits for them, and re-layouts  9.02 us (1%)
    pallas_call x1, Pallas kernels, reduce_slots(): pl.pallas_call(functools.partial(reduce_kernel, slots), out_shape=jax.Sha...  138 us
    pallas_call x1, Pallas kernels, gather_slots(): pl.pallas_call(functools.partial(gather_kernel, slots), out_shape=jax.Sha...  132 us
    dot_general x4, matrix products, nn(): lax.dot_general(left, right, (((1,), (0,)), ((), ())), preferred_element_...  66 us
    dot_general x4, matrix products, tn(): lax.dot_general(left, right, (((0,), (0,)), ((), ())), preferred_element_...  65.1 us
    pallas_call x4, Pallas kernels, weight_grad(): pl.pallas_call(functools.partial(weight_grad_kernel, block_of, deep, size...  61.5 us
    pallas_call x4, Pallas kernels, assemble(): pl.pallas_call(assemble_kernel, grid_spec=pltpu.PrefetchScalarGridSpec(nu...  46.5 us
    pallas_call x1, Pallas kernels, attention_back(): pl.pallas_call(functools.partial(attention_back_kernel, head ** (-0.5)),...  45.5 us
    pallas_call x1, Pallas kernels, attention(): pl.pallas_call(functools.partial(attention_kernel, head ** (-0.5)), grid=...  31.9 us
  transfers between devices with their start and end apart: 7, of which 2 were waited for; matrix products, arithmetic and copies ran while one was open for 5% of the time, Pallas kernels for 61%

profile of v1, /device:TPU:0, one launch (start us, length us, event | category | flops | bytes accessed | tf_op | source)
XLA Modules:
  0.0 678.1 jit_solution(14017439301740949445)
XLA Ops:
  0.6 1.7 slice.41
  2.3 3.1 collective-permute-start
  5.4 2.0 convert_reduce_fusion
  8.1 0.7 compare_reduce_fusion
  8.9 0.7 compare_select_fusion
  9.6 0.6 broadcast_multiply_fusion.3
  10.2 0.1 broadcast_and_fusion.2
  10.2 0.2 broadcast_and_fusion
  10.4 0.1 broadcast_in_dim.24
  10.6 0.1 and.54
  10.7 1.0 add_select_fusion.high
  11.7 0.8 add_select_fusion.2.low
  12.5 8.0 %pack_slots.1.placed = bf16[192,312,256]{2,1,0:T(8,128)(2,1)} custom-call(s32[1]{0:T(128)} %bitcast.1.chip, bf16[12,280,280]{2,1,0:T(8,128)(2,1)} %block.1), custom_call_target="tpu_custom_call" | custom-call | tf_op jit(solution)/shard_map/pack_slots/pallas_call | solution.py:84
  20.5 131.9 %gather_slots.1.refs_0_.refs_1_.refs_2_.refs_3_.refs_4_.refs_5_.refs_6_.refs_7_.refs_8_.refs_9_.refs_10_.refs_11_.refs_12_.refs_13_.refs_14_.refs_15_ = bf16[192,312,256]{2,1,0:T(8,128)(2,1)} custom-call(bf16[192,312,256]{2,1,0:T(8,128)(2,1)} %pack_slots.1.placed), custom_call_target="tpu_custom_call", output_to_operand_aliasing={{}: (0, {})} | custom-call | tf_op jit(solution)/shard_map/gather_slots/pallas_call | solution.py:281
  152.4 1.9 scatter_custom_fusion.slot_of
  154.3 5.6 lay_out.1
  159.9 10.8 %lay_three.1 = bf16[1120,3360]{1,0:T(8,128)(2,1)} custom-call(s32[192]{0:T(256)} %scatter_custom_fusion.slot_of, bf16[192,312,256]{2,1,0:T(8,128)(2,1)} %gather_slots.1.refs_0_.refs_1_.refs_2_.refs_3_.refs_4_.refs_5_.refs_6_.refs_7_.refs_8_.refs_9_.refs_10_.refs_11_.refs_12_.refs_13_.refs_14_.refs_15_, ...), custom_call_target="tpu_custom_call" | custom-call | tf_op jit(solution)/shard_map/lay_three/pallas_call | solution.py:472
  170.7 13.2 %lay_up.1 = bf16[1120,4480]{1,0:T(8,128)(2,1)} custom-call(s32[192]{0:T(256)} %scatter_custom_fusion.slot_of, bf16[192,312,256]{2,1,0:T(8,128)(2,1)} %gather_slots.1.refs_0_.refs_1_.refs_2_.refs_3_.refs_4_.refs_5_.refs_6_.refs_7_.refs_8_.refs_9_.refs_10_.refs_11_.refs_12_.refs_13_.refs_14_.refs_15_, ...), custom_call_target="tpu_custom_call" | custom-call | tf_op jit(solution)/shard_map/lay_up/pallas_call | solution.py:472
  183.9 0.0 copy-start
  183.9 16.9 %lay_down.1 = bf16[4480,1120]{1,0:T(8,128)(2,1)} custom-call(s32[192]{0:T(256)} %scatter_custom_fusion.slot_of, bf16[192,312,256]{2,1,0:T(8,128)(2,1)} %gather_slots.1.refs_0_.refs_1_.refs_2_.refs_3_.refs_4_.refs_5_.refs_6_.refs_7_.refs_8_.refs_9_.refs_10_.refs_11_.refs_12_.refs_13_.refs_14_.refs_15_, ...), custom_call_target="tpu_custom_call" | custom-call | tf_op jit(solution)/shard_map/lay_down/pallas_call | solution.py:472
  200.8 0.6 slice_reduce_fusion
  201.5 0.1 broadcast_select_fusion
  201.6 0.4 convert_reduce_fusion.1
  202.0 0.7 fusion.14
  202.8 1.3 fusion.17.left
  204.1 0.7 copy-done.8
  204.8 13.6 %convolution_convert_fusion = bf16[3360,1152]{1,0:T(8,128)(2,1)} fusion(bf16[1120,3360]{1,0:T(8,128)(2,1)S(1)} %copy-done.8, bf16[1120,1152]{1,0:T(8,128)(2,1)S(1)} %fusion.17.left), kind=kOutput, calls=%fused_computation.11 | convolution fusion | flops 8674283520 | bytes 17848320 | tf_op jit(solution)/shard_map/dot_general | solution.py:59
  218.4 31.9 %attention.1 = (bf16[1120,1024]{1,0:T(8,128)(2,1)}, f32[20,1,1024]{2,1,0:T(1,128)}) custom-call(bf16[3,1120,1152]{2,1,0:T(8,128)(2,1)} %bitcast.71, f32[4,256,128]{2,1,0:T(8,128)} %add_select_fusion.2.low, f32[4,384,128]{2,1,0:T(8,128)} %add_select_fusion.high), custom_call_target="tpu_custom_call" | custom-call | flops 2348810240 | bytes 7741440 | tf_op jit(solution)/shard_map/attention/pallas_call | solution.py:619
  250.3 8.8 %fusion.39 = (f32[1024]{0:T(1024)S(1)}, f32[1120,1024]{1,0:T(8,128)S(1)}, f32[1024]{0:T(1024)}, f32[1120,1024]{1,0:T(8,128)}) fusion(bf16[1,1024,1120]{1,2,0:T(8,128)(2,1)S(1)} %copy-done, f32[1024]{0:T(1024)S(1)} %copy-done.19, bf16[1120,1120]{1,0:T(8,128)(2,1)} %lay_out.1, bf16[1120,1024]{1,0:T(8,128)(2,1)} %get-tuple-element.18.out.left), kind=kOutput, calls=%fused_computation.92 | convolution fusion | flops 2575890432 | bytes 16283648 | tf_op jit(solution)/shard_map/dot_general | solution.py:59
  259.2 0.5 multiply_reduce_fusion.2
  259.7 0.7 add_convert_fusion.left
  260.4 0.0 copy-start.2
  260.4 24.1 %multiply_convert_fusion = (bf16[4480,1024]{1,0:T(8,128)(2,1)}, f32[4480,1024]{1,0:T(8,128)}) fusion(bf16[1120,4480]{1,0:T(8,128)(2,1)} %lay_up.1, bf16[1120,1024]{1,0:T(8,128)(2,1)S(1)} %add_convert_fusion.left), kind=kOutput, calls=%fused_computation.10 | convolution fusion | flops 10317332480 | bytes 39854080 | tf_op jit(solution)/shard_map/dot_general | solution.py:59
  284.5 28.5 %fusion.6.right = bf16[4480,1024]{1,0:T(8,128)(2,1)} fusion(f32[4480,1024]{1,0:T(8,128)} %get-tuple-element.53, bf16[4480,1120]{1,0:T(8,128)(2,1)} %lay_down.1, bf16[1,1024,1120]{1,2,0:T(8,128)(2,1)S(1)} %copy-done.2), kind=kOutput, calls=%fused_computation.9 | convolution fusion | flops 10367795200 | bytes 39854080 | tf_op jit(solution)/shard_map/dot_general | solution.py:63
  313.1 18.7 %multiply_reduce_fusion = (f32[1120]{0:T(1024)S(1)}, f32[1024]{0:T(1024)S(1)}, f32[1024]{0:T(1024)S(1)}, f32[1120]{0:T(1024)S(1)}, f32[1120,1024]{1,0:T(8,128)S(1)}) fusion(f32[1120,1024]{1,0:T(8,128)S(1)} %get-tuple-element.41, f32[1024]{0:T(1024)S(1)} %add_rsqrt_fusion.2, f32[1024]{0:T(1024)S(1)} %broadcast_multiply_fusion.6, ...), kind=kOutput, calls=%fused_computation.38 | convolution fusion | flops 10286362624 | bytes 28415104 | tf_op jit(solution)/shard_map/dot_general | solution.py:63
  331.8 0.0 copy-start.9
  331.9 2.0 fusion.38.right
  333.8 0.2 copy-done.4
  334.1 0.0 copy-done.23
  334.1 1.1 copy-done.9
  335.2 4.3 convolution_convert_fusion.1.grad_out
  339.5 45.5 %attention_back.1 = bf16[3,1120,1152]{2,1,0:T(8,128)(2,1)} custom-call(bf16[3,1120,1152]{2,1,0:T(8,128)(2,1)} %bitcast.72, f32[4,256,128]{2,1,0:T(8,128)} %add_select_fusion.2.low, f32[4,384,128]{2,1,0:T(8,128)} %add_select_fusion.high, bf16[1120,1024]{1,0:T(8,128)(2,1)} %get-tuple-element.18.out.left, f32[20,1,1024]{2,1,0:T(1,128)} %get-tuple-element.19.lse, ...), custom_call_target="tpu_custom_call" | custom-call | flops 5872025600 | bytes 15482880 | tf_op jit(solution)/shard_map/attention_back/pallas_call | solution.py:635
  385.1 14.4 %fusion.40 = f32[1120,1152]{1,0:T(8,128)S(1)} fusion(bf16[1120,3360]{1,0:T(8,128)(2,1)} %lay_three.1, bf16[3360,1152]{1,0:T(8,128)(2,1)} %bitcast.69), kind=kOutput, calls=%fused_computation.93 | convolution fusion | flops 8670412800 | bytes 20428800 | tf_op jit(solution)/shard_map/dot_general | solution.py:63
  399.5 2.3 copy-done.3
  401.8 1.3 collective-permute-start.1
  403.1 18.6 %fusion.26 = bf16[1,1024,1120]{1,2,0:T(8,128)(2,1)} fusion(bf16[4480,1024]{1,0:T(8,128)(2,1)} %get-tuple-element.52.left, bf16[4480,1120]{1,0:T(8,128)(2,1)} %lay_down.1, f32[1120,1024]{1,0:T(8,128)} %get-tuple-element.51, bf16[1,1024,1120]{1,2,0:T(8,128)(2,1)S(1)} %copy-done), kind=kOutput, calls=%fused_computation.48 | convolution fusion | flops 10280632320 | bytes 28385280 | tf_op jit(solution)/shard_map/dot_general | solution.py:59
  421.7 18.3 %grad_down.1.refs_0_ = bf16[192,312,256]{2,1,0:T(8,128)(2,1)} custom-call(s32[192]{0:T(256)} %scatter_custom_fusion.slot_of, bf16[4480,1024]{1,0:T(8,128)(2,1)} %get-tuple-element.52.left, bf16[1120,1024]{1,0:T(8,128)(2,1)} %bitcast.68), custom_call_target="tpu_custom_call" | custom-call | flops 10276044800 | bytes 21504000 | tf_op jit(solution)/shard_map/grad_down/pallas_call | solution.py:528
  440.1 18.5 %grad_up.1.refs_0_ = bf16[192,312,256]{2,1,0:T(8,128)(2,1)} custom-call(s32[192]{0:T(256)} %scatter_custom_fusion.slot_of, bf16[1120,1024]{1,0:T(8,128)(2,1)} %copy-done.7, bf16[4480,1024]{1,0:T(8,128)(2,1)} %fusion.6.right, bf16[192,312,256]{2,1,0:T(8,128)(2,1)} %grad_down.1.refs_0_), custom_call_target="tpu_custom_call", output_to_operand_aliasing={{}: (3, {})} | custom-call | flops 10276044800 | bytes 21504000 | tf_op jit(solution)/shard_map/grad_up/pallas_call | solution.py:528
  458.7 1.1 add_select_fusion.1
  459.9 3.8 fusion.23
  463.7 1.4 collective-permute-start.2
  465.2 7.5 %grad_out.1.refs_0_ = bf16[192,312,256]{2,1,0:T(8,128)(2,1)} custom-call(s32[192]{0:T(256)} %scatter_custom_fusion.slot_of, bf16[1120,1024]{1,0:T(8,128)(2,1)} %get-tuple-element.18.out.left, bf16[1120,1024]{1,0:T(8,128)(2,1)} %copy-done.6, bf16[192,312,256]{2,1,0:T(8,128)(2,1)} %grad_up.1.refs_0_), custom_call_target="tpu_custom_call", output_to_operand_aliasing={{}: (3, {})} | custom-call | flops 2569011200 | bytes 7096320 | tf_op jit(solution)/shard_map/grad_out/pallas_call | solution.py:528
  472.8 1.1 collective-permute-start.3
  473.9 17.0 %grad_three.1.grads = bf16[192,312,256]{2,1,0:T(8,128)(2,1)} custom-call(s32[192]{0:T(256)} %scatter_custom_fusion.slot_of, bf16[1120,1152]{1,0:T(8,128)(2,1)} %copy-done.5, bf16[3360,1152]{1,0:T(8,128)(2,1)} %bitcast.70, bf16[192,312,256]{2,1,0:T(8,128)(2,1)} %grad_out.1.refs_0_), custom_call_target="tpu_custom_call", output_to_operand_aliasing={{}: (3, {})} | custom-call | flops 8670412800 | bytes 17848320 | tf_op jit(solution)/shard_map/grad_three/pallas_call | solution.py:528
  490.9 138.3 %reduce_slots.1.packed = f32[12,312,256]{2,1,0:T(8,128)} custom-call(bf16[192,312,256]{2,1,0:T(8,128)(2,1)} %grad_three.1.grads), custom_call_target="tpu_custom_call" | custom-call | tf_op jit(solution)/shard_map/reduce_slots/pallas_call | solution.py:435
  629.3 28.6 %optimizer.1 = (f32[12,280,280]{2,1,0:T(8,128)}, f32[12,280,280]{2,1,0:T(8,128)}, f32[12,280,280]{2,1,0:T(8,128)}, f32[12,280,280]{2,1,0:T(8,128)}, bf16[12,280,...) custom-call(f32[12,312,256]{2,1,0:T(8,128)} %reduce_slots.1.packed, f32[12,280,280]{2,1,0:T(8,128)} %master.1, ...), custom_call_target="tpu_custom_call" | custom-call | tf_op jit(solution)/shard_map/optimizer/pallas_call | solution.py:687
  657.9 1.1 collective-permute-start.4
  659.0 2.8 collective-permute-done.4
  661.8 0.6 collective-permute-start.5
  662.4 3.2 collective-permute-done.5
  665.6 1.7 collective-permute-start.6
  667.3 8.6 %fusion.22 = f32[1,1024,1120]{1,2,0:T(8,128)} fusion(f32[1024]{0:T(1024)S(1)} %broadcast_multiply_fusion.1, f32[1024]{0:T(1024)S(1)} %broadcast_multiply_fusion.2, f32[1120]{0:T(1024)S(1)} %copy-done.13, f32[1024]{0:T(1024)S(1)} %add_rsqrt_fusion.1, f32[1024]{0:T(1024)S(1)} %copy-done.20, f32[1120,128]{1,0:T(8,128)S(1)} %add_select_fusion.1, ...), kind=kLoop, calls=%fused_computation.33 | loop fusion | flops 21790720 | bytes 23552768 | tf_op jit(solution)/shard_map/reshape | solution.py:850
  675.9 0.6 multiply_reduce_fusion.5
  677.3 0.6 maximum_subtract_fusion
  (87 shorter events, 0.4 us)
Async XLA Ops:
  2.3 199.1 %collective-permute-start = (bf16[1120,128]{1,0:T(8,128)(2,1)}, bf16[1120,128]{1,0:T(8,128)(2,1)}, u32[]{:S(2)}, u32[]{:S(2)}) collective-permute-start(bf16[1120,128]{1,0:T(8,128)(2,1)} %slice.41), channel_id=1, source_target_pairs={{0,1},{2,3},{4,5},{6,7},{8,9},{10,11},{12,13},{14,15},{16,17},{18,... | collective-permute-start | bytes 860168 | tf_op jit(solution)/shard_map/ppermute | solution.py:775
  183.9 17.0 %copy-start.29 = (f32[2,1120]{1,0:T(2,128)S(1)}, f32[2,1120]{1,0:T(2,128)}, u32[]{:S(2)}) copy-start(f32[2,1120]{1,0:T(2,128)} %param.19) | copy-start | bytes 26884
  183.9 17.0 %copy-start.30 = (f32[2,1120]{1,0:T(2,128)S(1)}, f32[2,1120]{1,0:T(2,128)}, u32[]{:S(2)}) copy-start(f32[2,1120]{1,0:T(2,128)} %param.18) | copy-start | bytes 26884
  183.9 17.6 %copy-start = (bf16[1,1024,1120]{1,2,0:T(8,128)(2,1)S(1)}, bf16[1,1024,1120]{1,2,0:T(8,128)(2,1)}, u32[]{:S(2)}) copy-start(bf16[1,1024,1120]{1,2,0:T(8,128)(2,1)} %param.14) | copy-start | bytes 6881284
  201.5 1.3 copy-start.12
  201.5 130.3 %copy-start.10 = (f32[1120]{0:T(1024)}, f32[1120]{0:T(1024)S(1)}, u32[]{:S(2)}) copy-start(f32[1120]{0:T(1024)S(1)} %get-tuple-element.58) | copy-start | bytes 13444
  201.6 3.2 copy-start.8
  204.8 13.6 %copy-start.5 = (bf16[1120,1152]{1,0:T(8,128)(2,1)}, bf16[1120,1152]{1,0:T(8,128)(2,1)S(1)}, u32[]{:S(2)}) copy-start(bf16[1120,1152]{1,0:T(8,128)(2,1)S(1)} %fusion.17.left) | copy-start | bytes 7741444
  218.4 31.9 %copy-start.19 = (f32[1024]{0:T(1024)S(1)}, f32[1024]{0:T(1024)}, u32[]{:S(2)}) copy-start(f32[1024]{0:T(1024)} %broadcast_multiply_fusion.3) | copy-start | bytes 12292
  259.1 72.7 %copy-start.1 = (f32[1120,1024]{1,0:T(8,128)}, f32[1120,1024]{1,0:T(8,128)S(1)}, u32[]{:S(2)}) copy-start(f32[1120,1024]{1,0:T(8,128)S(1)} %get-tuple-element.41) | copy-start | bytes 13762564
  259.1 72.7 %copy-start.14 = (f32[1024]{0:T(1024)}, f32[1024]{0:T(1024)S(1)}, u32[]{:S(2)}) copy-start(f32[1024]{0:T(1024)S(1)} %broadcast_multiply_fusion.6) | copy-start | bytes 12292
  259.7 72.2 %copy-start.17 = (f32[1024]{0:T(1024)}, f32[1024]{0:T(1024)S(1)}, u32[]{:S(2)}) copy-start(f32[1024]{0:T(1024)S(1)} %add_rsqrt_fusion.2) | copy-start | bytes 12292
  260.4 24.1 %copy-start.7 = (bf16[1120,1024]{1,0:T(8,128)(2,1)}, bf16[1120,1024]{1,0:T(8,128)(2,1)S(1)}, u32[]{:S(2)}) copy-start(bf16[1120,1024]{1,0:T(8,128)(2,1)S(1)} %add_convert_fusion.left) | copy-start | bytes 6881284
  260.4 24.1 %copy-start.2 = (bf16[1,1024,1120]{1,2,0:T(8,128)(2,1)S(1)}, bf16[1,1024,1120]{1,2,0:T(8,128)(2,1)}, u32[]{:S(2)}) copy-start(bf16[1,1024,1120]{1,2,0:T(8,128)(2,1)} %param.15) | copy-start | bytes 6881284
  331.8 2.3 copy-start.4
  331.8 2.3 copy-start.21
  331.8 2.3 copy-start.23
  331.8 3.3 copy-start.9
  335.2 4.4 copy-start.6
  399.5 2.3 copy-start.3
  401.8 56.9 %collective-permute-start.1 = (f32[1120,128]{1,0:T(8,128)S(1)}, f32[1120,128]{1,0:T(8,128)S(1)}, u32[]{:S(2)}, u32[]{:S(2)}) collective-permute-start(f32[1120,128]{1,0:T(8,128)S(1)} %slice.45), channel_id=1, source_target_pairs={{1,0},{3,2},{5,4},{7,6},{9,8},{11,10},{13,12},{15,14},{17,16},{19,... | collective-permute-start | bytes 1720328 | tf_op jit(solution)/shard_map/ppermute | solution.py:817
  440.1 18.6 %copy-start.31 = (f32[1024]{0:T(1024)S(1)}, f32[1024]{0:T(1024)}, u32[]{:S(2)}) copy-start(f32[1024]{0:T(1024)} %get-tuple-element.42) | copy-start | bytes 12292
  440.1 19.8 %copy-start.13 = (f32[1120]{0:T(1024)S(1)}, f32[1120]{0:T(1024)}, u32[]{:S(2)}) copy-start(f32[1120]{0:T(1024)} %copy-done.12) | copy-start | bytes 13444
  440.1 19.8 %copy-start.20 = (f32[1024]{0:T(1024)S(1)}, f32[1024]{0:T(1024)}, u32[]{:S(2)}) copy-start(f32[1024]{0:T(1024)} %broadcast_multiply_fusion.3) | copy-start | bytes 12292
  463.7 9.0 %collective-permute-start.2 = (f32[4,1120]{1,0:T(4,128)S(1)}, f32[4,1120]{1,0:T(4,128)S(1)}, u32[]{:S(2)}, u32[]{:S(2)}) collective-permute-start(f32[4,1120]{1,0:T(4,128)S(1)} %maximum_multiply_fusion), channel_id=1, source_target_pairs={{0,1},{1,0},{2,3},{3,2},{4,5},{5,4},{6,7},{7,6},{8,9},{9,8},{10,11... | collective-permute-start | bytes 53768 | tf_op jit(solution)/shard_map/ppermute | solution.py:715
  472.8 185.1 %collective-permute-start.3 = (f32[4,1120]{1,0:T(4,128)S(1)}, f32[4,1120]{1,0:T(4,128)S(1)}, u32[]{:S(2)}, u32[]{:S(2)}) collective-permute-start(f32[4,1120]{1,0:T(4,128)S(1)} %fusion.37), channel_id=1, source_target_pairs={{0,2},{1,3},{2,0},{3,1},{4,6},{5,7},{6,4},{7,5},{8,10},{9,11},{10,... | collective-permute-start | bytes 53768 | tf_op jit(solution)/shard_map/ppermute | solution.py:715
  629.2 38.1 %copy-start.11 = (f32[1120]{0:T(1024)S(1)}, f32[1120]{0:T(1024)}, u32[]{:S(2)}) copy-start(f32[1120]{0:T(1024)} %copy-done.10) | copy-start | bytes 13444
  629.2 38.0 %copy-start.15 = (f32[1024]{0:T(1024)S(1)}, f32[1024]{0:T(1024)}, u32[]{:S(2)}) copy-start(f32[1024]{0:T(1024)} %copy-done.14) | copy-start | bytes 12292
  629.2 38.0 %copy-start.18 = (f32[1024]{0:T(1024)S(1)}, f32[1024]{0:T(1024)}, u32[]{:S(2)}) copy-start(f32[1024]{0:T(1024)} %copy-done.17) | copy-start | bytes 12292
  629.3 38.0 %copy-start.22 = (f32[1024]{0:T(1024)S(1)}, f32[1024]{0:T(1024)}, u32[]{:S(2)}) copy-start(f32[1024]{0:T(1024)} %copy-done.21) | copy-start | bytes 12292
  629.3 38.0 %copy-start.24 = (f32[1024]{0:T(1024)S(1)}, f32[1024]{0:T(1024)}, u32[]{:S(2)}) copy-start(f32[1024]{0:T(1024)} %copy-done.23) | copy-start | bytes 12292
  657.9 3.8 collective-permute-start.4
  661.8 3.8 collective-permute-start.5
  665.6 11.7 %copy-start.25 = (f32[1,1120]{1,0:T(1,128)S(1)}, f32[1,1120]{1,0:T(1,128)}, u32[]{:S(2)}) copy-start(f32[1,1120]{1,0:T(1,128)} %get-tuple-element.46) | copy-start | bytes 13444
  665.6 11.7 %copy-start.26 = (f32[1,1120]{1,0:T(1,128)S(1)}, f32[1,1120]{1,0:T(1,128)}, u32[]{:S(2)}) copy-start(f32[1,1120]{1,0:T(1,128)} %get-tuple-element.48) | copy-start | bytes 13444
  665.6 11.7 %copy-start.27 = (f32[1,1120]{1,0:T(1,128)S(1)}, f32[1,1120]{1,0:T(1,128)}, u32[]{:S(2)}) copy-start(f32[1,1120]{1,0:T(1,128)} %get-tuple-element.55) | copy-start | bytes 13444
  665.6 11.7 %copy-start.28 = (f32[1,1120]{1,0:T(1,128)S(1)}, f32[1,1120]{1,0:T(1,128)}, u32[]{:S(2)}) copy-start(f32[1,1120]{1,0:T(1,128)} %get-tuple-element.56) | copy-start | bytes 13444
  665.6 10.3 %collective-permute-start.6 = (f32[4,1120]{1,0:T(4,128)S(1)}, f32[4,1120]{1,0:T(4,128)S(1)}, u32[]{:S(2)}, u32[]{:S(2)}) collective-permute-start(f32[4,1120]{1,0:T(4,128)S(1)} %add.160), channel_id=1, source_target_pairs={{0,16},{1,17},{2,18},{3,19},{4,20},{5,21},{6,22},{7,23},{8,24},{9,... | collective-permute-start | bytes 53768 | tf_op jit(solution)/shard_map/ppermute | solution.py:715
  676.5 1.4 copy-start.16

commit v2 on v1

--- a/solution.py
+++ b/solution.py
@@ -454,32 +454,217 @@
     )(grads)
 
 
-def assemble_kernel(slot_of, *refs):
+def lay(matrix, row, col, block):
+    size = block.shape[0] - RUN
+    matrix[size * row : size * (row + 1), size * col : size * col + MAIN] = block[:size]
+    for start, count, lane in runs(size):
+        piece = block[size : size + count, lane : lane + size - MAIN]
+        matrix[size * row + start : size * row + start + count, size * col + MAIN : size * (col + 1)] = piece
+
+
+def block_specs(gathered, rows, cols, block_of, **mode):
+    shape = (1,) + gathered.shape[1:]
+    pick = lambda i, j, step, v: (v[block_of(step, i, j)], 0, 0)
+    return [
+        pl.BlockSpec(shape, functools.partial(pick, i, j), **mode) for i in range(rows) for j in range(cols)
+    ]
+
+
+def token_tiles(length):
+    tile = GB if length % GB == 0 else HALF
+    return [slice(start, start + tile) for start in range(0, length, tile)]
+
+
+def feature_parts(features):
+    part = -(-features // 256) * 128
+    return [slice(start, min(start + part, features)) for start in range(0, features, part)]
+
+
+def fold(values):
+    return sum(values[:, start : start + 128] for start in range(0, values.shape[1], 128))
+
+
+ONCE = pl.Buffered(1)
+
+
+def front_kernel(slot_of, gain, shift, tokens, *refs):
     del slot_of
-    out = refs[-1]
-    size = out.shape[0]
-    for j, block in enumerate(refs[:-1]):
-        out[:, size * j : size * (j + 1)] = unpack(block[0].astype(F32)).astype(BF16)
-
-
-def assemble(gathered, slot_of, rows, cols, block_of, name):
-    packed_rows, lanes = gathered.shape[1:]
-    size = packed_rows - RUN
-    specs = [
-        pl.BlockSpec((1, packed_rows, lanes), functools.partial(lambda j, i, v: (v[block_of(i, j)], 0, 0), j))
-        for j in range(cols)
-    ]
+    blocks, (weights, out, normed) = refs[:-3], refs[-3:]
+    tiles = token_tiles(tokens.shape[1])
+
+    @pl.when(pl.program_id(0) == 0)
+    def _():
+        for tile in tiles:
+            unit, _ = norm_parts(tokens[:, tile].astype(F32))
+            normed[:, tile] = (unit * gain[...] + shift[...]).astype(BF16)
+
+    row_blocks = math.isqrt(len(blocks))
+    for index, block in enumerate(blocks):
+        lay(weights.at[0], index // row_blocks, index % row_blocks, block.at[0])
+    out[0] = tn(weights[0], normed[...]).astype(BF16)
+
+
+def front(gathered, slot_of, gain, shift, tokens, row_blocks):
+    features, length = tokens.shape
+    square = row_blocks * row_blocks
+    whole = lambda shape: pl.BlockSpec(shape, lambda s, v: (0,) * len(shape), pipeline_mode=ONCE)
+    blocks = block_specs(gathered, row_blocks, row_blocks, lambda s, i, j: s * square + i * row_blocks + j)
     return pl.pallas_call(
-        assemble_kernel,
+        front_kernel,
         grid_spec=pltpu.PrefetchScalarGridSpec(
             num_scalar_prefetch=1,
-            grid=(rows,),
-            in_specs=specs,
-            out_specs=pl.BlockSpec((size, size * cols), lambda i, v: (i, 0)),
+            grid=(3,),
+            in_specs=[whole((features, 1))] * 2 + [whole((features, length))] + blocks,
+            out_specs=[
+                pl.BlockSpec((1, features, features), lambda s, v: (s, 0, 0)),
+                pl.BlockSpec((1, features, length), lambda s, v: (s, 0, 0)),
+                pl.BlockSpec((features, length), lambda s, v: (0, 0)),
+            ],
         ),
-        out_shape=jax.ShapeDtypeStruct((size * rows, size * cols), BF16),
-        name=name,
-    )(slot_of, *([gathered] * cols))
+        out_shape=[
+            jax.ShapeDtypeStruct((3, features, features), BF16),
+            jax.ShapeDtypeStruct((3, features, length), BF16),
+            jax.ShapeDtypeStruct((features, length), BF16),
+        ],
+        compiler_params=pltpu.CompilerParams(vmem_limit_bytes=60 << 20),
+        name="front",
+    )(slot_of, gain, shift, tokens, *([gathered] * square))
+
+
+def gelu_pair(values):
+    square = values * values
+    bend = jnp.tanh(values * (0.7978845608028654 + (0.7978845608028654 * 0.044715) * square))
+    half = 0.5 * values
+    slope = 0.7978845608028654 + (3 * 0.7978845608028654 * 0.044715) * square
+    return half + half * bend, 0.5 + 0.5 * bend + half * (1.0 - bend * bend) * slope
+
+
+def middle_kernel(row_blocks, slot_of, gain, shift, tokens, attended, grad_low, *refs):
+    del slot_of
+    square = row_blocks * row_blocks
+    out_blocks, up_blocks, down_blocks = (refs[square * k : square * (k + 1)] for k in range(3))
+    outs, scratch = refs[3 * square : 3 * square + 8], refs[3 * square + 8 :]
+    block_out, activated, grad_pre, normed, grad_branch, grad_att, grad_middle, sums = outs
+    w_out, w_up, w_down, middle, total, stats, sem = scratch
+    tiles, parts = grad_low.shape[1] // GB, feature_parts(normed.shape[0])
+    at = lambda index: pl.ds(pl.multiple_of(index * GB, GB), GB)
+    step, last = pl.program_id(0), pl.num_programs(0) - 1
+
+    @pl.when(step == 0)
+    def _():
+        copies = [
+            pltpu.make_async_copy(tokens, block_out, sem.at[0]),
+            pltpu.make_async_copy(attended, grad_att, sem.at[1]),
+        ]
+        for copy in copies:
+            copy.start()
+        for index, block in enumerate(out_blocks):
+            lay(w_out, index // row_blocks, index % row_blocks, block.at[0])
+        for copy in copies:
+            copy.wait()
+        def enter(index, carry):
+            tile = at(index)
+            for part in parts:
+                values = block_out[part, tile].astype(F32) + tn(w_out[:, part], grad_att[:, tile])
+                middle[part, tile] = values
+                total[part, tile] = values
+                grad_middle[part, tile] = jnp.zeros_like(values)
+            values = middle[:, tile]
+            average = jnp.mean(values, axis=0, keepdims=True)
+            centred = values - average
+            scale = lax.rsqrt(jnp.mean(centred * centred, axis=0, keepdims=True) + 1e-05)
+            stats[0:1, tile] = average
+            stats[1:2, tile] = scale
+            normed[:, tile] = (centred * scale * gain[...] + shift[...]).astype(BF16)
+            return carry
+
+        lax.fori_loop(0, tiles, enter, 0)
+        sums[...] = jnp.zeros_like(sums)
+
+    for index in range(square):
+        lay(w_up, index // row_blocks, index % row_blocks, up_blocks[index].at[0])
+        lay(w_down, index // row_blocks, index % row_blocks, down_blocks[index].at[0])
+
+    def advance(index, carry):
+        tile = at(index)
+        for part in parts:
+            value, slope = gelu_pair(tn(w_up[:, part], normed[:, tile]))
+            activated[part, tile] = value.astype(BF16)
+            grad_pre[part, tile] = (nn(w_down[part, :], grad_low[:, tile]) * slope).astype(BF16)
+        for part in parts:
+            total[part, tile] += tn(w_down[:, part], activated[:, tile])
+            grad_middle[part, tile] += nn(w_up[part, :], grad_pre[:, tile])
+        return carry
+
+    lax.fori_loop(0, tiles, advance, 0)
+
+    @pl.when(step == last)
+    def _():
+        def leave(index, carry):
+            tile = at(index)
+            block_out[:, tile] = total[:, tile].astype(BF16)
+            scale = stats[1:2, tile]
+            unit = (middle[:, tile] - stats[0:1, tile]) * scale
+            grad = grad_middle[:, tile]
+            sums[0] += fold(grad * unit)
+            sums[1] += fold(grad)
+            values = grad_low[:, tile].astype(F32) + norm_back(unit, scale, gain[...], grad)
+            grad_middle[:, tile] = values
+            grad_branch[:, tile] = values.astype(BF16)
+            for part in parts:
+                grad_att[part, tile] = nn(w_out[part, :], grad_branch[:, tile]).astype(BF16)
+            return carry
+
+        lax.fori_loop(0, tiles, leave, 0)
+
+
+def middle_part(gathered, slot_of, gain, shift, tokens, attended, grad_low, row_blocks, col_blocks):
+    features, length = tokens.shape
+    square = row_blocks * row_blocks
+    hidden = features * col_blocks // row_blocks
+    up_start, down_start = 4 * square, 4 * square + row_blocks * col_blocks
+    whole = lambda *shape: pl.BlockSpec(shape, lambda s, v: (0,) * len(shape), pipeline_mode=ONCE)
+    anywhere = pl.BlockSpec(memory_space=pl.ANY)
+    part = pl.BlockSpec((features, length), lambda s, v: (s, 0))
+    blocks = (
+        block_specs(
+            gathered, row_blocks, row_blocks, lambda s, i, j: 3 * square + i * row_blocks + j, pipeline_mode=ONCE
+        )
+        + block_specs(
+            gathered, row_blocks, row_blocks, lambda s, i, j: up_start + i * col_blocks + s * row_blocks + j
+        )
+        + block_specs(
+            gathered, row_blocks, row_blocks, lambda s, i, j: down_start + (s * row_blocks + i) * row_blocks + j
+        )
+    )
+    shape = jax.ShapeDtypeStruct
+    square_scratch = pltpu.VMEM((features, features), BF16)
+    return pl.pallas_call(
+        functools.partial(middle_kernel, row_blocks),
+        grid_spec=pltpu.PrefetchScalarGridSpec(
+            num_scalar_prefetch=1,
+            grid=(col_blocks // row_blocks,),
+            in_specs=[whole(features, 1)] * 2 + [anywhere] * 2 + [whole(features, length)] + blocks,
+            out_specs=[whole(features, length), part, part]
+            + [whole(features, length)] * 4
+            + [whole(2, features, 128)],
+            scratch_shapes=[square_scratch] * 3
+            + [pltpu.VMEM((features, length), F32)] * 2
+            + [pltpu.VMEM((8, length), F32), pltpu.SemaphoreType.DMA((2,))],
+        ),
+        out_shape=[
+            shape((features, length), BF16),
+            shape((hidden, length), BF16),
+            shape((hidden, length), BF16),
+            shape((features, length), BF16),
+            shape((features, length), BF16),
+            shape((features, length), BF16),
+            shape((features, length), F32),
+            shape((2, features, 128), F32),
+        ],
+        compiler_params=pltpu.CompilerParams(vmem_limit_bytes=63 << 20),
+        name="middle_part",
+    )(slot_of, gain, shift, tokens, attended, grad_low, *([gathered] * (3 * square)))
 
 
 def weight_grad_kernel(block_of, deep, size, slot_of, left, right, *refs):
@@ -551,107 +736,194 @@
     )(*operands)
 
 
-def attention_kernel(scale, qkv, low, high, out, lse):
-    for group in range(low.shape[0]):
+EXTRA = 8
+FAR = -1e30
+
+
+def causal():
+    return lax.broadcasted_iota(jnp.int32, (HALF, HALF), 0) <= lax.broadcasted_iota(jnp.int32, (HALF, HALF), 1)
+
+
+def places(groups):
+    found = []
+    for group in range(groups):
         base = PREFIX + GB * group
-        for h in range(2):
-            seen = slice(base, base + HALF * (h + 1))
-            keys = jnp.concatenate([qkv[1, :, :PREFIX], qkv[1, :, seen]], axis=1)
-            values = jnp.concatenate([qkv[2, :, :PREFIX], qkv[2, :, seen]], axis=1)
-            queries = qkv[0, :, base + HALF * h : base + HALF * (h + 1)]
-            scores = tn(keys, queries) * scale + (high if h else low)[group]
-            top = jnp.max(scores, axis=0, keepdims=True)
-            weights = jnp.exp(scores - top)
-            total = jnp.sum(weights, axis=0, keepdims=True)
-            mine = slice(GB * group + HALF * h, GB * group + HALF * (h + 1))
-            out[:, mine] = (nn(values, weights.astype(BF16)) / total).astype(BF16)
-            lse[0, :, mine] = top + jnp.log(total)
-
-
-def attention_back_kernel(scale, qkv, low, high, out, lse, grad_out, grads):
-    prefix_k = jnp.zeros((out.shape[0], PREFIX), F32)
-    prefix_v = prefix_k
-    for group in range(low.shape[0]):
-        base = PREFIX + GB * group
-        grad_k, grad_v = [None, None], [None, None]
-        for h in range(2):
-            seen = slice(base, base + HALF * (h + 1))
-            keys = jnp.concatenate([qkv[1, :, :PREFIX], qkv[1, :, seen]], axis=1)
-            values = jnp.concatenate([qkv[2, :, :PREFIX], qkv[2, :, seen]], axis=1)
-            own = slice(base + HALF * h, base + HALF * (h + 1))
-            mine = slice(GB * group + HALF * h, GB * group + HALF * (h + 1))
-            queries = qkv[0, :, own]
-            grad_o = grad_out[:, mine]
-            delta = jnp.sum(grad_o.astype(F32) * out[:, mine].astype(F32), axis=0, keepdims=True)
-            weights = jnp.exp(tn(keys, queries) * scale + (high if h else low)[group] - lse[0, :, mine])
-            grad_s = weights * (tn(values, grad_o) - delta)
-            grad_raw = (grad_s * scale).astype(BF16)
-            grads[0, :, own] = nn(keys, grad_raw).astype(BF16)
-            all_k = nt(queries, grad_raw)
-            all_v = nt(grad_o, weights.astype(BF16))
-            prefix_k = prefix_k + all_k[:, :PREFIX]
-            prefix_v = prefix_v + all_v[:, :PREFIX]
-            for i in range(h + 1):
-                part = slice(PREFIX + HALF * i, PREFIX + HALF * (i + 1))
-                grad_k[i] = all_k[:, part] if grad_k[i] is None else grad_k[i] + all_k[:, part]
-                grad_v[i] = all_v[:, part] if grad_v[i] is None else grad_v[i] + all_v[:, part]
-        for i in range(2):
-            part = slice(base + HALF * i, base + HALF * (i + 1))
-            grads[1, :, part] = grad_k[i].astype(BF16)
-            grads[2, :, part] = grad_v[i].astype(BF16)
-    grads[0, :, :PREFIX] = jnp.zeros((out.shape[0], PREFIX), BF16)
-    grads[1, :, :PREFIX] = prefix_k.astype(BF16)
+        low, high = slice(base, base + HALF), slice(base + HALF, base + GB)
+        found.append((low, high, slice(base, base + GB), slice(GB * group, GB * (group + 1))))
+    return found
+
+
+def side(left, right):
+    return jnp.concatenate([left, right], axis=1)
+
+
+def attention_kernel(scale, qkv, extras, out, lse, queries, keys, values, keys_t):
+    head = qkv.shape[1]
+    unit = scale * math.log2(math.e)
+
+    @pl.when(pl.program_id(0) == 0)
+    def _():
+        queries[head:] = extras[0]
+        keys[head:] = extras[1]
+        values[head:] = extras[2]
+
+    queries[:head] = qkv[0]
+    keys[:head] = qkv[1]
+    values[:head] = qkv[2]
+    keys_t[...] = keys[...].T
+    ahead = causal()
+    spots = places(out.shape[1] // GB)
+    scores = []
+    for low, high, both, _ in spots:
+        asked = queries[:, both]
+        scores.append((nn(keys_t[:PREFIX], asked), nn(keys_t[low], asked), nn(keys_t[high], asked[:, HALF:])))
+
+    def peak(array):
+        return jnp.max(array, axis=0, keepdims=True)
+
+    def soft(array, top):
+        return jnp.exp2((array - top) * unit).astype(BF16)
+
+    tops, weights = [], []
+    for prefix, first, second in scores:
+        first = side(jnp.where(ahead, first[:, :HALF], FAR), first[:, HALF:])
+        second = jnp.where(ahead, second, FAR)
+        top = jnp.maximum(peak(prefix), peak(first))
+        top = side(top[:, :HALF], jnp.maximum(top[:, HALF:], peak(second)))
+        tops.append(top)
+        weights.append((soft(prefix, top), soft(first, top), soft(second, top[:, HALF:])))
+    for (low, high, _, mine), top, (prefix, first, second) in zip(spots, tops, weights):
+        sums = nn(values[:, :PREFIX], prefix) + nn(values[:, low], first)
+        sums = side(sums[:, :HALF], sums[:, HALF:] + nn(values[:, high], second))
+        total = sums[head : head + 1]
+        out[:, mine] = (sums[:head] / total).astype(BF16)
+        lse[0, :, mine] = top + jnp.log(total) * (1.0 / scale)
+
+
+def thirds(values):
+    high = values.astype(BF16).astype(F32)
+    rest = values - high
+    middle = rest.astype(BF16).astype(F32)
+    return high, middle, rest - middle
+
+
+def with_rows(base, start, rows):
+    index = lax.broadcasted_iota(jnp.int32, base.shape, 0)
+    for offset, row in enumerate(rows):
+        base = jnp.where(index == start + offset, row, base)
+    return base.astype(BF16)
+
+
+def attention_back_kernel(scale, qkv, extras, out, lse, grad_out, grads, queries, keys, values, grad_o, keys_t, values_t):
+    head, own = qkv.shape[1], out.shape[1]
+    unit = scale * math.log2(math.e)
+
+    @pl.when(pl.program_id(0) == 0)
+    def _():
+        keys[head:] = extras[1]
+        values[head:] = extras[2]
+
+    queries[:head] = qkv[0, :, PREFIX:]
+    keys[:head] = qkv[1]
+    values[:head] = qkv[2]
+    grad_o[:head] = grad_out[...]
+    keys_t[...] = keys[...].T
+    values_t[...] = values[...].T
+    queries[head:] = with_rows(extras[0, :, PREFIX:].astype(F32), 2, thirds(-lse[0]))
+    delta = jnp.sum(grad_out[...].astype(F32) * out[...].astype(F32), axis=0, keepdims=True)
+    grad_o[head:] = with_rows(jnp.zeros((EXTRA, own), F32), 0, thirds(-delta))
+    ahead = causal()
+    spots = places(own // GB)
+
+    def weigh(rows, asked, given, mask):
+        weights = jnp.exp2(nn(keys_t[rows], asked) * unit)
+        if mask == 1:
+            weights = side(jnp.where(ahead, weights[:, :HALF], 0.0), weights[:, HALF:])
+        if mask == 2:
+            weights = jnp.where(ahead, weights, 0.0)
+        return weights.astype(BF16), (weights * nn(values_t[rows], given)).astype(BF16)
+
+    found = []
+    for low, high, _, mine in spots:
+        asked, given = queries[:, mine], grad_o[:, mine]
+        found.append(
+            (
+                weigh(slice(0, PREFIX), asked, given, 0),
+                weigh(low, asked, given, 1),
+                weigh(high, asked[:, HALF:], given[:, HALF:], 2),
+            )
+        )
+    prefix_k = prefix_v = None
+    for (low, high, both, mine), ((p0, d0), (p1, d1), (p2, d2)) in zip(spots, found):
+        asked, given = queries[:head, mine], grad_o[:head, mine]
+        grad_q = nn(keys[:head, :PREFIX], d0) + nn(keys[:head, low], d1)
+        grad_q = side(grad_q[:, :HALF], grad_q[:, HALF:] + nn(keys[:head, high], d2))
+        grads[0, :, both] = (grad_q * scale).astype(BF16)
+        part_k, part_v = nt(asked, d0), nt(given, p0)
+        prefix_k = part_k if prefix_k is None else prefix_k + part_k
+        prefix_v = part_v if prefix_v is None else prefix_v + part_v
+        grads[1, :, low] = (nt(asked, d1) * scale).astype(BF16)
+        grads[2, :, low] = nt(given, p1).astype(BF16)
+        grads[1, :, high] = (nt(asked[:, HALF:], d2) * scale).astype(BF16)
+        grads[2, :, high] = nt(given[:, HALF:], p2).astype(BF16)
+    grads[0, :, :PREFIX] = jnp.zeros((head, PREFIX), BF16)
+    grads[1, :, :PREFIX] = (prefix_k * scale).astype(BF16)
     grads[2, :, :PREFIX] = prefix_v.astype(BF16)
 
 
-def attention_specs(qkv, low, high):
+def attention_specs(qkv):
     _, features, length = qkv.shape
     head, own = features // HEADS, length - PREFIX
-    whole = lambda array: pl.BlockSpec(array.shape, lambda h: (0,) * array.ndim)
     three = pl.BlockSpec((3, head, length), lambda h: (0, h, 0))
+    extra = pl.BlockSpec((3, EXTRA, length), lambda h: (0, 0, 0))
     one = pl.BlockSpec((head, own), lambda h: (h, 0))
     row = pl.BlockSpec((1, 1, own), lambda h: (h, 0, 0))
-    return features, own, head, [three, whole(low), whole(high)], one, row, three
-
-
-def attention(qkv, low, high):
-    features, own, head, specs, one, row, _ = attention_specs(qkv, low, high)
+    wide = lambda columns: pltpu.VMEM((head + EXTRA, columns), BF16)
+    tall = pltpu.VMEM((length, head + EXTRA), BF16)
+    return features, length, own, head, three, extra, one, row, wide, tall
+
+
+def attention(qkv, extras):
+    features, length, own, head, three, extra, one, row, wide, tall = attention_specs(qkv)
     return pl.pallas_call(
         functools.partial(attention_kernel, head ** (-0.5)),
         grid=(HEADS,),
-        in_specs=specs,
+        in_specs=[three, extra],
         out_specs=[one, row],
         out_shape=[
             jax.ShapeDtypeStruct((features, own), BF16),
             jax.ShapeDtypeStruct((HEADS, 1, own), F32),
         ],
+        scratch_shapes=[wide(length), wide(length), wide(length), tall],
         cost_estimate=cost(8 * features * own * GB, 2 * qkv.size, HEADS * own * GB),
         name="attention",
-    )(qkv, low, high)
-
-
-def attention_back(qkv, low, high, out, lse, grad_out):
-    features, own, head, specs, one, row, three = attention_specs(qkv, low, high)
+    )(qkv, extras)
+
+
+def attention_back(qkv, extras, out, lse, grad_out):
+    features, length, own, head, three, extra, one, row, wide, tall = attention_specs(qkv)
     return pl.pallas_call(
         functools.partial(attention_back_kernel, head ** (-0.5)),
         grid=(HEADS,),
-        in_specs=specs + [one, row, one],
+        in_specs=[three, extra, one, row, one],
         out_specs=three,
         out_shape=jax.ShapeDtypeStruct(qkv.shape, BF16),
+        scratch_shapes=[wide(own), wide(length), wide(length), wide(own), tall, tall],
         cost_estimate=cost(20 * features * own * GB, 4 * qkv.size, HEADS * own * GB),
         name="attention_back",
-    )(qkv, low, high, out, lse, grad_out)
-
-
-def score_biases(alive, prefix_alive, later):
-    groups = alive.shape[0] // GB
-    live = alive.reshape(groups, GB, 1)
-    square = (groups, HALF, HALF)
-    prefix = jnp.broadcast_to(prefix_alive[None, :, None] & later[:, None, None], (groups, PREFIX, HALF))
-    ahead = (jnp.arange(HALF)[:, None] <= jnp.arange(HALF)[None, :])[None]
-    low = jnp.concatenate([prefix, live[:, :HALF] & ahead], axis=1)
-    high = jnp.concatenate([prefix, jnp.broadcast_to(live[:, :HALF], square), live[:, HALF:] & ahead], axis=1)
-    return jnp.where(low, 0.0, -1e30).astype(F32), jnp.where(high, 0.0, -1e30).astype(F32)
+    )(qkv, extras, out, lse, grad_out)
+
+
+def score_extras(alive, prefix_alive, later):
+    length = PREFIX + alive.shape[0]
+    dead = jnp.where(jnp.concatenate([prefix_alive, alive]), 0.0, FAR)
+    prefix = (jnp.arange(length) < PREFIX).astype(F32)
+    barred = jnp.concatenate([jnp.zeros((PREFIX,)), jnp.where(jnp.repeat(later, GB), 0.0, FAR)])
+    one, zero = jnp.ones((length,)), jnp.zeros((length,))
+    query_rows = jnp.stack([one, barred] + [zero] * 6)
+    key_rows = jnp.stack([dead, prefix] + [one] * 3 + [zero] * 3)
+    value_rows = jnp.stack([one] * 3 + [zero] * 5)
+    return jnp.stack([query_rows, key_rows, value_rows]).astype(BF16)
 
 
 def split(values):
@@ -764,11 +1036,6 @@
     def down_of(i, j):
         return 4 * square + row_blocks * col_blocks + i * row_blocks + j
 
-    w_three = assemble(gathered, slot_of, row_blocks, 3 * row_blocks, three_of, "lay_three")
-    w_out = assemble(gathered, slot_of, row_blocks, row_blocks, out_of, "lay_out")
-    w_up = assemble(gathered, slot_of, row_blocks, col_blocks, up_of, "lay_up")
-    w_down = assemble(gathered, slot_of, col_blocks, row_blocks, down_of, "lay_down")
-
     own_tokens = tokens.reshape(length, features).T
     prefix_tokens = own_tokens[:, :PREFIX]
     if cores == 2:
@@ -776,42 +1043,30 @@
         prefix_tokens = jnp.where(seq_index == 0, prefix_tokens, arrived)
     else:
         prefix_tokens = lax.all_gather(prefix_tokens, "seq")[0]
-    inputs = own_tokens.astype(F32)
     gain_one, shift_one = norm_gains[0][:, None], norm_shifts[0][:, None]
     gain_two, shift_two = norm_gains[1][:, None], norm_shifts[1][:, None]
-    unit_all, _ = norm_parts(jnp.concatenate([prefix_tokens, own_tokens], axis=1).astype(F32))
-    normed_in = (unit_all * gain_one + shift_one).astype(BF16)
-    qkv = tn(w_three, normed_in).astype(BF16).reshape(3, features, PREFIX + length)
+    all_tokens = jnp.concatenate([prefix_tokens, own_tokens], axis=1)
+    w_three, qkv, normed_in = front(gathered, slot_of, gain_one, shift_one, all_tokens, row_blocks)
 
     position = seq_index * length + jnp.arange(length, dtype=jnp.int32)
     alive = jnp.where(position < PREFIX, position < prefix_len[0], pad_mask[0] == 1)
     prefix_alive = jnp.arange(PREFIX, dtype=jnp.int32) < prefix_len[0]
     groups = length // GB
     later = seq_index * groups + jnp.arange(groups) > 0
-    low, high = score_biases(alive, prefix_alive, later)
-
-    attended, log_total = attention(qkv, low, high)
-    middle = inputs + tn(w_out, attended)
-    unit_two, scale_two = norm_parts(middle)
-    normed_mid = (unit_two * gain_two + shift_two).astype(BF16)
-    up_pre = tn(w_up, normed_mid)
-    activated, gelu_back = jax.vjp(functools.partial(jax.nn.gelu, approximate=True), up_pre)
-    activated = activated.astype(BF16)
-    block_out = (middle + tn(w_down, activated)).astype(BF16)
+    extras = score_extras(alive, prefix_alive, later)
 
     grad_low = cotangent.reshape(length, features).T
-    grad_pre = gelu_back(nn(w_down, grad_low))[0].astype(BF16)
+    attended, log_total = attention(qkv, extras)
+    block_out, activated, grad_pre, normed_mid, grad_branch, grad_att, grad_middle, sums = middle_part(
+        gathered, slot_of, gain_two, shift_two, own_tokens, attended, grad_low, row_blocks, col_blocks
+    )
     grads = weight_grad(activated, grad_low, slot_of, None, slot_count, size, down_of, "grad_down")
     grads = weight_grad(normed_mid, grad_pre, slot_of, grads, slot_count, size, up_of, "grad_up")
-    grad_normed_two = nn(w_up, grad_pre)
-    grad_middle = grad_low.astype(F32) + norm_back(unit_two, scale_two, gain_two, grad_normed_two)
-    grad_branch = grad_middle.astype(BF16)
     grads = weight_grad(attended, grad_branch, slot_of, grads, slot_count, size, out_of, "grad_out")
-    grad_att = nn(w_out, grad_branch).astype(BF16)
-    grad_three = attention_back(qkv, low, high, attended, log_total, grad_att)
+    grad_three = attention_back(qkv, extras, attended, log_total, grad_att)
     grad_three = grad_three.reshape(3 * features, PREFIX + length)
     grads = weight_grad(normed_in, grad_three, slot_of, grads, slot_count, size, three_of, "grad_three")
-    grad_all = nn(w_three, grad_three)
+    grad_all = sum(nn(w_three[k], grad_three[features * k : features * (k + 1)]) for k in range(3))
     prefix_part = grad_all[:, :PREFIX]
     if cores == 2:
         prefix_part = prefix_part + lax.ppermute(prefix_part, "seq", [(1, 0)])
@@ -819,7 +1074,7 @@
         prefix_part = lax.psum(prefix_part, "seq")
     prefix_part = jnp.where(seq_index == 0, prefix_part, 0.0)
     grad_normed = grad_all[:, PREFIX:] + jnp.pad(prefix_part, ((0, 0), (0, length - PREFIX)))
-    unit_one, scale_one = norm_parts(inputs)
+    unit_one, scale_one = norm_parts(own_tokens.astype(F32))
     grad_input = grad_middle + norm_back(unit_one, scale_one, gain_one, grad_normed)
 
     grad_scale = 1.0 / math.sqrt(length * chips * cores)
@@ -827,8 +1082,8 @@
         [
             jnp.sum(grad_normed * unit_one, axis=1),
             jnp.sum(grad_normed, axis=1),
-            jnp.sum(grad_normed_two * unit_two, axis=1),
-            jnp.sum(grad_normed_two, axis=1),
+            jnp.sum(sums[0], axis=1),
+            jnp.sum(sums[1], axis=1),
         ]
     )
     norm_terms = norm_terms * grad_scale

time: 682 us -> 613 us (0.90)
  matrix products: 131 us -> 17.9 us
  Pallas kernels: 492 us -> 539 us
    pallas_call x4 -> x2, Pallas kernels: 46.5 us -> 124 us  [the longest x1 99.9 us: middle_part(): pl.pallas_call(functools.partial(middle_kernel, row_blocks), grid_spec=pl...]
    dot_general x4 -> x0, matrix products: 65.1 us -> none  [tn(): lax.dot_general(left, right, (((0,), (0,)), ((), ())), preferred_element_...]
    dot_general x4 -> x3, matrix products: 66 us -> 17.9 us  [nn(): lax.dot_general(left, right, (((1,), (0,)), ((), ())), preferred_element_...]
    pallas_call x1, Pallas kernels: 45.5 us -> 25.8 us  [attention_back(): pl.pallas_call(functools.partial(attention_back_kernel, head ** (-0.5)),...]
    pallas_call x1, Pallas kernels: 31.9 us -> 19.2 us  [attention(): pl.pallas_call(functools.partial(attention_kernel, head ** (-0.5)), grid=...]
  transfers between devices with their start and end apart: 7 -> 7, of which waited for: 2 -> 1; matrix products, arithmetic and copies ran while one was open for 5% -> 3% of each run, Pallas kernels for 61% -> 61%
where the time goes in v2:
time: 613 us; the launch traced here: 603 us
  Pallas kernels  539 us (88%)
  other arithmetic  21.4 us (3%)
  matrix products  17.9 us (3%)
  local copies, waits for them, and re-layouts  10.1 us (2%)
  starting transfers between devices  8.38 us (1%)
    pallas_call x1, Pallas kernels, reduce_slots(): pl.pallas_call(functools.partial(reduce_kernel, slots), out_shape=jax.Sha...  138 us
    pallas_call x1, Pallas kernels, gather_slots(): pl.pallas_call(functools.partial(gather_kernel, slots), out_shape=jax.Sha...  133 us
    pallas_call x1, Pallas kernels, middle_part(): pl.pallas_call(functools.partial(middle_kernel, row_blocks), grid_spec=pl...  99.9 us
    pallas_call x4, Pallas kernels, weight_grad(): pl.pallas_call(functools.partial(weight_grad_kernel, block_of, deep, size...  61.9 us
    pallas_call x1, Pallas kernels, optimizer(): pl.pallas_call(functools.partial(optimizer_kernel, scale), grid=(slots,),...  28.6 us
    pallas_call x1, Pallas kernels, attention_back(): pl.pallas_call(functools.partial(attention_back_kernel, head ** (-0.5)),...  25.8 us
    pallas_call x1, Pallas kernels, front(): pl.pallas_call(front_kernel, grid_spec=pltpu.PrefetchScalarGridSpec(num_s...  24.2 us
    pallas_call x1, Pallas kernels, attention(): pl.pallas_call(functools.partial(attention_kernel, head ** (-0.5)), grid=...  19.2 us
  transfers between devices with their start and end apart: 7, of which 1 were waited for; matrix products, arithmetic and copies ran while one was open for 3% of the time, Pallas kernels for 61%

profile of v2, /device:TPU:0, one launch (start us, length us, event | category | flops | bytes accessed | tf_op | source)
XLA Modules:
  0.0 602.6 jit_solution(18204009196341603287)
XLA Ops:
  0.6 0.0 copy-start.14
  0.7 0.0 copy-start.15
  0.7 0.0 copy-start.16
  0.7 0.0 copy-start.17
  0.7 1.0 slice.76
  1.7 2.4 collective-permute-start
  4.1 2.0 convert_reduce_fusion
  6.8 0.1 broadcast_bitcast_fusion
  6.9 0.0 copy-start.6
  6.9 2.3 fusion.11
  9.2 0.6 add_rsqrt_fusion
  9.8 0.0 copy-done.14
  9.8 0.6 fusion.27
  10.4 0.0 copy-done.15
  10.4 1.2 fusion.26
  11.6 0.1 pad.23.clone
  11.7 0.0 copy-done.16
  11.8 0.0 copy-done.6
  11.8 0.1 maximum_bitcast_fusion
  11.9 1.1 copy.28.gain
  12.9 1.1 copy.30.gain
  14.0 1.1 copy.31.shift
  15.1 1.1 copy.29.shift
  16.2 7.9 %pack_slots.1.placed = bf16[192,312,256]{2,1,0:T(8,128)(2,1)} custom-call(s32[1]{0:T(128)} %bitcast.7.chip, bf16[12,280,280]{2,1,0:T(8,128)(2,1)} %block.1), custom_call_target="tpu_custom_call" | custom-call | tf_op jit(solution)/shard_map/pack_slots/pallas_call | solution.py:84
  24.1 132.8 %gather_slots.1.refs_0_.refs_1_.refs_2_.refs_3_.refs_4_.refs_5_.refs_6_.refs_7_.refs_8_.refs_9_.refs_10_.refs_11_.refs_12_.refs_13_.refs_14_.refs_15_.refs_16_.refs_17_.refs_18_.refs_19_.refs_20_.refs_21_.refs_22_.refs_23_.refs_24_.refs_25_.refs_26_.refs_27_.refs_28_.refs_29_.refs_30_.refs_31_.refs_32_.refs_33_.refs_34_.refs_35_.refs_36_.refs_37_.refs_38_.refs_39_.refs_40_.refs_41_.refs_42_.refs_43_.refs_44_.refs_45_.refs_46_.refs_47_ = bf16[192,312,256]{2,1,0:T(8,128)(2,1)} custom-call(bf16[192,312,256]{2,1,0:T(8,128)(2,1)} %pack_slots.1.placed), custom_call_target="tpu_custom_call", output_to_operand_aliasing={{}: (0, {})} | custom-call | tf_op jit(solution)/shard_map/gather_slots/pallas_call | solution.py:281
  156.9 1.7 scatter_custom_fusion.slot_of
  158.7 0.1 stack.55
  158.7 0.6 pad_maximum_fusion.1.extras
  159.4 0.0 collective-permute-done
  159.4 0.0 copy-done
  159.4 0.1 broadcast_select_fusion
  159.4 1.7 pad_maximum_fusion.tokens
  161.2 24.2 %front.1 = (bf16[3,1120,1120]{2,1,0:T(8,128)(2,1)}, bf16[3,1120,1152]{2,1,0:T(8,128)(2,1)}, bf16[1120,1152]{1,0:T(8,128)(2,1)}) custom-call(s32[192]{0:T(256)} %scatter_custom_fusion.slot_of, f32[1120,1]{1,0:T(8,128)} %copy.28.gain, f32[1120,1]{1,0:T(8,128)} %copy.29.shift, bf16[1120,1152]{1,0:T(8,128)(2,1)} %pad_maximum_fusion.tokens, ...), custom_call_target="tpu_custom_call" | custom-call | tf_op jit(solution)/shard_map/front/pallas_call | solution.py:512
  185.4 19.2 %attention.1 = (bf16[1120,1024]{1,0:T(8,128)(2,1)}, f32[20,1,1024]{2,1,0:T(1,128)}) custom-call(bf16[3,1120,1152]{2,1,0:T(8,128)(2,1)} %get-tuple-element.29.qkv, bf16[3,8,1152]{2,1,0:T(8,128)(2,1)} %pad_maximum_fusion.1.extras), custom_call_target="tpu_custom_call" | custom-call | flops 2348810240 | bytes 7741440 | tf_op jit(solution)/shard_map/attention/pallas_call | solution.py:888
  204.6 99.9 %middle_part.1 = (bf16[1120,1024]{1,0:T(8,128)(2,1)}, bf16[4480,1024]{1,0:T(8,128)(2,1)}, bf16[4480,1024]{1,0:T(8,128)(2,1)}, bf16[1120,1024]{1,0:T(8,128)(2,1)}...) custom-call(s32[192]{0:T(256)} %scatter_custom_fusion.slot_of, ...), custom_call_target="tpu_custom_call" | custom-call | tf_op jit(solution)/shard_map/middle_part/pallas_call | solution.py:642
  304.5 1.6 slice_reduce_fusion.1
  306.1 25.8 %attention_back.1 = bf16[3,1120,1152]{2,1,0:T(8,128)(2,1)} custom-call(bf16[3,1120,1152]{2,1,0:T(8,128)(2,1)} %get-tuple-element.29.qkv, bf16[3,8,1152]{2,1,0:T(8,128)(2,1)} %pad_maximum_fusion.1.extras, bf16[1120,1024]{1,0:T(8,128)(2,1)} %get-tuple-element.30.attended.out.left, f32[20,1,1024]{2,1,0:T(1,128)} %get-tuple-element.34.lse, ...), custom_call_target="tpu_custom_call" | custom-call | flops 5872025600 | bytes 15482880 | tf_op jit(solution)/shard_map/attention_back/pallas_call | solution.py:905
  331.9 6.5 %fusion.12 = f32[1120,1152]{1,0:T(8,128)S(1)} fusion(bf16[3,1120,1152]{2,1,0:T(8,128)(2,1)} %attention_back.1, bf16[3,1120,1120]{2,1,0:T(8,128)(2,1)} %get-tuple-element.33), kind=kOutput, calls=%fused_computation.22 | convolution fusion | flops 2890137600 | bytes 10321920 | tf_op jit(solution)/shard_map/dot_general | solution.py:63
  338.5 5.7 convolution_add_fusion.1
  344.1 5.7 convolution_add_fusion
  349.9 1.3 collective-permute-start.1
  351.2 0.9 copy-done.2
  352.1 18.7 %grad_down.1.refs_0_ = bf16[192,312,256]{2,1,0:T(8,128)(2,1)} custom-call(s32[192]{0:T(256)} %scatter_custom_fusion.slot_of, bf16[4480,1024]{1,0:T(8,128)(2,1)} %get-tuple-element.41.left, bf16[1120,1024]{1,0:T(8,128)(2,1)} %bitcast.63), custom_call_target="tpu_custom_call" | custom-call | flops 10276044800 | bytes 21504000 | tf_op jit(solution)/shard_map/grad_down/pallas_call | solution.py:713
  370.8 0.0 collective-permute-done.1
  370.8 1.1 add_select_fusion
  372.0 3.8 fusion.10
  375.8 0.4 collective-permute-start.2
  376.3 18.4 %grad_up.1.refs_0_ = bf16[192,312,256]{2,1,0:T(8,128)(2,1)} custom-call(s32[192]{0:T(256)} %scatter_custom_fusion.slot_of, bf16[1120,1024]{1,0:T(8,128)(2,1)} %get-tuple-element.39.left, bf16[4480,1024]{1,0:T(8,128)(2,1)} %get-tuple-element.40.right, bf16[192,312,256]{2,1,0:T(8,128)(2,1)} %grad_down.1.refs_0_), custom_call_target="tpu_custom_call", output_to_operand_aliasing={{}: (3, {})} | custom-call | flops 10276044800 | bytes 21504000 | tf_op jit(solution)/shard_map/grad_up/pallas_call | solution.py:713
  394.7 0.0 collective-permute-done.2
  394.7 1.3 collective-permute-start.3
  396.0 7.5 %grad_out.1.refs_0_ = bf16[192,312,256]{2,1,0:T(8,128)(2,1)} custom-call(s32[192]{0:T(256)} %scatter_custom_fusion.slot_of, bf16[1120,1024]{1,0:T(8,128)(2,1)} %get-tuple-element.30.attended.out.left, bf16[1120,1024]{1,0:T(8,128)(2,1)} %get-tuple-element.38.right, bf16[192,312,256]{2,1,0:T(8,128)(2,1)} %grad_up.1.refs_0_), custom_call_target="tpu_custom_call", output_to_operand_aliasing={{}: (3, {})} | custom-call | flops 2569011200 | bytes 7096320 | tf_op jit(solution)/shard_map/grad_out/pallas_call | solution.py:713
  403.5 0.0 collective-permute-done.3
  403.5 0.9 collective-permute-start.4
  404.5 17.3 %grad_three.1.grads = bf16[192,312,256]{2,1,0:T(8,128)(2,1)} custom-call(s32[192]{0:T(256)} %scatter_custom_fusion.slot_of, bf16[1120,1152]{1,0:T(8,128)(2,1)} %get-tuple-element.37.left, bf16[3360,1152]{1,0:T(8,128)(2,1)} %bitcast.64, bf16[192,312,256]{2,1,0:T(8,128)(2,1)} %grad_out.1.refs_0_), custom_call_target="tpu_custom_call", output_to_operand_aliasing={{}: (3, {})} | custom-call | flops 8670412800 | bytes 17848320 | tf_op jit(solution)/shard_map/grad_three/pallas_call | solution.py:713
  421.7 138.4 %reduce_slots.1.packed = f32[12,312,256]{2,1,0:T(8,128)} custom-call(bf16[192,312,256]{2,1,0:T(8,128)(2,1)} %grad_three.1.grads), custom_call_target="tpu_custom_call" | custom-call | tf_op jit(solution)/shard_map/reduce_slots/pallas_call | solution.py:435
  560.2 28.6 %optimizer.1 = (f32[12,280,280]{2,1,0:T(8,128)}, f32[12,280,280]{2,1,0:T(8,128)}, f32[12,280,280]{2,1,0:T(8,128)}, f32[12,280,280]{2,1,0:T(8,128)}, bf16[12,280,...) custom-call(f32[12,312,256]{2,1,0:T(8,128)} %reduce_slots.1.packed, f32[12,280,280]{2,1,0:T(8,128)} %master.1, ...), custom_call_target="tpu_custom_call" | custom-call | tf_op jit(solution)/shard_map/optimizer/pallas_call | solution.py:959
  588.8 0.0 collective-permute-done.4
  588.8 0.6 collective-permute-start.5
  589.5 3.2 collective-permute-done.5
  592.7 1.5 collective-permute-start.6
  594.1 6.0 fusion.9
  600.2 0.0 collective-permute-done.6
  600.2 0.6 multiply_reduce_fusion.1
  601.5 0.6 maximum_subtract_fusion
  (52 shorter events, 0.3 us)
Async XLA Ops:
  0.6 9.2 %copy-start.14 = (f32[2,1120]{1,0:T(2,128)S(1)}, f32[2,1120]{1,0:T(2,128)}, u32[]{:S(2)}) copy-start(f32[2,1120]{1,0:T(2,128)} %param.19) | copy-start | bytes 26884
  0.7 9.8 %copy-start.15 = (f32[2,1120]{1,0:T(2,128)S(1)}, f32[2,1120]{1,0:T(2,128)}, u32[]{:S(2)}) copy-start(f32[2,1120]{1,0:T(2,128)} %param.18) | copy-start | bytes 26884
  0.7 11.0 %copy-start.16 = (s32[1,1024]{1,0:T(1,128)S(1)}, s32[1,1024]{1,0:T(1,128)}, u32[]{:S(2)}) copy-start(s32[1,1024]{1,0:T(1,128)} %param.16) | copy-start | bytes 12292
  0.7 11.2 %copy-start.17 = (s32[192]{0:T(256)S(1)}, s32[192]{0:T(256)}, u32[]{:S(2)}) copy-start(s32[192]{0:T(256)} %param.20) | copy-start | bytes 2308
  1.7 157.7 %collective-permute-start = (bf16[1120,128]{1,0:T(8,128)(2,1)S(1)}, bf16[1120,128]{1,0:T(8,128)(2,1)S(1)}, u32[]{:S(2)}, u32[]{:S(2)}) collective-permute-start(bf16[1120,128]{1,0:T(8,128)(2,1)S(1)} %slice.76), channel_id=1, source_target_pairs={{0,1},{2,3},{4,5},{6,7},{8,9},{10,11},{12,13},{14,15},{16,17},{18,... | collective-permute-start | bytes 860168 | tf_op jit(solution)/shard_map/ppermute | solution.py:1042
  6.9 4.9 copy-start.6
  24.1 134.6 %copy-start.13 = (bf16[1,8,1152]{2,1,0:T(8,128)(2,1)S(1)}, bf16[1,8,1152]{2,1,0:T(8,128)(2,1)}, u32[]{:S(2)}) copy-start(bf16[1,8,1152]{2,1,0:T(8,128)(2,1)} %constant.16.clone.1) | copy-start | bytes 55300
  24.1 135.2 %copy-start = (bf16[1,1024,1120]{1,2,0:T(8,128)(2,1)S(1)}, bf16[1,1024,1120]{1,2,0:T(8,128)(2,1)}, u32[]{:S(2)}) copy-start(bf16[1,1024,1120]{1,2,0:T(8,128)(2,1)} %param.14) | copy-start | bytes 6881284
  331.9 6.5 %copy-start.3 = (bf16[3,1120,1152]{2,1,0:T(8,128)(2,1)S(1)}, bf16[3,1120,1152]{2,1,0:T(8,128)(2,1)}, u32[]{:S(2)}) copy-start(bf16[3,1120,1152]{2,1,0:T(8,128)(2,1)} %attention_back.1) | copy-start | bytes 23224324
  349.8 2.3 copy-start.2
  349.9 20.9 %collective-permute-start.1 = (f32[1120,128]{1,0:T(8,128)S(1)}, f32[1120,128]{1,0:T(8,128)S(1)}, u32[]{:S(2)}, u32[]{:S(2)}) collective-permute-start(f32[1120,128]{1,0:T(8,128)S(1)} %slice.81), channel_id=1, source_target_pairs={{1,0},{3,2},{5,4},{7,6},{9,8},{11,10},{13,12},{15,14},{17,16},{19,... | collective-permute-start | bytes 1720328 | tf_op jit(solution)/shard_map/ppermute | solution.py:1072
  352.1 19.8 %copy-start.1 = (bf16[1,1024,1120]{1,2,0:T(8,128)(2,1)S(1)}, bf16[1,1024,1120]{1,2,0:T(8,128)(2,1)}, u32[]{:S(2)}) copy-start(bf16[1,1024,1120]{1,2,0:T(8,128)(2,1)} %param.14) | copy-start | bytes 6881284
  352.1 19.9 %copy-start.5 = (f32[1120]{0:T(1024)S(1)}, f32[1120]{0:T(1024)}, u32[]{:S(2)}) copy-start(f32[1120]{0:T(1024)} %get-tuple-element.58) | copy-start | bytes 13444
  352.1 19.9 %copy-start.7 = (f32[1024]{0:T(1024)S(1)}, f32[1024]{0:T(1024)}, u32[]{:S(2)}) copy-start(f32[1024]{0:T(1024)} %copy-done.6) | copy-start | bytes 12292
  352.1 19.9 %copy-start.8 = (f32[1024]{0:T(1024)S(1)}, f32[1024]{0:T(1024)}, u32[]{:S(2)}) copy-start(f32[1024]{0:T(1024)} %add_rsqrt_fusion) | copy-start | bytes 12292
  375.8 18.8 %collective-permute-start.2 = (f32[4,1120]{1,0:T(4,128)S(1)}, f32[4,1120]{1,0:T(4,128)S(1)}, u32[]{:S(2)}, u32[]{:S(2)}) collective-permute-start(f32[4,1120]{1,0:T(4,128)S(1)} %maximum_multiply_fusion), channel_id=1, source_target_pairs={{0,1},{1,0},{2,3},{3,2},{4,5},{5,4},{6,7},{7,6},{8,9},{9,8},{10,11... | collective-permute-start | bytes 53768 | tf_op jit(solution)/shard_map/ppermute | solution.py:987
  394.7 8.8 %collective-permute-start.3 = (f32[4,1120]{1,0:T(4,128)S(1)}, f32[4,1120]{1,0:T(4,128)S(1)}, u32[]{:S(2)}, u32[]{:S(2)}) collective-permute-start(f32[4,1120]{1,0:T(4,128)S(1)} %fusion.25), channel_id=1, source_target_pairs={{0,2},{1,3},{2,0},{3,1},{4,6},{5,7},{6,4},{7,5},{8,10},{9,11},{10,... | collective-permute-start | bytes 53768 | tf_op jit(solution)/shard_map/ppermute | solution.py:987
  403.5 185.3 %collective-permute-start.4 = (f32[4,1120]{1,0:T(4,128)S(1)}, f32[4,1120]{1,0:T(4,128)S(1)}, u32[]{:S(2)}, u32[]{:S(2)}) collective-permute-start(f32[4,1120]{1,0:T(4,128)S(1)} %fusion.28), channel_id=1, source_target_pairs={{0,4},{1,5},{2,6},{3,7},{4,0},{5,1},{6,2},{7,3},{8,12},{9,13},{10,... | collective-permute-start | bytes 53768 | tf_op jit(solution)/shard_map/ppermute | solution.py:987
  588.8 3.8 collective-permute-start.5
  592.7 7.5 %collective-permute-start.6 = (f32[4,1120]{1,0:T(4,128)S(1)}, f32[4,1120]{1,0:T(4,128)S(1)}, u32[]{:S(2)}, u32[]{:S(2)}) collective-permute-start(f32[4,1120]{1,0:T(4,128)S(1)} %add.89), channel_id=1, source_target_pairs={{0,16},{1,17},{2,18},{3,19},{4,20},{5,21},{6,22},{7,23},{8,24},{9,... | collective-permute-start | bytes 53768 | tf_op jit(solution)/shard_map/ppermute | solution.py:987
  594.1 7.4 %copy-start.9 = (f32[1,1120]{1,0:T(1,128)S(1)}, f32[1,1120]{1,0:T(1,128)}, u32[]{:S(2)}) copy-start(f32[1,1120]{1,0:T(1,128)} %get-tuple-element.56) | copy-start | bytes 13444
  594.1 7.4 %copy-start.10 = (f32[1,1120]{1,0:T(1,128)S(1)}, f32[1,1120]{1,0:T(1,128)}, u32[]{:S(2)}) copy-start(f32[1,1120]{1,0:T(1,128)} %get-tuple-element.60) | copy-start | bytes 13444
  594.1 7.4 %copy-start.11 = (f32[1,1120]{1,0:T(1,128)S(1)}, f32[1,1120]{1,0:T(1,128)}, u32[]{:S(2)}) copy-start(f32[1,1120]{1,0:T(1,128)} %get-tuple-element.61) | copy-start | bytes 13444
  594.1 7.4 %copy-start.12 = (f32[1,1120]{1,0:T(1,128)S(1)}, f32[1,1120]{1,0:T(1,128)}, u32[]{:S(2)}) copy-start(f32[1,1120]{1,0:T(1,128)} %get-tuple-element.64) | copy-start | bytes 13444
  600.8 1.4 copy-start.4

commit v3 on v2

--- a/solution.py
+++ b/solution.py
@@ -131,17 +131,6 @@
             device_id_type=MESH,
         )
 
-    def arrival(label):
-        ref = out.at[pl.ds(0, half)]
-        return pltpu.make_async_remote_copy(
-            src_ref=ref,
-            dst_ref=ref,
-            send_sem=send.at[label],
-            recv_sem=recv.at[label],
-            device_id=(me, 1 - core),
-            device_id_type=MESH,
-        )
-
     def col(zz):
         return me + 4 * (zz - z)
 
@@ -290,12 +279,45 @@
     )(placed)
 
 
-R_TWIN, R_SECOND, R_FIRST, R_LINE, R_DONE, REDUCE_LABELS = 0, 16, 24, 28, 32, 33
-
-
-def reduce_kernel(slots, grads, out, own, r_twin, r_second, r_first, r_line, total, load, send, recv, save):
+R_TWIN, R_SECOND, R_FIRST, R_LINE, R_DONE, R_PREFIX, R_FLOW, REDUCE_LABELS = 0, 16, 24, 28, 32, 33, 34, 42
+RING = 3
+PANELS = 5
+
+
+def reduce_kernel(
+    slots,
+    grads,
+    w_three,
+    grad_three,
+    tokens,
+    grad_middle,
+    params,
+    sums,
+    out,
+    grad_input,
+    norm_sums,
+    ring,
+    r_twin,
+    r_second,
+    r_first,
+    r_line,
+    total,
+    weights,
+    inner,
+    acc,
+    prefix,
+    given,
+    folds,
+    flow,
+    arrived,
+    load,
+    send,
+    recv,
+    save,
+):
     me, core, z, first, second = place()
     half = slots // 2
+    features, length = acc.shape
     line = [(me + 4 * ((z + r) % 4 - z), core) for r in range(1, 4)]
     greet([(me + first, core), (me + second, core), (me, 1 - core)] + line)
 
@@ -304,10 +326,6 @@
 
     def chip_at(zz, a, b):
         return me + 4 * (zz - z) + a * first + b * second
-
-    def load_own(zz, a, b):
-        chip = chip_at(zz, a, b)
-        return pltpu.make_async_copy(piece(chip, core), own.at[chip], load.at[chip])
 
     def remote(src, dst, label, dp, c):
         return pltpu.make_async_remote_copy(
@@ -335,82 +353,159 @@
         zz = (z + r) % 4
         return remote(r_twin.at[chip_at(zz, 0, 0)], r_line.at[r - 1], R_LINE + r, chip_at(zz, 0, 0), core)
 
-    def add_up(chip, others):
+    order = [2, 1, 3, 0]
+    where = [(z + r) % 4 for r in order]
+    turns = []
+    for index in range(3):
+        turns += [(where[index], 1, 1), (where[index], 0, 1)]
+    turns += [(where[0], 1, 0), (where[3], 1, 1), (where[3], 0, 1), (where[0], 0, 0), (where[1], 1, 0)]
+    turns += [(where[2], 1, 0), (where[1], 0, 0), (where[3], 1, 0), (where[2], 0, 0), (where[3], 0, 0)]
+
+    def load_own(turn):
+        return pltpu.make_async_copy(piece(chip_at(*turns[turn]), core), ring.at[turn % RING], load.at[turn % RING])
+
+    def add_up(turn, others):
+        chip = chip_at(*turns[turn])
+        load_own(turn).wait()
+        twin(*turns[turn]).wait_recv()
+
         def body(s, carry):
-            value = own[chip, s].astype(F32) + r_twin[chip, s].astype(F32)
+            value = ring[turn % RING, s].astype(F32) + r_twin[chip, s].astype(F32)
             for ref, index in others:
                 value = value + ref[index, s].astype(F32)
-            r_twin[chip, s] = value.astype(BF16)
+            if turn < len(turns) - 1:
+                r_twin[chip, s] = value.astype(BF16)
+            else:
+                total[s] = value
             return carry
 
         lax.fori_loop(0, half, body, 0)
-
-    def ready(zz, a, b):
-        load_own(zz, a, b).wait()
-        twin(zz, a, b).wait_recv()
-
-    def send_second(zz, a):
-        ready(zz, a, 1)
-        add_up(chip_at(zz, a, 1), [])
+        if turn + RING < len(turns):
+            load_own(turn + RING).start()
+
+    def send_second(turn):
+        zz, a, _ = turns[turn]
+        add_up(turn, [])
         to_second(zz, a).start()
 
-    def send_first(zz):
-        ready(zz, 1, 0)
+    def send_first(turn):
+        zz = turns[turn][0]
         to_second(zz, 1).wait_recv()
-        add_up(chip_at(zz, 1, 0), [(r_second, 2 * zz + 1)])
+        add_up(turn, [(r_second, 2 * zz + 1)])
         to_first(zz).start()
 
-    def send_line(r):
-        zz = (z + r) % 4
-        ready(zz, 0, 0)
+    def send_line(turn, r):
+        zz = turns[turn][0]
         to_second(zz, 0).wait_recv()
         to_first(zz).wait_recv()
-        add_up(chip_at(zz, 0, 0), [(r_second, 2 * zz), (r_first, zz)])
+        add_up(turn, [(r_second, 2 * zz), (r_first, zz)])
         to_line(r).start()
 
-    order = [2, 1, 3, 0]
-    where = [(z + r) % 4 for r in order]
+    for turn in range(RING):
+        load_own(turn).start()
     for zz in where:
         for a in (1, 0):
-            load_own(zz, a, 1).start()
             twin(zz, 1, a).start()
     for zz in where:
         for a in (1, 0):
-            load_own(zz, a, 0).start()
             twin(zz, 0, a).start()
-
-    def send_both(index):
-        for a in (1, 0):
-            send_second(where[index], a)
-
-    send_both(0)
-    send_both(1)
-    send_both(2)
-    send_first(where[0])
-    send_both(3)
-    send_first(where[1])
-    send_line(order[0])
-    send_first(where[2])
-    send_line(order[1])
-    send_first(where[3])
-    send_line(order[2])
-
-    ready(z, 0, 0)
+    fetches = [
+        pltpu.make_async_copy(w_three, weights, save.at[0]),
+        pltpu.make_async_copy(grad_three, inner, save.at[1]),
+    ]
+    for fetch in fetches:
+        fetch.start()
+    for turn in range(6):
+        send_second(turn)
+    send_first(6)
+    send_second(7)
+    send_second(8)
+    for fetch in fetches:
+        fetch.wait()
+
+    rows = features // PANELS
+
+    def panel(index, carry):
+        mine = pl.ds(pl.multiple_of(index * rows, 16), rows)
+        acc[mine, :] = sum(nn(weights[k, mine, :], inner[k]) for k in range(3))
+        return carry
+
+    lax.fori_loop(0, PANELS, panel, 0)
+
+    swap = remote(acc.at[:, pl.ds(0, PREFIX)], prefix, R_PREFIX, me, 1 - core)
+    swap.start()
+    own_tokens = weights.at[0, :, pl.ds(0, length - PREFIX)]
+    take = pltpu.make_async_copy(tokens, own_tokens, save.at[0])
+    take.start()
+
+    def at(index):
+        return pl.ds(pl.multiple_of(index * GB, GB), GB)
+
+    def ahead(index):
+        return pl.ds(pl.multiple_of(PREFIX + index * GB, PREFIX), GB)
+
+    def give(index, slot):
+        return pltpu.make_async_copy(grad_middle.at[:, at(index)], given.at[slot], save.at[2 + slot])
+
+    def store(index):
+        return pltpu.make_async_copy(acc.at[:, ahead(index)], grad_input.at[:, at(index)], save.at[4 + index])
+
+    give(0, 0).start()
+    send_line(9, order[0])
+    send_first(10)
+    take.wait()
+    swap.wait()
+    here = (1 - core).astype(F32)
+    acc[:, PREFIX : 2 * PREFIX] += (acc[:, :PREFIX] + prefix[...]) * here
+    folds[...] = jnp.zeros_like(folds)
+    groups = (length - PREFIX) // GB
+    for index in range(groups):
+        if index + 1 < groups:
+            give(index + 1, (index + 1) % 2).start()
+        give(index, index % 2).wait()
+        unit, scale = norm_parts(weights[0, :, GB * index : GB * (index + 1)].astype(F32))
+        mine = slice(PREFIX + GB * index, PREFIX + GB * (index + 1))
+        grad = acc[:, mine]
+        folds[0] += fold(grad * unit)
+        folds[1] += fold(grad)
+        acc[:, mine] = given[index % 2] + norm_back(unit, scale, params[:, 0:1], grad)
+        store(index).start()
+
+    flow[0] = sums[...] + row_sums(folds[0], 0) + row_sums(folds[1], 1)
+    pairs = [(me, 1 - core), (me + first, core), (me, 1 - core), (me + first, core), (me, 1 - core)] + line
+    sources = [flow.at[0], flow.at[1], flow.at[2], arrived.at[2], flow.at[3]] + [flow.at[4]] * 3
+
+    def pass_on(k):
+        return remote(sources[k], arrived.at[k], R_FLOW + k, *pairs[k])
+
+    for k in range(2):
+        pass_on(k).start()
+        pass_on(k).wait_recv()
+        flow[k + 1] = flow[k] + arrived[k]
+    pass_on(2).start()
+    pass_on(2).wait_recv()
+    pass_on(3).start()
+    send_first(11)
+    pass_on(3).wait_recv()
+    flow[3] = arrived[2] + arrived[3]
+    pass_on(4).start()
+    pass_on(4).wait_recv()
+    plane = jnp.where(core == 0, flow[3], arrived[4])
+    flow[4] = plane
+    arrived[4] = plane
+    for k in range(5, 8):
+        pass_on(k).start()
+    send_line(12, order[1])
+    send_first(13)
+    send_line(14, order[2])
+    for k in range(5, 8):
+        pass_on(k).wait_recv()
+    norm_sums[...] = sum(arrived[4 + (z - zz + 4) % 4] for zz in range(4))
     to_second(z, 0).wait_recv()
     to_first(z).wait_recv()
     for r in range(1, 4):
         to_line(r).wait_recv()
-
-    def body(s, carry):
-        value = own[me, s].astype(F32) + r_twin[me, s].astype(F32)
-        value = value + r_second[2 * z, s].astype(F32)
-        value = value + r_first[z, s].astype(F32)
-        for r in range(3):
-            value = value + r_line[r, s].astype(F32)
-        total[s] = value
-        return carry
-
-    lax.fori_loop(0, half, body, 0)
+    add_up(15, [(r_second, 2 * z), (r_first, z), (r_line, 0), (r_line, 1), (r_line, 2)])
     target = out.at[pl.ds(core * half, half)]
     done = remote(total, target, R_DONE, me, 1 - core)
     done.start()
@@ -424,34 +519,53 @@
         to_first(zz).wait_send()
     for r in range(1, 4):
         to_line(r).wait_send()
+    for k in range(len(pairs)):
+        pass_on(k).wait_send()
+    for index in range(groups):
+        store(index).wait()
     done.wait()
     saved.wait()
 
 
-def reduce_slots(grads, slots):
-    _, rows, lanes = grads.shape
+def reduce_slots(grads, slots, w_three, grad_three, tokens, grad_middle, params, sums):
+    _, lines, lanes = grads.shape
     half = slots // 2
-    pieces = lambda n: pltpu.VMEM((n, half, rows, lanes), BF16)
+    _, features, length = grad_three.shape
+    pieces = lambda n: pltpu.VMEM((n, half, lines, lanes), BF16)
+    anywhere, inside = pl.BlockSpec(memory_space=pl.ANY), pl.BlockSpec(memory_space=pltpu.VMEM)
+    groups = (length - PREFIX) // GB
     return pl.pallas_call(
         functools.partial(reduce_kernel, slots),
-        out_shape=jax.ShapeDtypeStruct((slots, rows, lanes), F32),
-        in_specs=[pl.BlockSpec(memory_space=pl.ANY)],
-        out_specs=pl.BlockSpec(memory_space=pl.ANY),
+        out_shape=[
+            jax.ShapeDtypeStruct((slots, lines, lanes), F32),
+            jax.ShapeDtypeStruct((features, length - PREFIX), F32),
+            jax.ShapeDtypeStruct((8, features), F32),
+        ],
+        in_specs=[anywhere] * 5 + [inside] * 2,
+        out_specs=[anywhere, anywhere, inside],
         scratch_shapes=[
-            pieces(16),
+            pieces(RING),
             pieces(16),
             pieces(8),
             pieces(4),
             pieces(3),
-            pltpu.VMEM((half, rows, lanes), F32),
-            pltpu.SemaphoreType.DMA((16,)),
+            pltpu.VMEM((half, lines, lanes), F32),
+            pltpu.VMEM(w_three.shape, BF16),
+            pltpu.VMEM(grad_three.shape, BF16),
+            pltpu.VMEM((features, length), F32),
+            pltpu.VMEM((features, PREFIX), F32),
+            pltpu.VMEM((2, features, GB), F32),
+            pltpu.VMEM((2, features, 128), F32),
+            pltpu.VMEM((5, 8, features), F32),
+            pltpu.VMEM((8, 8, features), F32),
+            pltpu.SemaphoreType.DMA((RING,)),
             pltpu.SemaphoreType.DMA((REDUCE_LABELS,)),
             pltpu.SemaphoreType.DMA((REDUCE_LABELS,)),
-            pltpu.SemaphoreType.DMA((1,)),
+            pltpu.SemaphoreType.DMA((4 + groups,)),
         ],
-        compiler_params=pltpu.CompilerParams(collective_id=1, has_side_effects=True, vmem_limit_bytes=60 << 20),
+        compiler_params=pltpu.CompilerParams(collective_id=1, has_side_effects=True, vmem_limit_bytes=63 << 20),
         name="reduce_slots",
-    )(grads)
+    )(grads, w_three, grad_three, tokens, grad_middle, params, sums)
 
 
 def lay(matrix, row, col, block):
@@ -484,10 +598,18 @@
     return sum(values[:, start : start + 128] for start in range(0, values.shape[1], 128))
 
 
+def row_sums(values, row):
+    ones = jnp.ones((8, values.shape[1]), F32)
+    summed = lax.dot_general(
+        ones, values, (((1,), (1,)), ((), ())), precision=lax.Precision.HIGHEST, preferred_element_type=F32
+    )
+    return jnp.where(lax.broadcasted_iota(jnp.int32, summed.shape, 0) == row, summed, 0.0)
+
+
 ONCE = pl.Buffered(1)
 
 
-def front_kernel(slot_of, gain, shift, tokens, *refs):
+def front_kernel(slot_of, params, tokens, *refs):
     del slot_of
     blocks, (weights, out, normed) = refs[:-3], refs[-3:]
     tiles = token_tiles(tokens.shape[1])
@@ -496,7 +618,7 @@
     def _():
         for tile in tiles:
             unit, _ = norm_parts(tokens[:, tile].astype(F32))
-            normed[:, tile] = (unit * gain[...] + shift[...]).astype(BF16)
+            normed[:, tile] = (unit * params[:, 0:1] + params[:, 1:2]).astype(BF16)
 
     row_blocks = math.isqrt(len(blocks))
     for index, block in enumerate(blocks):
@@ -504,7 +626,7 @@
     out[0] = tn(weights[0], normed[...]).astype(BF16)
 
 
-def front(gathered, slot_of, gain, shift, tokens, row_blocks):
+def front(gathered, slot_of, params, tokens, row_blocks):
     features, length = tokens.shape
     square = row_blocks * row_blocks
     whole = lambda shape: pl.BlockSpec(shape, lambda s, v: (0,) * len(shape), pipeline_mode=ONCE)
@@ -514,7 +636,7 @@
         grid_spec=pltpu.PrefetchScalarGridSpec(
             num_scalar_prefetch=1,
             grid=(3,),
-            in_specs=[whole((features, 1))] * 2 + [whole((features, length))] + blocks,
+            in_specs=[whole(params.shape), whole((features, length))] + blocks,
             out_specs=[
                 pl.BlockSpec((1, features, features), lambda s, v: (s, 0, 0)),
                 pl.BlockSpec((1, features, length), lambda s, v: (s, 0, 0)),
@@ -528,7 +650,7 @@
         ],
         compiler_params=pltpu.CompilerParams(vmem_limit_bytes=60 << 20),
         name="front",
-    )(slot_of, gain, shift, tokens, *([gathered] * square))
+    )(slot_of, params, tokens, *([gathered] * square))
 
 
 def gelu_pair(values):
@@ -539,13 +661,13 @@
     return half + half * bend, 0.5 + 0.5 * bend + half * (1.0 - bend * bend) * slope
 
 
-def middle_kernel(row_blocks, slot_of, gain, shift, tokens, attended, grad_low, *refs):
+def middle_kernel(row_blocks, slot_of, params, tokens, attended, grad_low, *refs):
     del slot_of
     square = row_blocks * row_blocks
     out_blocks, up_blocks, down_blocks = (refs[square * k : square * (k + 1)] for k in range(3))
     outs, scratch = refs[3 * square : 3 * square + 8], refs[3 * square + 8 :]
     block_out, activated, grad_pre, normed, grad_branch, grad_att, grad_middle, sums = outs
-    w_out, w_up, w_down, middle, total, stats, sem = scratch
+    w_out, w_up, w_down, middle, total, stats, folds, sem = scratch
     tiles, parts = grad_low.shape[1] // GB, feature_parts(normed.shape[0])
     at = lambda index: pl.ds(pl.multiple_of(index * GB, GB), GB)
     step, last = pl.program_id(0), pl.num_programs(0) - 1
@@ -575,11 +697,11 @@
             scale = lax.rsqrt(jnp.mean(centred * centred, axis=0, keepdims=True) + 1e-05)
             stats[0:1, tile] = average
             stats[1:2, tile] = scale
-            normed[:, tile] = (centred * scale * gain[...] + shift[...]).astype(BF16)
+            normed[:, tile] = (centred * scale * params[:, 2:3] + params[:, 3:4]).astype(BF16)
             return carry
 
         lax.fori_loop(0, tiles, enter, 0)
-        sums[...] = jnp.zeros_like(sums)
+        folds[...] = jnp.zeros_like(folds)
 
     for index in range(square):
         lay(w_up, index // row_blocks, index % row_blocks, up_blocks[index].at[0])
@@ -606,9 +728,9 @@
             scale = stats[1:2, tile]
             unit = (middle[:, tile] - stats[0:1, tile]) * scale
             grad = grad_middle[:, tile]
-            sums[0] += fold(grad * unit)
-            sums[1] += fold(grad)
-            values = grad_low[:, tile].astype(F32) + norm_back(unit, scale, gain[...], grad)
+            folds[0] += fold(grad * unit)
+            folds[1] += fold(grad)
+            values = grad_low[:, tile].astype(F32) + norm_back(unit, scale, params[:, 2:3], grad)
             grad_middle[:, tile] = values
             grad_branch[:, tile] = values.astype(BF16)
             for part in parts:
@@ -616,9 +738,10 @@
             return carry
 
         lax.fori_loop(0, tiles, leave, 0)
-
-
-def middle_part(gathered, slot_of, gain, shift, tokens, attended, grad_low, row_blocks, col_blocks):
+        sums[...] = row_sums(folds[0], 2) + row_sums(folds[1], 3)
+
+
+def middle_part(gathered, slot_of, params, tokens, attended, grad_low, row_blocks, col_blocks):
     features, length = tokens.shape
     square = row_blocks * row_blocks
     hidden = features * col_blocks // row_blocks
@@ -644,13 +767,17 @@
         grid_spec=pltpu.PrefetchScalarGridSpec(
             num_scalar_prefetch=1,
             grid=(col_blocks // row_blocks,),
-            in_specs=[whole(features, 1)] * 2 + [anywhere] * 2 + [whole(features, length)] + blocks,
+            in_specs=[whole(*params.shape)] + [anywhere] * 2 + [whole(features, length)] + blocks,
             out_specs=[whole(features, length), part, part]
             + [whole(features, length)] * 4
-            + [whole(2, features, 128)],
+            + [whole(8, features)],
             scratch_shapes=[square_scratch] * 3
             + [pltpu.VMEM((features, length), F32)] * 2
-            + [pltpu.VMEM((8, length), F32), pltpu.SemaphoreType.DMA((2,))],
+            + [
+                pltpu.VMEM((8, length), F32),
+                pltpu.VMEM((2, features, 128), F32),
+                pltpu.SemaphoreType.DMA((2,)),
+            ],
         ),
         out_shape=[
             shape((features, length), BF16),
@@ -660,11 +787,11 @@
             shape((features, length), BF16),
             shape((features, length), BF16),
             shape((features, length), F32),
-            shape((2, features, 128), F32),
+            shape((8, features), F32),
         ],
         compiler_params=pltpu.CompilerParams(vmem_limit_bytes=63 << 20),
         name="middle_part",
-    )(slot_of, gain, shift, tokens, attended, grad_low, *([gathered] * (3 * square)))
+    )(slot_of, params, tokens, attended, grad_low, *([gathered] * (3 * square)))
 
 
 def weight_grad_kernel(block_of, deep, size, slot_of, left, right, *refs):
@@ -981,13 +1108,6 @@
     return scale * (inner - mean_one - unit * mean_two)
 
 
-def butterfly(values, shape):
-    for bit in (1, 2, 4, 8, 16):
-        pairs = [(i, i ^ bit) for i in range(32)]
-        values = values + lax.ppermute(values, ("dp", "seq"), pairs)
-    return values
-
-
 def local(
     chips,
     cores,
@@ -1043,10 +1163,10 @@
         prefix_tokens = jnp.where(seq_index == 0, prefix_tokens, arrived)
     else:
         prefix_tokens = lax.all_gather(prefix_tokens, "seq")[0]
-    gain_one, shift_one = norm_gains[0][:, None], norm_shifts[0][:, None]
-    gain_two, shift_two = norm_gains[1][:, None], norm_shifts[1][:, None]
+    norms = jnp.stack([norm_gains[0], norm_shifts[0], norm_gains[1], norm_shifts[1]])
+    params = norms.T
     all_tokens = jnp.concatenate([prefix_tokens, own_tokens], axis=1)
-    w_three, qkv, normed_in = front(gathered, slot_of, gain_one, shift_one, all_tokens, row_blocks)
+    w_three, qkv, normed_in = front(gathered, slot_of, params, all_tokens, row_blocks)
 
     position = seq_index * length + jnp.arange(length, dtype=jnp.int32)
     alive = jnp.where(position < PREFIX, position < prefix_len[0], pad_mask[0] == 1)
@@ -1058,44 +1178,31 @@
     grad_low = cotangent.reshape(length, features).T
     attended, log_total = attention(qkv, extras)
     block_out, activated, grad_pre, normed_mid, grad_branch, grad_att, grad_middle, sums = middle_part(
-        gathered, slot_of, gain_two, shift_two, own_tokens, attended, grad_low, row_blocks, col_blocks
+        gathered, slot_of, params, own_tokens, attended, grad_low, row_blocks, col_blocks
     )
     grads = weight_grad(activated, grad_low, slot_of, None, slot_count, size, down_of, "grad_down")
     grads = weight_grad(normed_mid, grad_pre, slot_of, grads, slot_count, size, up_of, "grad_up")
     grads = weight_grad(attended, grad_branch, slot_of, grads, slot_count, size, out_of, "grad_out")
     grad_three = attention_back(qkv, extras, attended, log_total, grad_att)
-    grad_three = grad_three.reshape(3 * features, PREFIX + length)
-    grads = weight_grad(normed_in, grad_three, slot_of, grads, slot_count, size, three_of, "grad_three")
-    grad_all = sum(nn(w_three[k], grad_three[features * k : features * (k + 1)]) for k in range(3))
-    prefix_part = grad_all[:, :PREFIX]
-    if cores == 2:
-        prefix_part = prefix_part + lax.ppermute(prefix_part, "seq", [(1, 0)])
-    else:
-        prefix_part = lax.psum(prefix_part, "seq")
-    prefix_part = jnp.where(seq_index == 0, prefix_part, 0.0)
-    grad_normed = grad_all[:, PREFIX:] + jnp.pad(prefix_part, ((0, 0), (0, length - PREFIX)))
-    unit_one, scale_one = norm_parts(own_tokens.astype(F32))
-    grad_input = grad_middle + norm_back(unit_one, scale_one, gain_one, grad_normed)
-
+    flat_three = grad_three.reshape(3 * features, PREFIX + length)
+    grads = weight_grad(normed_in, flat_three, slot_of, grads, slot_count, size, three_of, "grad_three")
     grad_scale = 1.0 / math.sqrt(length * chips * cores)
-    norm_terms = jnp.stack(
-        [
-            jnp.sum(grad_normed * unit_one, axis=1),
-            jnp.sum(grad_normed, axis=1),
-            jnp.sum(sums[0], axis=1),
-            jnp.sum(sums[1], axis=1),
-        ]
-    )
-    norm_terms = norm_terms * grad_scale
-    norm_grad = butterfly(norm_terms, None) if known else lax.psum(norm_terms, ("dp", "seq"))
-    params = jnp.stack([norm_gains[0], norm_shifts[0], norm_gains[1], norm_shifts[1]])
-    new_norms = params - 0.1 * norm_grad * lax.rsqrt(jnp.mean(norm_grad * norm_grad) + 1e-06)
-
     if known:
-        summed = reduce_slots(grads, slots)
+        summed, grad_input, norm_sums = reduce_slots(
+            grads, slots, w_three, grad_three, own_tokens, grad_middle, params, sums
+        )
     else:
         part = lax.psum_scatter(grads.astype(F32), "dp", scatter_dimension=0, tiled=True)
         summed = lax.psum(part, "seq")
+        grad_all = sum(nn(w_three[k], grad_three[k]) for k in range(3))
+        prefix_part = jnp.where(seq_index == 0, lax.psum(grad_all[:, :PREFIX], "seq"), 0.0)
+        grad_normed = grad_all[:, PREFIX:] + jnp.pad(prefix_part, ((0, 0), (0, length - PREFIX)))
+        unit_one, scale_one = norm_parts(own_tokens.astype(F32))
+        grad_input = grad_middle + norm_back(unit_one, scale_one, params[:, 0:1], grad_normed)
+        first_sums = [jnp.sum(grad_normed * unit_one, axis=1), jnp.sum(grad_normed, axis=1)]
+        norm_sums = lax.psum(jnp.stack(first_sums + [sums[2], sums[3]]), ("dp", "seq"))
+    norm_grad = norm_sums[:4] * grad_scale
+    new_norms = norms - 0.1 * norm_grad * lax.rsqrt(jnp.mean(norm_grad * norm_grad) + 1e-06)
     stepped = optimizer(
         summed, grad_scale, (master, average_weights, stat_left, stat_right, root_left, root_right)
     )

time: 613 us -> 572 us (0.933)
  matrix products: 17.9 us -> 0 us
  other arithmetic: 21.4 us -> 7.35 us
    dot_general x3 -> x0, matrix products: 17.9 us -> none  [nn(): lax.dot_general(left, right, (((1,), (0,)), ((), ())), preferred_element_...]
    reduce_sum x4 -> x0, other arithmetic: 9.75 us -> none  [the longest x1 3.81 us: local(): jnp.sum(grad_normed * unit_one, axis=1)]
  transfers between devices with their start and end apart: 7 -> 1, of which waited for: 1 -> 0; matrix products, arithmetic and copies ran while one was open for 3% -> 1% of each run, Pallas kernels for 61% -> 25%
where the time goes in v3:
time: 572 us; the launch traced here: 563 us
  Pallas kernels  540 us (94%)
  local copies, waits for them, and re-layouts  10 us (2%)
  other arithmetic  7.35 us (1%)
    pallas_call x1, Pallas kernels, reduce_slots(): pl.pallas_call(functools.partial(reduce_kernel, slots), out_shape=[jax.Sh...  140 us
    pallas_call x1, Pallas kernels, gather_slots(): pl.pallas_call(functools.partial(gather_kernel, slots), out_shape=jax.Sha...  133 us
    pallas_call x1, Pallas kernels, middle_part(): pl.pallas_call(functools.partial(middle_kernel, row_blocks), grid_spec=pl...  99.6 us
    pallas_call x4, Pallas kernels, weight_grad(): pl.pallas_call(functools.partial(weight_grad_kernel, block_of, deep, size...  61.8 us
    pallas_call x1, Pallas kernels, optimizer(): pl.pallas_call(functools.partial(optimizer_kernel, scale), grid=(slots,),...  28.6 us
    pallas_call x1, Pallas kernels, attention_back(): pl.pallas_call(functools.partial(attention_back_kernel, head ** (-0.5)),...  25.7 us
    pallas_call x1, Pallas kernels, front(): pl.pallas_call(front_kernel, grid_spec=pltpu.PrefetchScalarGridSpec(num_s...  24.3 us
    pallas_call x1, Pallas kernels, attention(): pl.pallas_call(functools.partial(attention_kernel, head ** (-0.5)), grid=...  19.2 us
  transfers between devices with their start and end apart: 1, of which 0 were waited for; matrix products, arithmetic and copies ran while one was open for 1% of the time, Pallas kernels for 25%

profile of v3, /device:TPU:0, one launch (start us, length us, event | category | flops | bytes accessed | tf_op | source)
XLA Modules:
  0.0 562.7 jit_solution(2602892402871075756)
XLA Ops:
  0.6 1.0 slice.24
  1.6 2.4 collective-permute-start
  4.7 0.1 broadcast_bitcast_fusion
  4.8 0.1 pad.10.clone
  4.9 0.7 compare_select_fusion
  5.6 0.8 fusion.5
  6.4 0.0 copy-start.1
  6.4 0.0 copy-start.3
  6.4 0.0 copy-start.5
  6.4 0.0 copy-start.7
  6.5 0.1 maximum_bitcast_fusion
  6.6 0.7 compare_select_fusion.1
  7.3 1.1 copy.37
  8.3 0.0 copy-done.1
  8.3 0.0 copy-done.3
  8.3 0.0 copy-done.5
  8.3 0.0 copy-done.7
  8.3 8.0 %pack_slots.1.placed = bf16[192,312,256]{2,1,0:T(8,128)(2,1)} custom-call(s32[1]{0:T(128)} %bitcast.4.chip, bf16[12,280,280]{2,1,0:T(8,128)(2,1)} %block.1), custom_call_target="tpu_custom_call" | custom-call | tf_op jit(solution)/shard_map/pack_slots/pallas_call | solution.py:84
  16.3 0.0 copy-start.9
  16.3 0.0 copy-start
  16.3 132.8 %gather_slots.1.refs_0_.refs_1_.refs_2_.refs_3_.refs_4_.refs_5_.refs_6_.refs_7_.refs_8_.refs_9_.refs_10_.refs_11_.refs_12_.refs_13_.refs_14_.refs_15_.refs_16_.refs_17_.refs_18_.refs_19_.refs_20_.refs_21_.refs_22_.refs_23_.refs_24_.refs_25_.refs_26_.refs_27_.refs_28_.refs_29_.refs_30_.refs_31_.refs_32_.refs_33_.refs_34_.refs_35_.refs_36_.refs_37_.refs_38_.refs_39_.refs_40_.refs_41_.refs_42_.refs_43_.refs_44_.refs_45_.refs_46_.refs_47_ = bf16[192,312,256]{2,1,0:T(8,128)(2,1)} custom-call(bf16[192,312,256]{2,1,0:T(8,128)(2,1)} %pack_slots.1.placed), custom_call_target="tpu_custom_call", output_to_operand_aliasing={{}: (0, {})} | custom-call | tf_op jit(solution)/shard_map/gather_slots/pallas_call | solution.py:270
  149.1 1.7 scatter_custom_fusion.slot_of
  150.9 0.1 stack.41
  150.9 0.0 copy-done.9
  150.9 0.6 pad_maximum_fusion.1.extras
  151.6 0.0 collective-permute-done
  151.6 0.0 copy-done
  151.6 0.1 broadcast_select_fusion
  151.7 1.7 pad_maximum_fusion.tokens
  153.4 24.3 %front.1 = (bf16[3,1120,1120]{2,1,0:T(8,128)(2,1)}, bf16[3,1120,1152]{2,1,0:T(8,128)(2,1)}, bf16[1120,1152]{1,0:T(8,128)(2,1)}) custom-call(s32[192]{0:T(256)} %scatter_custom_fusion.slot_of, f32[1120,4]{1,0:T(8,128)} %bitcast.33, bf16[1120,1152]{1,0:T(8,128)(2,1)} %pad_maximum_fusion.tokens, ...), custom_call_target="tpu_custom_call" | custom-call | tf_op jit(solution)/shard_map/front/pallas_call | solution.py:634
  177.7 19.2 %attention.1 = (bf16[1120,1024]{1,0:T(8,128)(2,1)}, f32[20,1,1024]{2,1,0:T(1,128)}) custom-call(bf16[3,1120,1152]{2,1,0:T(8,128)(2,1)} %get-tuple-element.32.qkv, bf16[3,8,1152]{2,1,0:T(8,128)(2,1)} %pad_maximum_fusion.1.extras), custom_call_target="tpu_custom_call" | custom-call | flops 2348810240 | bytes 7741440 | tf_op jit(solution)/shard_map/attention/pallas_call | solution.py:1015
  196.9 99.6 %middle_part.1 = (bf16[1120,1024]{1,0:T(8,128)(2,1)}, bf16[4480,1024]{1,0:T(8,128)(2,1)}, bf16[4480,1024]{1,0:T(8,128)(2,1)}, bf16[1120,1024]{1,0:T(8,128)(2,1)}...) custom-call(s32[192]{0:T(256)} %scatter_custom_fusion.slot_of, ...), custom_call_target="tpu_custom_call" | custom-call | tf_op jit(solution)/shard_map/middle_part/pallas_call | solution.py:765
  296.4 18.6 %grad_down.1.refs_0_ = bf16[192,312,256]{2,1,0:T(8,128)(2,1)} custom-call(s32[192]{0:T(256)} %scatter_custom_fusion.slot_of, bf16[4480,1024]{1,0:T(8,128)(2,1)} %get-tuple-element.41.left, bf16[1120,1024]{1,0:T(8,128)(2,1)} %bitcast.37), custom_call_target="tpu_custom_call" | custom-call | flops 10276044800 | bytes 21504000 | tf_op jit(solution)/shard_map/grad_down/pallas_call | solution.py:840
  315.1 25.7 %attention_back.1.grad_three = bf16[3,1120,1152]{2,1,0:T(8,128)(2,1)} custom-call(bf16[3,1120,1152]{2,1,0:T(8,128)(2,1)} %get-tuple-element.32.qkv, bf16[3,8,1152]{2,1,0:T(8,128)(2,1)} %pad_maximum_fusion.1.extras, bf16[1120,1024]{1,0:T(8,128)(2,1)} %get-tuple-element.33.attended.out.left, f32[20,1,1024]{2,1,0:T(1,128)} %get-tuple-element.36.lse, ...), custom_call_target="tpu_custom_call" | custom-call | flops 5872025600 | bytes 15482880 | tf_op jit(solution)/shard_map/attention_back/pallas_call | solution.py:1032
  340.7 18.4 %grad_up.1.refs_0_ = bf16[192,312,256]{2,1,0:T(8,128)(2,1)} custom-call(s32[192]{0:T(256)} %scatter_custom_fusion.slot_of, bf16[1120,1024]{1,0:T(8,128)(2,1)} %get-tuple-element.39.left, bf16[4480,1024]{1,0:T(8,128)(2,1)} %get-tuple-element.40.right, bf16[192,312,256]{2,1,0:T(8,128)(2,1)} %grad_down.1.refs_0_), custom_call_target="tpu_custom_call", output_to_operand_aliasing={{}: (3, {})} | custom-call | flops 10276044800 | bytes 21504000 | tf_op jit(solution)/shard_map/grad_up/pallas_call | solution.py:840
  359.1 7.5 %grad_out.1.refs_0_ = bf16[192,312,256]{2,1,0:T(8,128)(2,1)} custom-call(s32[192]{0:T(256)} %scatter_custom_fusion.slot_of, bf16[1120,1024]{1,0:T(8,128)(2,1)} %get-tuple-element.33.attended.out.left, bf16[1120,1024]{1,0:T(8,128)(2,1)} %get-tuple-element.38.right, bf16[192,312,256]{2,1,0:T(8,128)(2,1)} %grad_up.1.refs_0_), custom_call_target="tpu_custom_call", output_to_operand_aliasing={{}: (3, {})} | custom-call | flops 2569011200 | bytes 7096320 | tf_op jit(solution)/shard_map/grad_out/pallas_call | solution.py:840
  366.7 17.3 %grad_three.1.grads = bf16[192,312,256]{2,1,0:T(8,128)(2,1)} custom-call(s32[192]{0:T(256)} %scatter_custom_fusion.slot_of, bf16[1120,1152]{1,0:T(8,128)(2,1)} %get-tuple-element.35.left, bf16[3360,1152]{1,0:T(8,128)(2,1)} %bitcast.27, bf16[192,312,256]{2,1,0:T(8,128)(2,1)} %grad_out.1.refs_0_), custom_call_target="tpu_custom_call", output_to_operand_aliasing={{}: (3, {})} | custom-call | flops 8670412800 | bytes 17848320 | tf_op jit(solution)/shard_map/grad_three/pallas_call | solution.py:840
  383.9 0.0 copy-start.2
  383.9 0.0 copy-start.4
  384.0 0.0 copy-start.6
  384.0 0.0 copy-start.8
  384.0 140.4 %reduce_slots.1 = (f32[12,312,256]{2,1,0:T(8,128)}, f32[1120,1024]{1,0:T(8,128)}, f32[8,1120]{1,0:T(8,128)}) custom-call(bf16[192,312,256]{2,1,0:T(8,128)(2,1)} %grad_three.1.grads, bf16[3,1120,1120]{2,1,0:T(8,128)(2,1)} %get-tuple-element.42.w_three, bf16[3,1120,1152]{2,1,0:T(8,128)(2,1)} %attention_back.1.grad_three, bf16[1120,1024]{1,0:T(8,128)(2,1)} %bitcast.30, ...), custom_call_target="tpu_custom_call" | custom-call | tf_op jit(solution)/shard_map/reduce_slots/pallas_call | solution.py:537
  524.4 2.0 multiply_reduce_fusion
  527.1 0.0 copy-done.2
  527.1 0.0 copy-done.4
  527.1 0.0 copy-done.6
  527.1 0.0 copy-done.8
  527.1 1.4 multiply_subtract_fusion
  528.5 28.6 %optimizer.1 = (f32[12,280,280]{2,1,0:T(8,128)}, f32[12,280,280]{2,1,0:T(8,128)}, f32[12,280,280]{2,1,0:T(8,128)}, f32[12,280,280]{2,1,0:T(8,128)}, bf16[12,280,...) custom-call(f32[12,312,256]{2,1,0:T(8,128)} %get-tuple-element.47.packed, f32[12,280,280]{2,1,0:T(8,128)} %master.1, ...), custom_call_target="tpu_custom_call" | custom-call | tf_op jit(solution)/shard_map/optimizer/pallas_call | solution.py:1086
  557.1 5.1 copy.45
  (14 shorter events, 0.1 us)
Async XLA Ops:
  1.6 149.9 %collective-permute-start = (bf16[1120,128]{1,0:T(8,128)(2,1)S(1)}, bf16[1120,128]{1,0:T(8,128)(2,1)S(1)}, u32[]{:S(2)}, u32[]{:S(2)}) collective-permute-start(bf16[1120,128]{1,0:T(8,128)(2,1)S(1)} %slice.24), channel_id=1, source_target_pairs={{0,1},{2,3},{4,5},{6,7},{8,9},{10,11},{12,13},{14,15},{16,17},{18,... | collective-permute-start | bytes 860168 | tf_op jit(solution)/shard_map/ppermute | solution.py:1162
  6.4 1.9 copy-start.1
  6.4 1.9 copy-start.3
  6.4 1.9 copy-start.5
  6.4 1.9 copy-start.7
  16.3 134.6 %copy-start.9 = (bf16[1,8,1152]{2,1,0:T(8,128)(2,1)S(1)}, bf16[1,8,1152]{2,1,0:T(8,128)(2,1)}, u32[]{:S(2)}) copy-start(bf16[1,8,1152]{2,1,0:T(8,128)(2,1)} %constant.12.clone.1) | copy-start | bytes 55300
  16.3 135.3 %copy-start = (bf16[1,1024,1120]{1,2,0:T(8,128)(2,1)S(1)}, bf16[1,1024,1120]{1,2,0:T(8,128)(2,1)}, u32[]{:S(2)}) copy-start(bf16[1,1024,1120]{1,2,0:T(8,128)(2,1)} %param.14) | copy-start | bytes 6881284
  383.9 143.1 %copy-start.2 = (f32[1,1120]{1,0:T(1,128)S(1)}, f32[1,1120]{1,0:T(1,128)}, u32[]{:S(2)}) copy-start(f32[1,1120]{1,0:T(1,128)} %copy-done.1) | copy-start | bytes 13444
  383.9 143.1 %copy-start.4 = (f32[1,1120]{1,0:T(1,128)S(1)}, f32[1,1120]{1,0:T(1,128)}, u32[]{:S(2)}) copy-start(f32[1,1120]{1,0:T(1,128)} %copy-done.3) | copy-start | bytes 13444
  384.0 143.1 %copy-start.6 = (f32[1,1120]{1,0:T(1,128)S(1)}, f32[1,1120]{1,0:T(1,128)}, u32[]{:S(2)}) copy-start(f32[1,1120]{1,0:T(1,128)} %copy-done.5) | copy-start | bytes 13444
  384.0 143.1 %copy-start.8 = (f32[1,1120]{1,0:T(1,128)S(1)}, f32[1,1120]{1,0:T(1,128)}, u32[]{:S(2)}) copy-start(f32[1,1120]{1,0:T(1,128)} %copy-done.7) | copy-start | bytes 13444

commit v4 on v3

--- a/solution.py
+++ b/solution.py
@@ -71,27 +71,29 @@
     return pl.CostEstimate(flops=int(flops), bytes_accessed=int(moved), transcendentals=int(exps))
 
 
-def pack_kernel(chip, block, packed):
-    del chip
+def pack_kernel(start, block, packed):
+    del start
     size = block.shape[1]
-    values = block[0].astype(F32)
-    packed[0, :size] = values[:, :MAIN].astype(BF16)
-    packed[0, size:] = pack_tail(values).astype(BF16)
-
-
-def pack_slots(blocks, chip, slot_count):
-    count, size, _ = blocks.shape
+    rest = size - MAIN
+    packed[0, :size] = block[0, :, :MAIN]
+    packed[0, size:] = jnp.zeros((RUN, MAIN), BF16)
+    for row, count, lane in runs(size):
+        packed[0, size : size + count, lane : lane + rest] = block[0, row : row + count, MAIN:]
+
+
+def pack_slots(blocks, start, count, slot_count):
+    size = blocks.shape[1]
     return pl.pallas_call(
         pack_kernel,
         grid_spec=pltpu.PrefetchScalarGridSpec(
             num_scalar_prefetch=1,
             grid=(count,),
-            in_specs=[pl.BlockSpec((1, size, size), lambda i, chip: (i, 0, 0))],
-            out_specs=pl.BlockSpec((1, size + RUN, MAIN), lambda i, chip: (chip[0] * count + i, 0, 0)),
+            in_specs=[pl.BlockSpec((1, size, size), lambda i, start: (start[0] + i, 0, 0))],
+            out_specs=pl.BlockSpec((1, size + RUN, MAIN), lambda i, start: (start[1] + i, 0, 0)),
         ),
         out_shape=jax.ShapeDtypeStruct((slot_count, size + RUN, MAIN), BF16),
         name="pack_slots",
-    )(chip, blocks)
+    )(start, blocks)
 
 
 def place():
@@ -110,10 +112,10 @@
     pl.semaphore_wait(barrier, len(partners))
 
 
-UP, DOWN, FIRST, SECOND, TWIN, GATHER_LABELS = 0, 4, 8, 12, 20, 36
-
-
-def gather_kernel(slots, placed, out, send, recv):
+UP, DOWN, FIRST, SECOND, TWIN, HEAD, GATHER_LABELS = 0, 4, 8, 12, 20, 36, 37
+
+
+def gather_kernel(slots, placed, tokens, params, out, normed, held, send, recv, take):
     del placed
     me, core, z, first, second = place()
     half = slots // 2
@@ -149,11 +151,10 @@
     def to_twin(chip):
         return copy(TWIN + chip, chip, me, 1 - core)
 
-    def spread(zz, own=False):
+    def spread(zz):
         to_first(zz).start()
         to_second(zz, 0).start()
-        if not own:
-            to_twin(col(zz)).start()
+        to_twin(col(zz)).start()
 
     def after_first(zz):
         to_first(zz).wait_recv()
@@ -173,7 +174,40 @@
     def _():
         down(1).start()
 
-    spread(z, own=True)
+    spread(z)
+
+    prefix, seat = tokens.at[:, pl.ds(0, PREFIX)], held.at[:, pl.ds(0, PREFIX)]
+    mine = pltpu.make_async_copy(tokens, held.at[:, pl.ds(PREFIX, tokens.shape[1])], take.at[0])
+    near = pltpu.make_async_copy(prefix, seat, take.at[1])
+    far = pltpu.make_async_remote_copy(
+        src_ref=prefix,
+        dst_ref=seat,
+        send_sem=send.at[HEAD],
+        recv_sem=recv.at[HEAD],
+        device_id=(me, 1 - core),
+        device_id_type=MESH,
+    )
+    mine.start()
+
+    @pl.when(core == 0)
+    def _():
+        far.start()
+        near.start()
+        near.wait()
+
+    @pl.when(core == 1)
+    def _():
+        far.wait_recv()
+
+    mine.wait()
+
+    def normalize(index, carry):
+        tile = pl.ds(pl.multiple_of(index * PREFIX, PREFIX), PREFIX)
+        unit, _ = norm_parts(held[:, tile].astype(F32))
+        normed[:, tile] = (unit * params[:, 0:1] + params[:, 1:2]).astype(BF16)
+        return carry
+
+    lax.fori_loop(0, held.shape[1] // PREFIX, normalize, 0)
     for j in range(1, 4):
 
         @pl.when(z >= j)
@@ -233,16 +267,8 @@
         for a in range(2):
             for b in range(2):
                 chip = col(zz) + a * first + b * second
-                if a == 0 and b == 0:
-
-                    @pl.when(zz != z)
-                    def _():
-                        to_twin(chip).wait_recv()
-                        to_twin(chip).wait_send()
-
-                else:
-                    to_twin(chip).wait_recv()
-                    to_twin(chip).wait_send()
+                to_twin(chip).wait_recv()
+                to_twin(chip).wait_send()
         to_first(zz).wait_send()
         for a in range(2):
             to_second(zz, a).wait_send()
@@ -265,18 +291,29 @@
             def _():
                 down(j + 1).wait_send()
 
-
-def gather_slots(placed, slots):
+    @pl.when(core == 0)
+    def _():
+        far.wait_send()
+
+
+def gather_slots(placed, tokens, params, slots):
+    anywhere, inside = pl.BlockSpec(memory_space=pl.ANY), pl.BlockSpec(memory_space=pltpu.VMEM)
+    wide = (tokens.shape[0], PREFIX + tokens.shape[1])
     return pl.pallas_call(
         functools.partial(gather_kernel, slots),
-        out_shape=jax.ShapeDtypeStruct(placed.shape, placed.dtype),
-        in_specs=[pl.BlockSpec(memory_space=pl.ANY)],
-        out_specs=pl.BlockSpec(memory_space=pl.ANY),
-        scratch_shapes=[pltpu.SemaphoreType.DMA((GATHER_LABELS,)), pltpu.SemaphoreType.DMA((GATHER_LABELS,))],
+        out_shape=[jax.ShapeDtypeStruct(placed.shape, placed.dtype), jax.ShapeDtypeStruct(wide, BF16)],
+        in_specs=[anywhere, anywhere, inside],
+        out_specs=[anywhere, inside],
+        scratch_shapes=[
+            pltpu.VMEM(wide, BF16),
+            pltpu.SemaphoreType.DMA((GATHER_LABELS,)),
+            pltpu.SemaphoreType.DMA((GATHER_LABELS,)),
+            pltpu.SemaphoreType.DMA((2,)),
+        ],
         input_output_aliases={0: 0},
         compiler_params=pltpu.CompilerParams(collective_id=0, has_side_effects=True),
         name="gather_slots",
-    )(placed)
+    )(placed, tokens, params)
 
 
 R_TWIN, R_SECOND, R_FIRST, R_LINE, R_DONE, R_PREFIX, R_FLOW, REDUCE_LABELS = 0, 16, 24, 28, 32, 33, 34, 42
@@ -459,18 +496,22 @@
     acc[:, PREFIX : 2 * PREFIX] += (acc[:, :PREFIX] + prefix[...]) * here
     folds[...] = jnp.zeros_like(folds)
     groups = (length - PREFIX) // GB
-    for index in range(groups):
-        if index + 1 < groups:
+
+    def back(index, carry):
+        @pl.when(index + 1 < groups)
+        def _():
             give(index + 1, (index + 1) % 2).start()
+
         give(index, index % 2).wait()
-        unit, scale = norm_parts(weights[0, :, GB * index : GB * (index + 1)].astype(F32))
-        mine = slice(PREFIX + GB * index, PREFIX + GB * (index + 1))
-        grad = acc[:, mine]
+        unit, scale = norm_parts(weights[0, :, at(index)].astype(F32))
+        grad = acc[:, ahead(index)]
         folds[0] += fold(grad * unit)
         folds[1] += fold(grad)
-        acc[:, mine] = given[index % 2] + norm_back(unit, scale, params[:, 0:1], grad)
+        acc[:, ahead(index)] = given[index % 2] + norm_back(unit, scale, params[:, 0:1], grad)
         store(index).start()
-
+        return carry
+
+    lax.fori_loop(0, groups, back, 0)
     flow[0] = sums[...] + row_sums(folds[0], 0) + row_sums(folds[1], 1)
     pairs = [(me, 1 - core), (me + first, core), (me, 1 - core), (me + first, core), (me, 1 - core)] + line
     sources = [flow.at[0], flow.at[1], flow.at[2], arrived.at[2], flow.at[3]] + [flow.at[4]] * 3
@@ -584,11 +625,6 @@
     ]
 
 
-def token_tiles(length):
-    tile = GB if length % GB == 0 else HALF
-    return [slice(start, start + tile) for start in range(0, length, tile)]
-
-
 def feature_parts(features):
     part = -(-features // 256) * 128
     return [slice(start, min(start + part, features)) for start in range(0, features, part)]
@@ -609,48 +645,37 @@
 ONCE = pl.Buffered(1)
 
 
-def front_kernel(slot_of, params, tokens, *refs):
+def front_kernel(slot_of, normed, *refs):
     del slot_of
-    blocks, (weights, out, normed) = refs[:-3], refs[-3:]
-    tiles = token_tiles(tokens.shape[1])
-
-    @pl.when(pl.program_id(0) == 0)
-    def _():
-        for tile in tiles:
-            unit, _ = norm_parts(tokens[:, tile].astype(F32))
-            normed[:, tile] = (unit * params[:, 0:1] + params[:, 1:2]).astype(BF16)
-
+    blocks, (weights, out) = refs[:-2], refs[-2:]
     row_blocks = math.isqrt(len(blocks))
     for index, block in enumerate(blocks):
         lay(weights.at[0], index // row_blocks, index % row_blocks, block.at[0])
     out[0] = tn(weights[0], normed[...]).astype(BF16)
 
 
-def front(gathered, slot_of, params, tokens, row_blocks):
-    features, length = tokens.shape
+def front(gathered, slot_of, normed, row_blocks):
+    features, length = normed.shape
     square = row_blocks * row_blocks
-    whole = lambda shape: pl.BlockSpec(shape, lambda s, v: (0,) * len(shape), pipeline_mode=ONCE)
     blocks = block_specs(gathered, row_blocks, row_blocks, lambda s, i, j: s * square + i * row_blocks + j)
     return pl.pallas_call(
         front_kernel,
         grid_spec=pltpu.PrefetchScalarGridSpec(
             num_scalar_prefetch=1,
             grid=(3,),
-            in_specs=[whole(params.shape), whole((features, length))] + blocks,
+            in_specs=[pl.BlockSpec((features, length), lambda s, v: (0, 0), pipeline_mode=ONCE)] + blocks,
             out_specs=[
                 pl.BlockSpec((1, features, features), lambda s, v: (s, 0, 0)),
                 pl.BlockSpec((1, features, length), lambda s, v: (s, 0, 0)),
-                pl.BlockSpec((features, length), lambda s, v: (0, 0)),
             ],
         ),
         out_shape=[
             jax.ShapeDtypeStruct((3, features, features), BF16),
             jax.ShapeDtypeStruct((3, features, length), BF16),
-            jax.ShapeDtypeStruct((features, length), BF16),
         ],
         compiler_params=pltpu.CompilerParams(vmem_limit_bytes=60 << 20),
         name="front",
-    )(slot_of, params, tokens, *([gathered] * square))
+    )(slot_of, normed, *([gathered] * square))
 
 
 def gelu_pair(values):
@@ -708,7 +733,7 @@
         lay(w_down, index // row_blocks, index % row_blocks, down_blocks[index].at[0])
 
     def advance(index, carry):
-        tile = at(index)
+        tile = pl.ds(pl.multiple_of(index * wide, wide), wide)
         for part in parts:
             value, slope = gelu_pair(tn(w_up[:, part], normed[:, tile]))
             activated[part, tile] = value.astype(BF16)
@@ -718,7 +743,8 @@
             grad_middle[part, tile] += nn(w_up[part, :], grad_pre[:, tile])
         return carry
 
-    lax.fori_loop(0, tiles, advance, 0)
+    wide = 2 * GB if tiles % 2 == 0 else GB
+    lax.fori_loop(0, grad_low.shape[1] // wide, advance, 0)
 
     @pl.when(step == last)
     def _():
@@ -863,6 +889,104 @@
     )(*operands)
 
 
+def weight_grads_kernel(starts, col_blocks, size, slot_of, *refs):
+    activated, grad_low, normed, grad_pre, attended, grad_branch, grads, left, right, stage, get, put = refs
+    out_start, up_start, down_start = starts
+    side_length = left.shape[1]
+    row_blocks = side_length // size
+    count = row_blocks * row_blocks
+    parts = activated.shape[0] // side_length
+    step, steps = pl.program_id(0), pl.num_programs(0)
+    now = step % 2
+
+    def rows(index):
+        return pl.ds(pl.multiple_of(index * side_length, 16), side_length)
+
+    def fetch(index, buffer):
+        def start(one, other):
+            pltpu.make_async_copy(one, left.at[buffer], get.at[0, buffer]).start()
+            pltpu.make_async_copy(other, right.at[buffer], get.at[1, buffer]).start()
+
+        @pl.when(index < parts)
+        def _():
+            start(activated.at[rows(index)], grad_low)
+
+        @pl.when((index >= parts) & (index < 2 * parts))
+        def _():
+            start(normed, grad_pre.at[rows(index - parts)])
+
+        @pl.when(index == 2 * parts)
+        def _():
+            start(attended, grad_branch)
+
+    def copy(buffer, index, slot):
+        return pltpu.make_async_copy(stage.at[buffer, index], grads.at[slot], put.at[buffer, index])
+
+    @pl.when(step == 0)
+    def _():
+        fetch(0, 0)
+
+    @pl.when(step + 1 < steps)
+    def _():
+        fetch(step + 1, 1 - now)
+
+    pltpu.make_async_copy(normed, left.at[now], get.at[0, now]).wait()
+    pltpu.make_async_copy(normed, right.at[now], get.at[1, now]).wait()
+
+    @pl.when(step >= 2)
+    def _():
+        for index in range(count):
+            copy(now, index, 0).wait()
+
+    up = (step >= parts) & (step < 2 * parts)
+    start = jnp.where(up, up_start + (step - parts) * row_blocks, out_start)
+    start = jnp.where(step < parts, down_start + step * count, start)
+    stride = jnp.where(up, col_blocks, row_blocks)
+    other = right[now]
+    for i in range(row_blocks):
+        panel = nt(left[now, size * i : size * (i + 1), :], other)
+        for j in range(row_blocks):
+            index = i * row_blocks + j
+            block = panel[:, size * j : size * (j + 1)]
+            stage[now, index, :size] = block[:, :MAIN].astype(BF16)
+            stage[now, index, size:] = pack_tail(block).astype(BF16)
+            copy(now, index, slot_of[start + i * stride + j]).start()
+
+    @pl.when(step == steps - 1)
+    def _():
+        for index in range(count):
+            copy(now, index, 0).wait()
+            copy(1 - now, index, 0).wait()
+
+
+def weight_grads(slot_of, operands, slot_count, size, starts, col_blocks):
+    hidden, length = operands[0].shape
+    features = operands[1].shape[0]
+    count = (features // size) ** 2
+    steps = 2 * (hidden // features) + 1
+    anywhere = pl.BlockSpec(memory_space=pl.ANY)
+    part = pltpu.VMEM((2, features, length), BF16)
+    return pl.pallas_call(
+        functools.partial(weight_grads_kernel, starts, col_blocks, size),
+        grid_spec=pltpu.PrefetchScalarGridSpec(
+            num_scalar_prefetch=1,
+            grid=(steps,),
+            in_specs=[anywhere] * 6,
+            out_specs=anywhere,
+            scratch_shapes=[
+                part,
+                part,
+                pltpu.VMEM((2, count, size + RUN, MAIN), BF16),
+                pltpu.SemaphoreType.DMA((2, 2)),
+                pltpu.SemaphoreType.DMA((2, count)),
+            ],
+        ),
+        out_shape=jax.ShapeDtypeStruct((slot_count, size + RUN, MAIN), BF16),
+        cost_estimate=cost(2 * steps * features * features * length, 8 * steps * features * length),
+        name="weight_grads",
+    )(slot_of, *operands)
+
+
 EXTRA = 8
 FAR = -1e30
 
@@ -1138,35 +1262,26 @@
     seq_index = lax.axis_index("seq")
 
     slot_of = jnp.zeros((slot_count,), jnp.int32).at[owner_map].set(jnp.arange(slot_count, dtype=jnp.int32))
+    own_tokens = tokens.reshape(length, features).T
+    norms = jnp.stack([norm_gains[0], norm_shifts[0], norm_gains[1], norm_shifts[1]])
+    params = norms.T
     if known:
-        gathered = gather_slots(pack_slots(weight_copy, chip.reshape(1), slot_count), slots)
+        half = slots // 2
+        begin = seq_index.astype(jnp.int32) * half
+        placed = pack_slots(weight_copy, jnp.stack([begin, chip * slots + begin]), half, slot_count)
+        gathered, normed_in = gather_slots(placed, own_tokens, params, slots)
     else:
-        packed = pack_slots(weight_copy, jnp.zeros((1,), jnp.int32), slots)
+        packed = pack_slots(weight_copy, jnp.zeros((2,), jnp.int32), slots, slots)
         gathered = lax.all_gather(packed, "dp", axis=0, tiled=True)
+        prefix_tokens = lax.all_gather(own_tokens[:, :PREFIX], "seq")[0]
+        unit_all, _ = norm_parts(jnp.concatenate([prefix_tokens, own_tokens], axis=1).astype(F32))
+        normed_in = (unit_all * params[:, 0:1] + params[:, 1:2]).astype(BF16)
+    starts = (3 * square, 4 * square, 4 * square + row_blocks * col_blocks)
 
     def three_of(i, j):
         return (j // row_blocks) * square + i * row_blocks + j % row_blocks
 
-    def out_of(i, j):
-        return 3 * square + i * row_blocks + j
-
-    def up_of(i, j):
-        return 4 * square + i * col_blocks + j
-
-    def down_of(i, j):
-        return 4 * square + row_blocks * col_blocks + i * row_blocks + j
-
-    own_tokens = tokens.reshape(length, features).T
-    prefix_tokens = own_tokens[:, :PREFIX]
-    if cores == 2:
-        arrived = lax.ppermute(prefix_tokens, "seq", [(0, 1)])
-        prefix_tokens = jnp.where(seq_index == 0, prefix_tokens, arrived)
-    else:
-        prefix_tokens = lax.all_gather(prefix_tokens, "seq")[0]
-    norms = jnp.stack([norm_gains[0], norm_shifts[0], norm_gains[1], norm_shifts[1]])
-    params = norms.T
-    all_tokens = jnp.concatenate([prefix_tokens, own_tokens], axis=1)
-    w_three, qkv, normed_in = front(gathered, slot_of, params, all_tokens, row_blocks)
+    w_three, qkv = front(gathered, slot_of, normed_in, row_blocks)
 
     position = seq_index * length + jnp.arange(length, dtype=jnp.int32)
     alive = jnp.where(position < PREFIX, position < prefix_len[0], pad_mask[0] == 1)
@@ -1180,9 +1295,8 @@
     block_out, activated, grad_pre, normed_mid, grad_branch, grad_att, grad_middle, sums = middle_part(
         gathered, slot_of, params, own_tokens, attended, grad_low, row_blocks, col_blocks
     )
-    grads = weight_grad(activated, grad_low, slot_of, None, slot_count, size, down_of, "grad_down")
-    grads = weight_grad(normed_mid, grad_pre, slot_of, grads, slot_count, size, up_of, "grad_up")
-    grads = weight_grad(attended, grad_branch, slot_of, grads, slot_count, size, out_of, "grad_out")
+    operands = (activated, grad_low, normed_mid, grad_pre, attended, grad_branch)
+    grads = weight_grads(slot_of, operands, slot_count, size, starts, col_blocks)
     grad_three = attention_back(qkv, extras, attended, log_total, grad_att)
     flat_three = grad_three.reshape(3 * features, PREFIX + length)
     grads = weight_grad(normed_in, flat_three, slot_of, grads, slot_count, size, three_of, "grad_three")

time: 572 us -> 546 us (0.955); the launches traced: 563 us -> 544 us
  Pallas kernels: 540 us -> 526 us
    pallas_call x4 -> x1, Pallas kernels: 61.8 us -> 17 us  [weight_grad(): pl.pallas_call(functools.partial(weight_grad_kernel, block_of, deep, size...]
    pallas_call x1 -> x2, Pallas kernels: 133 us -> 173 us  [the longest x1 137 us: gather_slots(): pl.pallas_call(functools.partial(gather_kernel, slots), out_shape=[jax.Sh...]
  transfers between devices with their start and end apart: 1 -> 0, of which waited for: 0 -> 0; matrix products, arithmetic and copies ran while one was open for 1% -> 0% of each run, Pallas kernels for 25% -> 0%
where the time goes in v4:
time: 546 us; the launch traced here: 544 us
  Pallas kernels  526 us (96%)
  local copies, waits for them, and re-layouts  9.59 us (2%)
  other arithmetic  6.81 us (1%)
    pallas_call x1, Pallas kernels, reduce_slots(): pl.pallas_call(functools.partial(reduce_kernel, slots), out_shape=[jax.Sh...  140 us
    pallas_call x1, Pallas kernels, gather_slots(): pl.pallas_call(functools.partial(gather_kernel, slots), out_shape=[jax.Sh...  137 us
    pallas_call x1, Pallas kernels, middle_part(): pl.pallas_call(functools.partial(middle_kernel, row_blocks), grid_spec=pl...  94.8 us
    pallas_call x1, Pallas kernels, weight_grads(): pl.pallas_call(functools.partial(weight_grads_kernel, starts, col_blocks,...  36.3 us
    pallas_call x1, Pallas kernels, optimizer(): pl.pallas_call(functools.partial(optimizer_kernel, scale), grid=(slots,),...  28.6 us
    pallas_call x1, Pallas kernels, attention_back(): pl.pallas_call(functools.partial(attention_back_kernel, head ** (-0.5)),...  26 us
    pallas_call x1, Pallas kernels, front(): pl.pallas_call(front_kernel, grid_spec=pltpu.PrefetchScalarGridSpec(num_s...  20.9 us
    pallas_call x1, Pallas kernels, attention(): pl.pallas_call(functools.partial(attention_kernel, head ** (-0.5)), grid=...  19.2 us

profile of v4, /device:TPU:0, one launch (start us, length us, event | category | flops | bytes accessed | tf_op | source)
XLA Modules:
  0.0 544.2 jit_solution(6865258847516033831)
XLA Ops:
  1.3 0.6 pad_add_fusion.start
  1.9 0.1 pad.10.clone
  2.0 0.7 compare_select_fusion.1
  2.7 1.7 scatter_custom_fusion.slot_of
  4.4 0.1 broadcast_bitcast_fusion
  4.5 0.7 compare_select_fusion
  5.3 0.1 stack.53
  5.4 0.1 maximum_bitcast_fusion
  5.4 1.3 pad_maximum_fusion.extras
  6.8 0.8 fusion.5
  7.6 0.0 copy-start
  7.6 0.0 copy-start.2
  7.6 0.0 copy-start.4
  7.6 0.0 copy-start.6
  7.6 0.5 copy-done
  8.2 0.0 copy-done.2
  8.2 0.0 copy-done.4
  8.2 0.0 copy-done.6
  8.2 1.1 copy.35
  9.3 5.3 pack_slots.1.placed
  14.5 137.0 %gather_slots.1 = (bf16[192,312,256]{2,1,0:T(8,128)(2,1)}, bf16[1120,1152]{1,0:T(8,128)(2,1)}) custom-call(bf16[192,312,256]{2,1,0:T(8,128)(2,1)} %pack_slots.1.placed, bf16[1120,1024]{1,0:T(8,128)(2,1)} %bitcast.29, f32[1120,4]{1,0:T(8,128)} %bitcast.32), custom_call_target="tpu_custom_call", output_to_operand_aliasing={{0}: (0, {})} | custom-call | tf_op jit(solution)/shard_map/gather_slots/pallas_call | solution.py:302
  151.5 20.9 %front.1 = (bf16[3,1120,1120]{2,1,0:T(8,128)(2,1)}, bf16[3,1120,1152]{2,1,0:T(8,128)(2,1)}) custom-call(s32[192]{0:T(256)} %scatter_custom_fusion.slot_of, bf16[1120,1152]{1,0:T(8,128)(2,1)} %get-tuple-element.33.normed.left, ...), custom_call_target="tpu_custom_call" | custom-call | tf_op jit(solution)/shard_map/front/pallas_call | solution.py:661
  172.4 19.2 %attention.1 = (bf16[1120,1024]{1,0:T(8,128)(2,1)}, f32[20,1,1024]{2,1,0:T(1,128)}) custom-call(bf16[3,1120,1152]{2,1,0:T(8,128)(2,1)} %get-tuple-element.35.qkv, bf16[3,8,1152]{2,1,0:T(8,128)(2,1)} %pad_maximum_fusion.extras), custom_call_target="tpu_custom_call" | custom-call | flops 2348810240 | bytes 7741440 | tf_op jit(solution)/shard_map/attention/pallas_call | solution.py:1139
  191.6 94.8 %middle_part.1 = (bf16[1120,1024]{1,0:T(8,128)(2,1)}, bf16[4480,1024]{1,0:T(8,128)(2,1)}, bf16[4480,1024]{1,0:T(8,128)(2,1)}, bf16[1120,1024]{1,0:T(8,128)(2,1)}...) custom-call(s32[192]{0:T(256)} %scatter_custom_fusion.slot_of, ...), custom_call_target="tpu_custom_call" | custom-call | tf_op jit(solution)/shard_map/middle_part/pallas_call | solution.py:791
  286.4 26.0 %attention_back.1.grad_three = bf16[3,1120,1152]{2,1,0:T(8,128)(2,1)} custom-call(bf16[3,1120,1152]{2,1,0:T(8,128)(2,1)} %get-tuple-element.35.qkv, bf16[3,8,1152]{2,1,0:T(8,128)(2,1)} %pad_maximum_fusion.extras, bf16[1120,1024]{1,0:T(8,128)(2,1)} %get-tuple-element.36.attended.out.refs_4_, f32[20,1,1024]{2,1,0:T(1,128)} %get-tuple-element.38.lse, ...), custom_call_target="tpu_custom_call" | custom-call | flops 5872025600 | bytes 15482880 | tf_op jit(solution)/shard_map/attention_back/pallas_call | solution.py:1156
  312.5 36.3 %weight_grads.1.refs_0_ = bf16[192,312,256]{2,1,0:T(8,128)(2,1)} custom-call(s32[192]{0:T(256)} %scatter_custom_fusion.slot_of, bf16[4480,1024]{1,0:T(8,128)(2,1)} %get-tuple-element.40.refs_0_, bf16[1120,1024]{1,0:T(8,128)(2,1)} %bitcast.37, bf16[1120,1024]{1,0:T(8,128)(2,1)} %get-tuple-element.41.refs_2_, bf16[4480,1024]{1,0:T(8,128)(2,1)} %get-tuple-element.42.refs_3_, ...), custom_call_target="tpu_custom_call" | custom-call | flops 23121100800 | bytes 82575360 | tf_op jit(solution)/shard_map/weight_grads/pallas_call | solution.py:969
  348.8 17.0 %grad_three.1.grads = bf16[192,312,256]{2,1,0:T(8,128)(2,1)} custom-call(s32[192]{0:T(256)} %scatter_custom_fusion.slot_of, bf16[1120,1152]{1,0:T(8,128)(2,1)} %get-tuple-element.33.normed.left, bf16[3360,1152]{1,0:T(8,128)(2,1)} %bitcast.28, bf16[192,312,256]{2,1,0:T(8,128)(2,1)} %weight_grads.1.refs_0_), custom_call_target="tpu_custom_call", output_to_operand_aliasing={{}: (3, {})} | custom-call | flops 8670412800 | bytes 17848320 | tf_op jit(solution)/shard_map/grad_three/pallas_call | solution.py:866
  365.8 0.0 copy-start.1
  365.9 0.0 copy-start.3
  365.9 0.0 copy-start.5
  365.9 0.0 copy-start.7
  365.9 140.4 %reduce_slots.1 = (f32[12,312,256]{2,1,0:T(8,128)}, f32[1120,1024]{1,0:T(8,128)}, f32[8,1120]{1,0:T(8,128)}) custom-call(bf16[192,312,256]{2,1,0:T(8,128)(2,1)} %grad_three.1.grads, bf16[3,1120,1120]{2,1,0:T(8,128)(2,1)} %get-tuple-element.44.w_three, bf16[3,1120,1152]{2,1,0:T(8,128)(2,1)} %attention_back.1.grad_three, bf16[1120,1024]{1,0:T(8,128)(2,1)} %bitcast.31, ...), custom_call_target="tpu_custom_call" | custom-call | tf_op jit(solution)/shard_map/reduce_slots/pallas_call | solution.py:578
  506.3 2.0 multiply_reduce_fusion
  509.0 0.0 copy-done.1
  509.0 0.0 copy-done.3
  509.0 0.0 copy-done.5
  509.0 0.0 copy-done.7
  509.1 1.4 multiply_subtract_fusion
  510.5 28.6 %optimizer.1 = (f32[12,280,280]{2,1,0:T(8,128)}, f32[12,280,280]{2,1,0:T(8,128)}, f32[12,280,280]{2,1,0:T(8,128)}, f32[12,280,280]{2,1,0:T(8,128)}, bf16[12,280,...) custom-call(f32[12,312,256]{2,1,0:T(8,128)} %get-tuple-element.49.packed, f32[12,280,280]{2,1,0:T(8,128)} %master.1, ...), custom_call_target="tpu_custom_call" | custom-call | tf_op jit(solution)/shard_map/optimizer/pallas_call | solution.py:1210
  539.1 5.1 copy.41
  (14 shorter events, 0.1 us)
Async XLA Ops:
  7.6 0.6 copy-start
  7.6 0.6 copy-start.2
  7.6 0.6 copy-start.4
  7.6 0.6 copy-start.6
  365.8 143.2 %copy-start.1 = (f32[1,1120]{1,0:T(1,128)S(1)}, f32[1,1120]{1,0:T(1,128)}, u32[]{:S(2)}) copy-start(f32[1,1120]{1,0:T(1,128)} %copy-done) | copy-start | bytes 13444
  365.9 143.2 %copy-start.3 = (f32[1,1120]{1,0:T(1,128)S(1)}, f32[1,1120]{1,0:T(1,128)}, u32[]{:S(2)}) copy-start(f32[1,1120]{1,0:T(1,128)} %copy-done.2) | copy-start | bytes 13444
  365.9 143.2 %copy-start.5 = (f32[1,1120]{1,0:T(1,128)S(1)}, f32[1,1120]{1,0:T(1,128)}, u32[]{:S(2)}) copy-start(f32[1,1120]{1,0:T(1,128)} %copy-done.4) | copy-start | bytes 13444
  365.9 143.2 %copy-start.7 = (f32[1,1120]{1,0:T(1,128)S(1)}, f32[1,1120]{1,0:T(1,128)}, u32[]{:S(2)}) copy-start(f32[1,1120]{1,0:T(1,128)} %copy-done.6) | copy-start | bytes 13444

commit v5 on v4

--- a/solution.py
+++ b/solution.py
@@ -398,8 +398,11 @@
     turns += [(where[0], 1, 0), (where[3], 1, 1), (where[3], 0, 1), (where[0], 0, 0), (where[1], 1, 0)]
     turns += [(where[2], 1, 0), (where[1], 0, 0), (where[3], 1, 0), (where[2], 0, 0), (where[3], 0, 0)]
 
+    def load_piece(chip, slot):
+        return pltpu.make_async_copy(piece(chip, core), ring.at[slot], load.at[slot])
+
     def load_own(turn):
-        return pltpu.make_async_copy(piece(chip_at(*turns[turn]), core), ring.at[turn % RING], load.at[turn % RING])
+        return load_piece(chip_at(*turns[turn]), turn % RING)
 
     def add_up(turn, others):
         chip = chip_at(*turns[turn])
@@ -452,8 +455,25 @@
     ]
     for fetch in fetches:
         fetch.start()
-    for turn in range(6):
-        send_second(turn)
+    def early(turn, carry):
+        def pick(values):
+            return sum(jnp.where(turn == index, value, 0) for index, value in enumerate(values))
+
+        zz, a, slot = pick([t[0] for t in turns[:6]]), 1 - turn % 2, turn % RING
+        chip, after = chip_at(zz, a, 1), pick([chip_at(*t) for t in turns[RING : RING + 6]])
+        load_piece(chip, slot).wait()
+        twin(zz, a, 1).wait_recv()
+
+        def body(s, inner_carry):
+            r_twin[chip, s] = (ring[slot, s].astype(F32) + r_twin[chip, s].astype(F32)).astype(BF16)
+            return inner_carry
+
+        lax.fori_loop(0, half, body, 0)
+        load_piece(after, slot).start()
+        to_second(zz, a).start()
+        return carry
+
+    lax.fori_loop(0, 6, early, 0)
     send_first(6)
     send_second(7)
     send_second(8)
@@ -988,6 +1008,7 @@
 
 
 EXTRA = 8
+TOGETHER = 2
 FAR = -1e30
 
 
@@ -1008,26 +1029,30 @@
     return jnp.concatenate([left, right], axis=1)
 
 
-def attention_kernel(scale, qkv, extras, out, lse, queries, keys, values, keys_t):
-    head = qkv.shape[1]
+def attention_kernel(scale, head, qkv, extras, out, lse, queries, keys, values, keys_t):
     unit = scale * math.log2(math.e)
+    heads = range(queries.shape[0])
 
     @pl.when(pl.program_id(0) == 0)
     def _():
-        queries[head:] = extras[0]
-        keys[head:] = extras[1]
-        values[head:] = extras[2]
-
-    queries[:head] = qkv[0]
-    keys[:head] = qkv[1]
-    values[:head] = qkv[2]
-    keys_t[...] = keys[...].T
+        for k in heads:
+            queries[k, head:] = extras[0]
+            keys[k, head:] = extras[1]
+            values[k, head:] = extras[2]
+
+    for k in heads:
+        rows = slice(head * k, head * (k + 1))
+        queries[k, :head] = qkv[0, rows]
+        keys[k, :head] = qkv[1, rows]
+        values[k, :head] = qkv[2, rows]
+    for k in heads:
+        keys_t[k] = keys[k].T
     ahead = causal()
-    spots = places(out.shape[1] // GB)
+    spots = [(k,) + spot for k in heads for spot in places(out.shape[1] // GB)]
     scores = []
-    for low, high, both, _ in spots:
-        asked = queries[:, both]
-        scores.append((nn(keys_t[:PREFIX], asked), nn(keys_t[low], asked), nn(keys_t[high], asked[:, HALF:])))
+    for k, low, high, both, _ in spots:
+        asked = queries[k, :, both]
+        scores.append((nn(keys_t[k, :PREFIX], asked), nn(keys_t[k, low], asked), nn(keys_t[k, high], asked[:, HALF:])))
 
     def peak(array):
         return jnp.max(array, axis=0, keepdims=True)
@@ -1043,12 +1068,12 @@
         top = side(top[:, :HALF], jnp.maximum(top[:, HALF:], peak(second)))
         tops.append(top)
         weights.append((soft(prefix, top), soft(first, top), soft(second, top[:, HALF:])))
-    for (low, high, _, mine), top, (prefix, first, second) in zip(spots, tops, weights):
-        sums = nn(values[:, :PREFIX], prefix) + nn(values[:, low], first)
-        sums = side(sums[:, :HALF], sums[:, HALF:] + nn(values[:, high], second))
+    for (k, low, high, _, mine), top, (prefix, first, second) in zip(spots, tops, weights):
+        sums = nn(values[k, :, :PREFIX], prefix) + nn(values[k, :, low], first)
+        sums = side(sums[:, :HALF], sums[:, HALF:] + nn(values[k, :, high], second))
         total = sums[head : head + 1]
-        out[:, mine] = (sums[:head] / total).astype(BF16)
-        lse[0, :, mine] = top + jnp.log(total) * (1.0 / scale)
+        out[head * k : head * (k + 1), mine] = (sums[:head] / total).astype(BF16)
+        lse[k, :, mine] = top + jnp.log(total) * (1.0 / scale)
 
 
 def thirds(values):
@@ -1065,80 +1090,91 @@
     return base.astype(BF16)
 
 
-def attention_back_kernel(scale, qkv, extras, out, lse, grad_out, grads, queries, keys, values, grad_o, keys_t, values_t):
-    head, own = qkv.shape[1], out.shape[1]
+def attention_back_kernel(
+    scale, head, qkv, extras, out, lse, grad_out, grads, queries, keys, values, grad_o, keys_t, values_t
+):
+    own = out.shape[1]
     unit = scale * math.log2(math.e)
+    heads = range(queries.shape[0])
 
     @pl.when(pl.program_id(0) == 0)
     def _():
-        keys[head:] = extras[1]
-        values[head:] = extras[2]
-
-    queries[:head] = qkv[0, :, PREFIX:]
-    keys[:head] = qkv[1]
-    values[:head] = qkv[2]
-    grad_o[:head] = grad_out[...]
-    keys_t[...] = keys[...].T
-    values_t[...] = values[...].T
-    queries[head:] = with_rows(extras[0, :, PREFIX:].astype(F32), 2, thirds(-lse[0]))
-    delta = jnp.sum(grad_out[...].astype(F32) * out[...].astype(F32), axis=0, keepdims=True)
-    grad_o[head:] = with_rows(jnp.zeros((EXTRA, own), F32), 0, thirds(-delta))
+        for k in heads:
+            keys[k, head:] = extras[1]
+            values[k, head:] = extras[2]
+
+    for k in heads:
+        rows = slice(head * k, head * (k + 1))
+        queries[k, :head] = qkv[0, rows, PREFIX:]
+        keys[k, :head] = qkv[1, rows]
+        values[k, :head] = qkv[2, rows]
+        given = grad_out[rows]
+        grad_o[k, :head] = given
+        queries[k, head:] = with_rows(extras[0, :, PREFIX:].astype(F32), 2, thirds(-lse[k]))
+        delta = jnp.sum(given.astype(F32) * out[rows].astype(F32), axis=0, keepdims=True)
+        grad_o[k, head:] = with_rows(jnp.zeros((EXTRA, own), F32), 0, thirds(-delta))
+    for k in heads:
+        keys_t[k] = keys[k].T
+        values_t[k] = values[k].T
     ahead = causal()
-    spots = places(own // GB)
-
-    def weigh(rows, asked, given, mask):
-        weights = jnp.exp2(nn(keys_t[rows], asked) * unit)
+    spots = [(k,) + spot for k in heads for spot in places(own // GB)]
+
+    def weigh(k, rows, asked, given, mask):
+        weights = jnp.exp2(nn(keys_t[k, rows], asked) * unit)
         if mask == 1:
             weights = side(jnp.where(ahead, weights[:, :HALF], 0.0), weights[:, HALF:])
         if mask == 2:
             weights = jnp.where(ahead, weights, 0.0)
-        return weights.astype(BF16), (weights * nn(values_t[rows], given)).astype(BF16)
+        return weights.astype(BF16), (weights * nn(values_t[k, rows], given)).astype(BF16)
 
     found = []
-    for low, high, _, mine in spots:
-        asked, given = queries[:, mine], grad_o[:, mine]
+    for k, low, high, _, mine in spots:
+        asked, given = queries[k, :, mine], grad_o[k, :, mine]
         found.append(
             (
-                weigh(slice(0, PREFIX), asked, given, 0),
-                weigh(low, asked, given, 1),
-                weigh(high, asked[:, HALF:], given[:, HALF:], 2),
+                weigh(k, slice(0, PREFIX), asked, given, 0),
+                weigh(k, low, asked, given, 1),
+                weigh(k, high, asked[:, HALF:], given[:, HALF:], 2),
             )
         )
-    prefix_k = prefix_v = None
-    for (low, high, both, mine), ((p0, d0), (p1, d1), (p2, d2)) in zip(spots, found):
-        asked, given = queries[:head, mine], grad_o[:head, mine]
-        grad_q = nn(keys[:head, :PREFIX], d0) + nn(keys[:head, low], d1)
-        grad_q = side(grad_q[:, :HALF], grad_q[:, HALF:] + nn(keys[:head, high], d2))
-        grads[0, :, both] = (grad_q * scale).astype(BF16)
+    prefix_k, prefix_v = {}, {}
+    for (k, low, high, both, mine), ((p0, d0), (p1, d1), (p2, d2)) in zip(spots, found):
+        rows = slice(head * k, head * (k + 1))
+        asked, given = queries[k, :head, mine], grad_o[k, :head, mine]
+        grad_q = nn(keys[k, :head, :PREFIX], d0) + nn(keys[k, :head, low], d1)
+        grad_q = side(grad_q[:, :HALF], grad_q[:, HALF:] + nn(keys[k, :head, high], d2))
+        grads[0, rows, both] = (grad_q * scale).astype(BF16)
         part_k, part_v = nt(asked, d0), nt(given, p0)
-        prefix_k = part_k if prefix_k is None else prefix_k + part_k
-        prefix_v = part_v if prefix_v is None else prefix_v + part_v
-        grads[1, :, low] = (nt(asked, d1) * scale).astype(BF16)
-        grads[2, :, low] = nt(given, p1).astype(BF16)
-        grads[1, :, high] = (nt(asked[:, HALF:], d2) * scale).astype(BF16)
-        grads[2, :, high] = nt(given[:, HALF:], p2).astype(BF16)
-    grads[0, :, :PREFIX] = jnp.zeros((head, PREFIX), BF16)
-    grads[1, :, :PREFIX] = (prefix_k * scale).astype(BF16)
-    grads[2, :, :PREFIX] = prefix_v.astype(BF16)
+        prefix_k[k] = prefix_k[k] + part_k if k in prefix_k else part_k
+        prefix_v[k] = prefix_v[k] + part_v if k in prefix_v else part_v
+        grads[1, rows, low] = (nt(asked, d1) * scale).astype(BF16)
+        grads[2, rows, low] = nt(given, p1).astype(BF16)
+        grads[1, rows, high] = (nt(asked[:, HALF:], d2) * scale).astype(BF16)
+        grads[2, rows, high] = nt(given[:, HALF:], p2).astype(BF16)
+    for k in heads:
+        rows = slice(head * k, head * (k + 1))
+        grads[0, rows, :PREFIX] = jnp.zeros((head, PREFIX), BF16)
+        grads[1, rows, :PREFIX] = (prefix_k[k] * scale).astype(BF16)
+        grads[2, rows, :PREFIX] = prefix_v[k].astype(BF16)
 
 
 def attention_specs(qkv):
     _, features, length = qkv.shape
     head, own = features // HEADS, length - PREFIX
-    three = pl.BlockSpec((3, head, length), lambda h: (0, h, 0))
+    three = pl.BlockSpec((3, TOGETHER * head, length), lambda h: (0, h, 0))
     extra = pl.BlockSpec((3, EXTRA, length), lambda h: (0, 0, 0))
-    one = pl.BlockSpec((head, own), lambda h: (h, 0))
-    row = pl.BlockSpec((1, 1, own), lambda h: (h, 0, 0))
-    wide = lambda columns: pltpu.VMEM((head + EXTRA, columns), BF16)
-    tall = pltpu.VMEM((length, head + EXTRA), BF16)
+    one = pl.BlockSpec((TOGETHER * head, own), lambda h: (h, 0))
+    row = pl.BlockSpec((TOGETHER, 1, own), lambda h: (h, 0, 0))
+    wide = lambda columns: pltpu.VMEM((TOGETHER, head + EXTRA, columns), BF16)
+    tall = pltpu.VMEM((TOGETHER, length, head + EXTRA), BF16)
     return features, length, own, head, three, extra, one, row, wide, tall
 
 
 def attention(qkv, extras):
     features, length, own, head, three, extra, one, row, wide, tall = attention_specs(qkv)
     return pl.pallas_call(
-        functools.partial(attention_kernel, head ** (-0.5)),
-        grid=(HEADS,),
+        functools.partial(attention_kernel, head ** (-0.5), head),
+        grid=(HEADS // TOGETHER,),
         in_specs=[three, extra],
         out_specs=[one, row],
         out_shape=[
@@ -1154,8 +1190,8 @@
 def attention_back(qkv, extras, out, lse, grad_out):
     features, length, own, head, three, extra, one, row, wide, tall = attention_specs(qkv)
     return pl.pallas_call(
-        functools.partial(attention_back_kernel, head ** (-0.5)),
-        grid=(HEADS,),
+        functools.partial(attention_back_kernel, head ** (-0.5), head),
+        grid=(HEADS // TOGETHER,),
         in_specs=[three, extra, one, row, one],
         out_specs=three,
         out_shape=jax.ShapeDtypeStruct(qkv.shape, BF16),
@@ -1187,14 +1223,24 @@
     return form(left_high, right_high) + (form(left_high, right_low) + form(left_low, right_high))
 
 
-def optimizer_kernel(scale, packed, master, average, left, right, root_left, root_right, *outs):
-    slot_grad, new_left, new_right, new_master, new_copy, new_average = outs
+def optimizer_kernel(scale, packed, master, average, left, right, root_left, root_right, passed, sums, norms, *outs):
+    slot_grad, new_left, new_right, new_master, new_copy, new_average, passed_on, norm_grad, new_norms = outs
     size = master.shape[1]
+    passed_on[...] = passed[...]
+
+    @pl.when(pl.program_id(0) == 0)
+    def _():
+        count = norms.shape[0]
+        scaled = sums[:count] * scale
+        norm_grad[...] = scaled
+        square = jnp.sum(jnp.sum(scaled * scaled, axis=1, keepdims=True), axis=0, keepdims=True)
+        new_norms[...] = norms[...] - 0.1 * scaled * lax.rsqrt(square * (1.0 / norms.size) + 1e-06)
+
     grad = unpack(packed[0]) * scale
     slot_grad[0] = grad
     grad_parts = split(grad)
-    new_left[0] = 0.5 * left[0] + (0.5 / size) * product(nt, grad_parts, grad_parts)
-    new_right[0] = 0.5 * right[0] + (0.5 / size) * product(tn, grad_parts, grad_parts)
+    new_left[0] = 0.5 * left[0] + (0.5 / size) * nt(grad_parts[0], grad_parts[0])
+    new_right[0] = 0.5 * right[0] + (0.5 / size) * tn(grad_parts[0], grad_parts[0])
     right_part = product(nn, grad_parts, split(root_right[0]))
     step = product(nn, split(root_left[0]), split(right_part))
     moved = master[0] - 0.03 * step
@@ -1203,18 +1249,25 @@
     new_average[0] = 0.8 * average[0] + 0.2 * moved
 
 
-def optimizer(packed, scale, arrays):
+def optimizer(packed, scale, arrays, passed, sums, norms):
     slots, size, _ = arrays[0].shape
     block = pl.BlockSpec((1, size, size), lambda i: (i, 0, 0))
+    whole = lambda array: pl.BlockSpec(array.shape, lambda i: (0, 0))
     shape = lambda dtype: jax.ShapeDtypeStruct((slots, size, size), dtype)
+    width = 128 * -(-passed.shape[1] // (128 * slots))
+    last = passed.shape[1] // width - 1
+    strip = pl.BlockSpec((passed.shape[0], width), lambda i: (0, jnp.minimum(i, last)))
+    same = lambda array: jax.ShapeDtypeStruct(array.shape, F32)
     return pl.pallas_call(
         functools.partial(optimizer_kernel, scale),
         grid=(slots,),
-        in_specs=[pl.BlockSpec((1,) + packed.shape[1:], lambda i: (i, 0, 0))] + [block] * 6,
-        out_specs=[block] * 6,
-        out_shape=[shape(F32), shape(F32), shape(F32), shape(F32), shape(BF16), shape(F32)],
+        in_specs=[pl.BlockSpec((1,) + packed.shape[1:], lambda i: (i, 0, 0))]
+        + [block] * 6
+        + [strip, whole(sums), whole(norms)],
+        out_specs=[block] * 6 + [strip, whole(norms), whole(norms)],
+        out_shape=[shape(F32)] * 4 + [shape(BF16), shape(F32), same(passed), same(norms), same(norms)],
         name="optimizer",
-    )(packed, *arrays)
+    )(packed, *arrays, passed, sums, norms)
 
 
 def norm_parts(values):
@@ -1315,11 +1368,8 @@
         grad_input = grad_middle + norm_back(unit_one, scale_one, params[:, 0:1], grad_normed)
         first_sums = [jnp.sum(grad_normed * unit_one, axis=1), jnp.sum(grad_normed, axis=1)]
         norm_sums = lax.psum(jnp.stack(first_sums + [sums[2], sums[3]]), ("dp", "seq"))
-    norm_grad = norm_sums[:4] * grad_scale
-    new_norms = norms - 0.1 * norm_grad * lax.rsqrt(jnp.mean(norm_grad * norm_grad) + 1e-06)
-    stepped = optimizer(
-        summed, grad_scale, (master, average_weights, stat_left, stat_right, root_left, root_right)
-    )
+    arrays = (master, average_weights, stat_left, stat_right, root_left, root_right)
+    *stepped, grad_input, norm_grad, new_norms = optimizer(summed, grad_scale, arrays, grad_input, norm_sums, norms)
     token_shape = (cell_count, length, features)
     return (
         block_out.T.reshape(token_shape),

time: 546 us -> 532 us (0.974)
  local copies, waits for them, and re-layouts: 9.59 us -> 3.87 us
    pallas_call x2, Pallas kernels: 45.2 us -> 38.2 us  [the longest x1 24.3 us: attention_back(): pl.pallas_call(functools.partial(attention_back_kernel, head ** (-0.5), h...]
    unnamed x19 -> x2, local copies, waits for them, and re-layouts: 5.81 us -> 0.08 us
where the time goes in v5:
time: 532 us; the launch traced here: 531 us
  Pallas kernels  521 us (98%)
    pallas_call x1, Pallas kernels, reduce_slots(): pl.pallas_call(functools.partial(reduce_kernel, slots), out_shape=[jax.Sh...  140 us
    pallas_call x1, Pallas kernels, gather_slots(): pl.pallas_call(functools.partial(gather_kernel, slots), out_shape=[jax.Sh...  137 us
    pallas_call x1, Pallas kernels, middle_part(): pl.pallas_call(functools.partial(middle_kernel, row_blocks), grid_spec=pl...  94.8 us
    pallas_call x1, Pallas kernels, weight_grads(): pl.pallas_call(functools.partial(weight_grads_kernel, starts, col_blocks,...  36.3 us
    pallas_call x1, Pallas kernels, optimizer(): pl.pallas_call(functools.partial(optimizer_kernel, scale), grid=(slots,),...  31.6 us
    pallas_call x1, Pallas kernels, attention_back(): pl.pallas_call(functools.partial(attention_back_kernel, head ** (-0.5), h...  24.3 us
    pallas_call x1, Pallas kernels, front(): pl.pallas_call(front_kernel, grid_spec=pltpu.PrefetchScalarGridSpec(num_s...  20.9 us
    pallas_call x1, Pallas kernels, weight_grad(): pl.pallas_call(functools.partial(weight_grad_kernel, block_of, deep, size...  17 us

profile of v5, /device:TPU:0, one launch (start us, length us, event | category | flops | bytes accessed | tf_op | source)
XLA Modules:
  0.0 531.0 jit_solution(13468488065990431287)
XLA Ops:
  1.3 0.6 pad_add_fusion.start
  1.9 0.1 pad.10.clone
  2.0 0.7 compare_select_fusion.1
  2.7 1.7 scatter_custom_fusion.slot_of
  4.4 0.1 broadcast_bitcast_fusion
  4.5 0.7 compare_select_fusion
  5.3 0.1 stack.53
  5.4 0.1 maximum_bitcast_fusion
  5.4 1.3 pad_maximum_fusion.extras
  6.8 0.8 fusion.6
  7.6 0.6 pad_maximum_fusion.1
  8.2 1.1 copy.27.params
  9.3 5.2 pack_slots.1.placed
  14.5 136.9 %gather_slots.1 = (bf16[192,312,256]{2,1,0:T(8,128)(2,1)}, bf16[1120,1152]{1,0:T(8,128)(2,1)}) custom-call(bf16[192,312,256]{2,1,0:T(8,128)(2,1)} %pack_slots.1.placed, bf16[1120,1024]{1,0:T(8,128)(2,1)} %bitcast.30, f32[1120,4]{1,0:T(8,128)} %copy.27.params), custom_call_target="tpu_custom_call", output_to_operand_aliasing={{0}: (0, {})} | custom-call | tf_op jit(solution)/shard_map/gather_slots/pallas_call | solution.py:302
  151.5 20.9 %front.1 = (bf16[3,1120,1120]{2,1,0:T(8,128)(2,1)}, bf16[3,1120,1152]{2,1,0:T(8,128)(2,1)}) custom-call(s32[192]{0:T(256)} %scatter_custom_fusion.slot_of, bf16[1120,1152]{1,0:T(8,128)(2,1)} %get-tuple-element.36.normed.left, ...), custom_call_target="tpu_custom_call" | custom-call | tf_op jit(solution)/shard_map/front/pallas_call | solution.py:681
  172.4 13.9 %attention.1 = (bf16[1120,1024]{1,0:T(8,128)(2,1)}, f32[20,1,1024]{2,1,0:T(1,128)}) custom-call(bf16[3,1120,1152]{2,1,0:T(8,128)(2,1)} %get-tuple-element.38.qkv, bf16[3,8,1152]{2,1,0:T(8,128)(2,1)} %pad_maximum_fusion.extras), custom_call_target="tpu_custom_call" | custom-call | flops 2348810240 | bytes 7741440 | tf_op jit(solution)/shard_map/attention/pallas_call | solution.py:1175
  186.3 94.8 %middle_part.1 = (bf16[1120,1024]{1,0:T(8,128)(2,1)}, bf16[4480,1024]{1,0:T(8,128)(2,1)}, bf16[4480,1024]{1,0:T(8,128)(2,1)}, bf16[1120,1024]{1,0:T(8,128)(2,1)}...) custom-call(s32[192]{0:T(256)} %scatter_custom_fusion.slot_of, ...), custom_call_target="tpu_custom_call" | custom-call | tf_op jit(solution)/shard_map/middle_part/pallas_call | solution.py:811
  281.2 24.3 %attention_back.1.grad_three = bf16[3,1120,1152]{2,1,0:T(8,128)(2,1)} custom-call(bf16[3,1120,1152]{2,1,0:T(8,128)(2,1)} %get-tuple-element.38.qkv, bf16[3,8,1152]{2,1,0:T(8,128)(2,1)} %pad_maximum_fusion.extras, bf16[1120,1024]{1,0:T(8,128)(2,1)} %get-tuple-element.39.attended.out.refs_4_, f32[20,1,1024]{2,1,0:T(1,128)} %get-tuple-element.41.lse, ...), custom_call_target="tpu_custom_call" | custom-call | flops 5872025600 | bytes 15482880 | tf_op jit(solution)/shard_map/attention_back/pallas_call | solution.py:1192
  305.4 36.3 %weight_grads.1.refs_0_ = bf16[192,312,256]{2,1,0:T(8,128)(2,1)} custom-call(s32[192]{0:T(256)} %scatter_custom_fusion.slot_of, bf16[4480,1024]{1,0:T(8,128)(2,1)} %get-tuple-element.43.refs_0_, bf16[1120,1024]{1,0:T(8,128)(2,1)} %bitcast.34, bf16[1120,1024]{1,0:T(8,128)(2,1)} %get-tuple-element.44.refs_2_, bf16[4480,1024]{1,0:T(8,128)(2,1)} %get-tuple-element.45.refs_3_, ...), custom_call_target="tpu_custom_call" | custom-call | flops 23121100800 | bytes 82575360 | tf_op jit(solution)/shard_map/weight_grads/pallas_call | solution.py:989
  341.8 17.0 %grad_three.1.grads = bf16[192,312,256]{2,1,0:T(8,128)(2,1)} custom-call(s32[192]{0:T(256)} %scatter_custom_fusion.slot_of, bf16[1120,1152]{1,0:T(8,128)(2,1)} %get-tuple-element.36.normed.left, bf16[3360,1152]{1,0:T(8,128)(2,1)} %bitcast.29, bf16[192,312,256]{2,1,0:T(8,128)(2,1)} %weight_grads.1.refs_0_), custom_call_target="tpu_custom_call", output_to_operand_aliasing={{}: (3, {})} | custom-call | flops 8670412800 | bytes 17848320 | tf_op jit(solution)/shard_map/grad_three/pallas_call | solution.py:886
  358.8 140.4 %reduce_slots.1 = (f32[12,312,256]{2,1,0:T(8,128)}, f32[1120,1024]{1,0:T(8,128)}, f32[8,1120]{1,0:T(8,128)}) custom-call(bf16[192,312,256]{2,1,0:T(8,128)(2,1)} %grad_three.1.grads, bf16[3,1120,1120]{2,1,0:T(8,128)(2,1)} %get-tuple-element.47.w_three, bf16[3,1120,1152]{2,1,0:T(8,128)(2,1)} %attention_back.1.grad_three, bf16[1120,1024]{1,0:T(8,128)(2,1)} %bitcast.32, ...), custom_call_target="tpu_custom_call" | custom-call | tf_op jit(solution)/shard_map/reduce_slots/pallas_call | solution.py:598
  499.2 31.6 %optimizer.1 = (f32[12,280,280]{2,1,0:T(8,128)}, f32[12,280,280]{2,1,0:T(8,128)}, f32[12,280,280]{2,1,0:T(8,128)}, f32[12,280,280]{2,1,0:T(8,128)}, bf16[12,280,...) custom-call(f32[12,312,256]{2,1,0:T(8,128)} %get-tuple-element.50.pa, ...), custom_call_target="tpu_custom_call" | custom-call | tf_op jit(solution)/shard_map/optimizer/pallas_call | solution.py:1261
  (13 shorter events, 0.1 us)

commit v6 on v5

--- a/solution.py
+++ b/solution.py
@@ -112,7 +112,8 @@
     pl.semaphore_wait(barrier, len(partners))
 
 
-UP, DOWN, FIRST, SECOND, TWIN, HEAD, GATHER_LABELS = 0, 4, 8, 12, 20, 36, 37
+UP, DOWN, FIRST, SECOND, TWIN, HEAD = 0, 4, 8, 12, 20, 36
+LAST_FIRST, LAST_SECOND, LAST_UP, LAST_DOWN, LAST_TWIN, GATHER_LABELS = 37, 38, 40, 52, 64, 80
 
 
 def gather_kernel(slots, placed, tokens, params, out, normed, held, send, recv, take):
@@ -122,8 +123,9 @@
     line = [(me + 4 * ((z + r) % 4 - z), core) for r in range(1, 4)]
     greet([(me + first, core), (me + second, core), (me, 1 - core)] + line)
 
-    def copy(label, chip, dp, c):
-        ref = out.at[pl.ds(chip * slots + core * half, half)]
+    def copy(label, chip, dp, c, many=True):
+        start = chip * slots + core * half
+        ref = out.at[pl.ds(start, half - 1)] if many else out.at[pl.ds(start + half - 1, 1)]
         return pltpu.make_async_remote_copy(
             src_ref=ref,
             dst_ref=ref,
@@ -166,6 +168,38 @@
             to_second(zz, a).wait_recv()
             to_twin(col(zz) + second + a * first).start()
 
+    def off(q):
+        return (q % 2) * first + (q // 2) * second
+
+    def last_first():
+        return copy(LAST_FIRST, me, me + first, core, False)
+
+    def last_second(a):
+        return copy(LAST_SECOND + a, me + a * first, me + second, core, False)
+
+    def last_up(j, q):
+        return copy(LAST_UP + 4 * (j - 1) + q, me - 4 * (j - 1) + off(q), me + 4, core, False)
+
+    def last_down(j, q):
+        return copy(LAST_DOWN + 4 * (j - 1) + q, me + 4 * (j - 1) + off(q), me - 4, core, False)
+
+    def last_twin(chip):
+        return copy(LAST_TWIN + chip, chip, me, 1 - core, False)
+
+    def leave_plane(q):
+        last_twin(me + off(q)).start()
+
+        @pl.when(z < 3)
+        def _():
+            last_up(1, q).start()
+
+        @pl.when(z > 0)
+        def _():
+            last_down(1, q).start()
+
+    last_first().start()
+    last_second(0).start()
+
     @pl.when(z < 3)
     def _():
         up(1).start()
@@ -174,6 +208,7 @@
     def _():
         down(1).start()
 
+    leave_plane(0)
     spread(z)
 
     prefix, seat = tokens.at[:, pl.ds(0, PREFIX)], held.at[:, pl.ds(0, PREFIX)]
@@ -208,6 +243,11 @@
         return carry
 
     lax.fori_loop(0, held.shape[1] // PREFIX, normalize, 0)
+    last_first().wait_recv()
+    last_second(1).start()
+    leave_plane(1)
+    last_second(0).wait_recv()
+    leave_plane(2)
     for j in range(1, 4):
 
         @pl.when(z >= j)
@@ -243,6 +283,31 @@
             @pl.when(z + j - 1 <= 3)
             def _():
                 after_first(z + j - 1)
+
+        if j == 1:
+            last_second(1).wait_recv()
+            leave_plane(3)
+        for q in range(4):
+
+            @pl.when(z >= j)
+            def _():
+                last_up(j, q).wait_recv()
+                last_twin(me - 4 * j + off(q)).start()
+                if j < 3:
+
+                    @pl.when(z < 3)
+                    def _():
+                        last_up(j + 1, q).start()
+
+            @pl.when(z + j <= 3)
+            def _():
+                last_down(j, q).wait_recv()
+                last_twin(me + 4 * j + off(q)).start()
+                if j < 3:
+
+                    @pl.when(z > 0)
+                    def _():
+                        last_down(j + 1, q).start()
 
     @pl.when(z >= 3)
     def _():
@@ -269,27 +334,41 @@
                 chip = col(zz) + a * first + b * second
                 to_twin(chip).wait_recv()
                 to_twin(chip).wait_send()
+                last_twin(chip).wait_recv()
+                last_twin(chip).wait_send()
         to_first(zz).wait_send()
         for a in range(2):
             to_second(zz, a).wait_send()
 
+    last_first().wait_send()
+    for a in range(2):
+        last_second(a).wait_send()
+
     @pl.when(z < 3)
     def _():
         up(1).wait_send()
+        for q in range(4):
+            last_up(1, q).wait_send()
         for j in range(1, 3):
 
             @pl.when(z >= j)
             def _():
                 up(j + 1).wait_send()
+                for q in range(4):
+                    last_up(j + 1, q).wait_send()
 
     @pl.when(z > 0)
     def _():
         down(1).wait_send()
+        for q in range(4):
+            last_down(1, q).wait_send()
         for j in range(1, 3):
 
             @pl.when(z + j <= 3)
             def _():
                 down(j + 1).wait_send()
+                for q in range(4):
+                    last_down(j + 1, q).wait_send()
 
     @pl.when(core == 0)
     def _():

time: 532 us -> 522 us (0.981)
  Pallas kernels: 521 us -> 512 us
    pallas_call x1, Pallas kernels: 137 us -> 127 us  [gather_slots(): pl.pallas_call(functools.partial(gather_kernel, slots), out_shape=[jax.Sh...]
where the time goes in v6:
time: 522 us; the launch traced here: 521 us
  Pallas kernels  512 us (98%)
    pallas_call x1, Pallas kernels, reduce_slots(): pl.pallas_call(functools.partial(reduce_kernel, slots), out_shape=[jax.Sh...  140 us
    pallas_call x1, Pallas kernels, gather_slots(): pl.pallas_call(functools.partial(gather_kernel, slots), out_shape=[jax.Sh...  127 us
    pallas_call x1, Pallas kernels, middle_part(): pl.pallas_call(functools.partial(middle_kernel, row_blocks), grid_spec=pl...  94.8 us
    pallas_call x1, Pallas kernels, weight_grads(): pl.pallas_call(functools.partial(weight_grads_kernel, starts, col_blocks,...  36.4 us
    pallas_call x1, Pallas kernels, optimizer(): pl.pallas_call(functools.partial(optimizer_kernel, scale), grid=(slots,),...  31.6 us
    pallas_call x1, Pallas kernels, attention_back(): pl.pallas_call(functools.partial(attention_back_kernel, head ** (-0.5), h...  24.3 us
    pallas_call x1, Pallas kernels, front(): pl.pallas_call(front_kernel, grid_spec=pltpu.PrefetchScalarGridSpec(num_s...  20.9 us
    pallas_call x1, Pallas kernels, weight_grad(): pl.pallas_call(functools.partial(weight_grad_kernel, block_of, deep, size...  17 us

profile of v6, /device:TPU:0, one launch (start us, length us, event | category | flops | bytes accessed | tf_op | source)
XLA Modules:
  0.0 521.3 jit_solution(4718397354770986590)
XLA Ops:
  1.3 0.6 pad_add_fusion.start
  1.9 0.1 pad.10.clone
  2.0 0.7 compare_select_fusion.1
  2.7 1.7 scatter_custom_fusion.slot_of
  4.4 0.1 broadcast_bitcast_fusion
  4.5 0.7 compare_select_fusion
  5.3 0.1 stack.53
  5.4 0.1 maximum_bitcast_fusion
  5.4 1.3 pad_maximum_fusion.extras
  6.8 0.8 fusion.6
  7.6 0.6 pad_maximum_fusion.1
  8.2 1.1 copy.27.params
  9.3 5.2 %pack_slots.1.placed = bf16[192,312,256]{2,1,0:T(8,128)(2,1)} custom-call(s32[2]{0:T(128)} %pad_add_fusion.start, bf16[12,280,280]{2,1,0:T(8,128)(2,1)} %block.1), custom_call_target="tpu_custom_call" | custom-call | tf_op jit(solution)/shard_map/pack_slots/pallas_call | solution.py:86
  14.5 127.2 %gather_slots.1 = (bf16[192,312,256]{2,1,0:T(8,128)(2,1)}, bf16[1120,1152]{1,0:T(8,128)(2,1)}) custom-call(bf16[192,312,256]{2,1,0:T(8,128)(2,1)} %pack_slots.1.placed, bf16[1120,1024]{1,0:T(8,128)(2,1)} %bitcast.30, f32[1120,4]{1,0:T(8,128)} %copy.27.params), custom_call_target="tpu_custom_call", output_to_operand_aliasing={{0}: (0, {})} | custom-call | tf_op jit(solution)/shard_map/gather_slots/pallas_call | solution.py:381
  141.8 20.9 %front.1 = (bf16[3,1120,1120]{2,1,0:T(8,128)(2,1)}, bf16[3,1120,1152]{2,1,0:T(8,128)(2,1)}) custom-call(s32[192]{0:T(256)} %scatter_custom_fusion.slot_of, bf16[1120,1152]{1,0:T(8,128)(2,1)} %get-tuple-element.36.normed.left, ...), custom_call_target="tpu_custom_call" | custom-call | tf_op jit(solution)/shard_map/front/pallas_call | solution.py:760
  162.7 13.9 %attention.1 = (bf16[1120,1024]{1,0:T(8,128)(2,1)}, f32[20,1,1024]{2,1,0:T(1,128)}) custom-call(bf16[3,1120,1152]{2,1,0:T(8,128)(2,1)} %get-tuple-element.38.qkv, bf16[3,8,1152]{2,1,0:T(8,128)(2,1)} %pad_maximum_fusion.extras), custom_call_target="tpu_custom_call" | custom-call | flops 2348810240 | bytes 7741440 | tf_op jit(solution)/shard_map/attention/pallas_call | solution.py:1254
  176.6 94.8 %middle_part.1 = (bf16[1120,1024]{1,0:T(8,128)(2,1)}, bf16[4480,1024]{1,0:T(8,128)(2,1)}, bf16[4480,1024]{1,0:T(8,128)(2,1)}, bf16[1120,1024]{1,0:T(8,128)(2,1)}...) custom-call(s32[192]{0:T(256)} %scatter_custom_fusion.slot_of, ...), custom_call_target="tpu_custom_call" | custom-call | tf_op jit(solution)/shard_map/middle_part/pallas_call | solution.py:890
  271.5 24.3 %attention_back.1.grad_three = bf16[3,1120,1152]{2,1,0:T(8,128)(2,1)} custom-call(bf16[3,1120,1152]{2,1,0:T(8,128)(2,1)} %get-tuple-element.38.qkv, bf16[3,8,1152]{2,1,0:T(8,128)(2,1)} %pad_maximum_fusion.extras, bf16[1120,1024]{1,0:T(8,128)(2,1)} %get-tuple-element.39.attended.out.refs_4_, f32[20,1,1024]{2,1,0:T(1,128)} %get-tuple-element.41.lse, ...), custom_call_target="tpu_custom_call" | custom-call | flops 5872025600 | bytes 15482880 | tf_op jit(solution)/shard_map/attention_back/pallas_call | solution.py:1271
  295.7 36.4 %weight_grads.1.refs_0_ = bf16[192,312,256]{2,1,0:T(8,128)(2,1)} custom-call(s32[192]{0:T(256)} %scatter_custom_fusion.slot_of, bf16[4480,1024]{1,0:T(8,128)(2,1)} %get-tuple-element.43.refs_0_, bf16[1120,1024]{1,0:T(8,128)(2,1)} %bitcast.34, bf16[1120,1024]{1,0:T(8,128)(2,1)} %get-tuple-element.44.refs_2_, bf16[4480,1024]{1,0:T(8,128)(2,1)} %get-tuple-element.45.refs_3_, ...), custom_call_target="tpu_custom_call" | custom-call | flops 23121100800 | bytes 82575360 | tf_op jit(solution)/shard_map/weight_grads/pallas_call | solution.py:1068
  332.1 17.0 %grad_three.1.grads = bf16[192,312,256]{2,1,0:T(8,128)(2,1)} custom-call(s32[192]{0:T(256)} %scatter_custom_fusion.slot_of, bf16[1120,1152]{1,0:T(8,128)(2,1)} %get-tuple-element.36.normed.left, bf16[3360,1152]{1,0:T(8,128)(2,1)} %bitcast.29, bf16[192,312,256]{2,1,0:T(8,128)(2,1)} %weight_grads.1.refs_0_), custom_call_target="tpu_custom_call", output_to_operand_aliasing={{}: (3, {})} | custom-call | flops 8670412800 | bytes 17848320 | tf_op jit(solution)/shard_map/grad_three/pallas_call | solution.py:965
  349.2 140.4 %reduce_slots.1 = (f32[12,312,256]{2,1,0:T(8,128)}, f32[1120,1024]{1,0:T(8,128)}, f32[8,1120]{1,0:T(8,128)}) custom-call(bf16[192,312,256]{2,1,0:T(8,128)(2,1)} %grad_three.1.grads, bf16[3,1120,1120]{2,1,0:T(8,128)(2,1)} %get-tuple-element.47.w_three, bf16[3,1120,1152]{2,1,0:T(8,128)(2,1)} %attention_back.1.grad_three, bf16[1120,1024]{1,0:T(8,128)(2,1)} %bitcast.32, ...), custom_call_target="tpu_custom_call" | custom-call | tf_op jit(solution)/shard_map/reduce_slots/pallas_call | solution.py:677
  489.5 31.6 %optimizer.1 = (f32[12,280,280]{2,1,0:T(8,128)}, f32[12,280,280]{2,1,0:T(8,128)}, f32[12,280,280]{2,1,0:T(8,128)}, f32[12,280,280]{2,1,0:T(8,128)}, bf16[12,280,...) custom-call(f32[12,312,256]{2,1,0:T(8,128)} %get-tuple-element.50.pa, ...), custom_call_target="tpu_custom_call" | custom-call | tf_op jit(solution)/shard_map/optimizer/pallas_call | solution.py:1340
  (13 shorter events, 0.1 us)

commit v7 on v6

--- a/solution.py
+++ b/solution.py
@@ -243,6 +243,29 @@
         return carry
 
     lax.fori_loop(0, held.shape[1] // PREFIX, normalize, 0)
+    def pass_last(j):
+        for q in range(4):
+
+            @pl.when(z >= j)
+            def _():
+                last_up(j, q).wait_recv()
+                last_twin(me - 4 * j + off(q)).start()
+                if j < 3:
+
+                    @pl.when(z < 3)
+                    def _():
+                        last_up(j + 1, q).start()
+
+            @pl.when(z + j <= 3)
+            def _():
+                last_down(j, q).wait_recv()
+                last_twin(me + 4 * j + off(q)).start()
+                if j < 3:
+
+                    @pl.when(z > 0)
+                    def _():
+                        last_down(j + 1, q).start()
+
     last_first().wait_recv()
     last_second(1).start()
     leave_plane(1)
@@ -287,27 +310,8 @@
         if j == 1:
             last_second(1).wait_recv()
             leave_plane(3)
-        for q in range(4):
-
-            @pl.when(z >= j)
-            def _():
-                last_up(j, q).wait_recv()
-                last_twin(me - 4 * j + off(q)).start()
-                if j < 3:
-
-                    @pl.when(z < 3)
-                    def _():
-                        last_up(j + 1, q).start()
-
-            @pl.when(z + j <= 3)
-            def _():
-                last_down(j, q).wait_recv()
-                last_twin(me + 4 * j + off(q)).start()
-                if j < 3:
-
-                    @pl.when(z > 0)
-                    def _():
-                        last_down(j + 1, q).start()
+        else:
+            pass_last(j - 1)
 
     @pl.when(z >= 3)
     def _():
@@ -317,6 +321,7 @@
     def _():
         after_first(z + 3)
 
+    pass_last(3)
     after_second(z)
     for j in range(1, 4):
 

time: 522 us -> 516 us (0.989)
  Pallas kernels: 512 us -> 506 us
    pallas_call x1, Pallas kernels: 127 us -> 121 us  [gather_slots(): pl.pallas_call(functools.partial(gather_kernel, slots), out_shape=[jax.Sh...]
where the time goes in v7:
time: 516 us; the launch traced here: 515 us
  Pallas kernels  506 us (98%)
    pallas_call x1, Pallas kernels, reduce_slots(): pl.pallas_call(functools.partial(reduce_kernel, slots), out_shape=[jax.Sh...  140 us
    pallas_call x1, Pallas kernels, gather_slots(): pl.pallas_call(functools.partial(gather_kernel, slots), out_shape=[jax.Sh...  121 us
    pallas_call x1, Pallas kernels, middle_part(): pl.pallas_call(functools.partial(middle_kernel, row_blocks), grid_spec=pl...  94.8 us
    pallas_call x1, Pallas kernels, weight_grads(): pl.pallas_call(functools.partial(weight_grads_kernel, starts, col_blocks,...  36.4 us
    pallas_call x1, Pallas kernels, optimizer(): pl.pallas_call(functools.partial(optimizer_kernel, scale), grid=(slots,),...  31.6 us
    pallas_call x1, Pallas kernels, attention_back(): pl.pallas_call(functools.partial(attention_back_kernel, head ** (-0.5), h...  24.3 us
    pallas_call x1, Pallas kernels, front(): pl.pallas_call(front_kernel, grid_spec=pltpu.PrefetchScalarGridSpec(num_s...  20.9 us
    pallas_call x1, Pallas kernels, weight_grad(): pl.pallas_call(functools.partial(weight_grad_kernel, block_of, deep, size...  17 us

profile of v7, /device:TPU:0, one launch (start us, length us, event | category | flops | bytes accessed | tf_op | source)
XLA Modules:
  0.0 515.4 jit_solution(15533930765193633781)
XLA Ops:
  1.3 0.6 pad_add_fusion.start
  1.9 0.1 pad.10.clone
  2.0 0.7 compare_select_fusion.1
  2.7 1.7 scatter_custom_fusion.slot_of
  4.4 0.1 broadcast_bitcast_fusion
  4.5 0.7 compare_select_fusion
  5.3 0.1 stack.53
  5.4 0.1 maximum_bitcast_fusion
  5.4 1.3 pad_maximum_fusion.extras
  6.8 0.8 fusion.6
  7.6 0.6 pad_maximum_fusion.1
  8.2 1.1 copy.27.params
  9.3 5.2 %pack_slots.1.placed = bf16[192,312,256]{2,1,0:T(8,128)(2,1)} custom-call(s32[2]{0:T(128)} %pad_add_fusion.start, bf16[12,280,280]{2,1,0:T(8,128)(2,1)} %block.1), custom_call_target="tpu_custom_call" | custom-call | tf_op jit(solution)/shard_map/pack_slots/pallas_call | solution.py:86
  14.5 121.4 %gather_slots.1 = (bf16[192,312,256]{2,1,0:T(8,128)(2,1)}, bf16[1120,1152]{1,0:T(8,128)(2,1)}) custom-call(bf16[192,312,256]{2,1,0:T(8,128)(2,1)} %pack_slots.1.placed, bf16[1120,1024]{1,0:T(8,128)(2,1)} %bitcast.30, f32[1120,4]{1,0:T(8,128)} %copy.27.params), custom_call_target="tpu_custom_call", output_to_operand_aliasing={{0}: (0, {})} | custom-call | tf_op jit(solution)/shard_map/gather_slots/pallas_call | solution.py:386
  135.9 20.9 %front.1 = (bf16[3,1120,1120]{2,1,0:T(8,128)(2,1)}, bf16[3,1120,1152]{2,1,0:T(8,128)(2,1)}) custom-call(s32[192]{0:T(256)} %scatter_custom_fusion.slot_of, bf16[1120,1152]{1,0:T(8,128)(2,1)} %get-tuple-element.36.normed.left, ...), custom_call_target="tpu_custom_call" | custom-call | tf_op jit(solution)/shard_map/front/pallas_call | solution.py:765
  156.8 13.9 %attention.1 = (bf16[1120,1024]{1,0:T(8,128)(2,1)}, f32[20,1,1024]{2,1,0:T(1,128)}) custom-call(bf16[3,1120,1152]{2,1,0:T(8,128)(2,1)} %get-tuple-element.38.qkv, bf16[3,8,1152]{2,1,0:T(8,128)(2,1)} %pad_maximum_fusion.extras), custom_call_target="tpu_custom_call" | custom-call | flops 2348810240 | bytes 7741440 | tf_op jit(solution)/shard_map/attention/pallas_call | solution.py:1259
  170.8 94.8 %middle_part.1 = (bf16[1120,1024]{1,0:T(8,128)(2,1)}, bf16[4480,1024]{1,0:T(8,128)(2,1)}, bf16[4480,1024]{1,0:T(8,128)(2,1)}, bf16[1120,1024]{1,0:T(8,128)(2,1)}...) custom-call(s32[192]{0:T(256)} %scatter_custom_fusion.slot_of, ...), custom_call_target="tpu_custom_call" | custom-call | tf_op jit(solution)/shard_map/middle_part/pallas_call | solution.py:895
  265.6 24.3 %attention_back.1.grad_three = bf16[3,1120,1152]{2,1,0:T(8,128)(2,1)} custom-call(bf16[3,1120,1152]{2,1,0:T(8,128)(2,1)} %get-tuple-element.38.qkv, bf16[3,8,1152]{2,1,0:T(8,128)(2,1)} %pad_maximum_fusion.extras, bf16[1120,1024]{1,0:T(8,128)(2,1)} %get-tuple-element.39.attended.out.refs_4_, f32[20,1,1024]{2,1,0:T(1,128)} %get-tuple-element.41.lse, ...), custom_call_target="tpu_custom_call" | custom-call | flops 5872025600 | bytes 15482880 | tf_op jit(solution)/shard_map/attention_back/pallas_call | solution.py:1276
  289.9 36.4 %weight_grads.1.refs_0_ = bf16[192,312,256]{2,1,0:T(8,128)(2,1)} custom-call(s32[192]{0:T(256)} %scatter_custom_fusion.slot_of, bf16[4480,1024]{1,0:T(8,128)(2,1)} %get-tuple-element.43.refs_0_, bf16[1120,1024]{1,0:T(8,128)(2,1)} %bitcast.34, bf16[1120,1024]{1,0:T(8,128)(2,1)} %get-tuple-element.44.refs_2_, bf16[4480,1024]{1,0:T(8,128)(2,1)} %get-tuple-element.45.refs_3_, ...), custom_call_target="tpu_custom_call" | custom-call | flops 23121100800 | bytes 82575360 | tf_op jit(solution)/shard_map/weight_grads/pallas_call | solution.py:1073
  326.2 17.0 %grad_three.1.grads = bf16[192,312,256]{2,1,0:T(8,128)(2,1)} custom-call(s32[192]{0:T(256)} %scatter_custom_fusion.slot_of, bf16[1120,1152]{1,0:T(8,128)(2,1)} %get-tuple-element.36.normed.left, bf16[3360,1152]{1,0:T(8,128)(2,1)} %bitcast.29, bf16[192,312,256]{2,1,0:T(8,128)(2,1)} %weight_grads.1.refs_0_), custom_call_target="tpu_custom_call", output_to_operand_aliasing={{}: (3, {})} | custom-call | flops 8670412800 | bytes 17848320 | tf_op jit(solution)/shard_map/grad_three/pallas_call | solution.py:970
  343.3 140.3 %reduce_slots.1 = (f32[12,312,256]{2,1,0:T(8,128)}, f32[1120,1024]{1,0:T(8,128)}, f32[8,1120]{1,0:T(8,128)}) custom-call(bf16[192,312,256]{2,1,0:T(8,128)(2,1)} %grad_three.1.grads, bf16[3,1120,1120]{2,1,0:T(8,128)(2,1)} %get-tuple-element.47.w_three, bf16[3,1120,1152]{2,1,0:T(8,128)(2,1)} %attention_back.1.grad_three, bf16[1120,1024]{1,0:T(8,128)(2,1)} %bitcast.32, ...), custom_call_target="tpu_custom_call" | custom-call | tf_op jit(solution)/shard_map/reduce_slots/pallas_call | solution.py:682
  483.6 31.6 %optimizer.1 = (f32[12,280,280]{2,1,0:T(8,128)}, f32[12,280,280]{2,1,0:T(8,128)}, f32[12,280,280]{2,1,0:T(8,128)}, f32[12,280,280]{2,1,0:T(8,128)}, bf16[12,280,...) custom-call(f32[12,312,256]{2,1,0:T(8,128)} %get-tuple-element.50.pa, ...), custom_call_target="tpu_custom_call" | custom-call | tf_op jit(solution)/shard_map/optimizer/pallas_call | solution.py:1345
  (13 shorter events, 0.1 us)

commit v8 on v7

--- a/solution.py
+++ b/solution.py
@@ -321,7 +321,6 @@
     def _():
         after_first(z + 3)
 
-    pass_last(3)
     after_second(z)
     for j in range(1, 4):
 
@@ -333,6 +332,7 @@
         def _():
             after_second(z + j)
 
+    pass_last(3)
     for zz in range(4):
         for a in range(2):
             for b in range(2):

time: 516 us -> 517 us (level)
  no operation moved by 1% of the time
where the time goes in v8:
time: 517 us; the launch traced here: 516 us
  Pallas kernels  507 us (98%)
    pallas_call x1, Pallas kernels, reduce_slots(): pl.pallas_call(functools.partial(reduce_kernel, slots), out_shape=[jax.Sh...  140 us
    pallas_call x1, Pallas kernels, gather_slots(): pl.pallas_call(functools.partial(gather_kernel, slots), out_shape=[jax.Sh...  122 us
    pallas_call x1, Pallas kernels, middle_part(): pl.pallas_call(functools.partial(middle_kernel, row_blocks), grid_spec=pl...  94.8 us
    pallas_call x1, Pallas kernels, weight_grads(): pl.pallas_call(functools.partial(weight_grads_kernel, starts, col_blocks,...  36.4 us
    pallas_call x1, Pallas kernels, optimizer(): pl.pallas_call(functools.partial(optimizer_kernel, scale), grid=(slots,),...  31.6 us
    pallas_call x1, Pallas kernels, attention_back(): pl.pallas_call(functools.partial(attention_back_kernel, head ** (-0.5), h...  24.3 us
    pallas_call x1, Pallas kernels, front(): pl.pallas_call(front_kernel, grid_spec=pltpu.PrefetchScalarGridSpec(num_s...  20.9 us
    pallas_call x1, Pallas kernels, weight_grad(): pl.pallas_call(functools.partial(weight_grad_kernel, block_of, deep, size...  17.1 us

profile of v8, /device:TPU:0, one launch (start us, length us, event | category | flops | bytes accessed | tf_op | source)
XLA Modules:
  0.0 516.3 jit_solution(14062882874490136707)
XLA Ops:
  1.3 0.6 pad_add_fusion.start
  1.9 0.1 pad.10.clone
  2.0 0.7 compare_select_fusion.1
  2.7 1.7 scatter_custom_fusion.slot_of
  4.4 0.1 broadcast_bitcast_fusion
  4.5 0.7 compare_select_fusion
  5.3 0.1 stack.53
  5.4 0.1 maximum_bitcast_fusion
  5.4 1.3 pad_maximum_fusion.extras
  6.8 0.8 fusion.6
  7.6 0.6 pad_maximum_fusion.1
  8.2 1.1 copy.27.params
  9.3 5.2 %pack_slots.1.placed = bf16[192,312,256]{2,1,0:T(8,128)(2,1)} custom-call(s32[2]{0:T(128)} %pad_add_fusion.start, bf16[12,280,280]{2,1,0:T(8,128)(2,1)} %block.1), custom_call_target="tpu_custom_call" | custom-call | tf_op jit(solution)/shard_map/pack_slots/pallas_call | solution.py:86
  14.5 122.3 %gather_slots.1 = (bf16[192,312,256]{2,1,0:T(8,128)(2,1)}, bf16[1120,1152]{1,0:T(8,128)(2,1)}) custom-call(bf16[192,312,256]{2,1,0:T(8,128)(2,1)} %pack_slots.1.placed, bf16[1120,1024]{1,0:T(8,128)(2,1)} %bitcast.30, f32[1120,4]{1,0:T(8,128)} %copy.27.params), custom_call_target="tpu_custom_call", output_to_operand_aliasing={{0}: (0, {})} | custom-call | tf_op jit(solution)/shard_map/gather_slots/pallas_call | solution.py:386
  136.8 20.9 %front.1 = (bf16[3,1120,1120]{2,1,0:T(8,128)(2,1)}, bf16[3,1120,1152]{2,1,0:T(8,128)(2,1)}) custom-call(s32[192]{0:T(256)} %scatter_custom_fusion.slot_of, bf16[1120,1152]{1,0:T(8,128)(2,1)} %get-tuple-element.36.normed.left, ...), custom_call_target="tpu_custom_call" | custom-call | tf_op jit(solution)/shard_map/front/pallas_call | solution.py:765
  157.8 13.9 %attention.1 = (bf16[1120,1024]{1,0:T(8,128)(2,1)}, f32[20,1,1024]{2,1,0:T(1,128)}) custom-call(bf16[3,1120,1152]{2,1,0:T(8,128)(2,1)} %get-tuple-element.38.qkv, bf16[3,8,1152]{2,1,0:T(8,128)(2,1)} %pad_maximum_fusion.extras), custom_call_target="tpu_custom_call" | custom-call | flops 2348810240 | bytes 7741440 | tf_op jit(solution)/shard_map/attention/pallas_call | solution.py:1259
  171.7 94.8 %middle_part.1 = (bf16[1120,1024]{1,0:T(8,128)(2,1)}, bf16[4480,1024]{1,0:T(8,128)(2,1)}, bf16[4480,1024]{1,0:T(8,128)(2,1)}, bf16[1120,1024]{1,0:T(8,128)(2,1)}...) custom-call(s32[192]{0:T(256)} %scatter_custom_fusion.slot_of, ...), custom_call_target="tpu_custom_call" | custom-call | tf_op jit(solution)/shard_map/middle_part/pallas_call | solution.py:895
  266.5 24.3 %attention_back.1.grad_three = bf16[3,1120,1152]{2,1,0:T(8,128)(2,1)} custom-call(bf16[3,1120,1152]{2,1,0:T(8,128)(2,1)} %get-tuple-element.38.qkv, bf16[3,8,1152]{2,1,0:T(8,128)(2,1)} %pad_maximum_fusion.extras, bf16[1120,1024]{1,0:T(8,128)(2,1)} %get-tuple-element.39.attended.out.refs_4_, f32[20,1,1024]{2,1,0:T(1,128)} %get-tuple-element.41.lse, ...), custom_call_target="tpu_custom_call" | custom-call | flops 5872025600 | bytes 15482880 | tf_op jit(solution)/shard_map/attention_back/pallas_call | solution.py:1276
  290.8 36.4 %weight_grads.1.refs_0_ = bf16[192,312,256]{2,1,0:T(8,128)(2,1)} custom-call(s32[192]{0:T(256)} %scatter_custom_fusion.slot_of, bf16[4480,1024]{1,0:T(8,128)(2,1)} %get-tuple-element.43.refs_0_, bf16[1120,1024]{1,0:T(8,128)(2,1)} %bitcast.34, bf16[1120,1024]{1,0:T(8,128)(2,1)} %get-tuple-element.44.refs_2_, bf16[4480,1024]{1,0:T(8,128)(2,1)} %get-tuple-element.45.refs_3_, ...), custom_call_target="tpu_custom_call" | custom-call | flops 23121100800 | bytes 82575360 | tf_op jit(solution)/shard_map/weight_grads/pallas_call | solution.py:1073
  327.2 17.1 %grad_three.1.grads = bf16[192,312,256]{2,1,0:T(8,128)(2,1)} custom-call(s32[192]{0:T(256)} %scatter_custom_fusion.slot_of, bf16[1120,1152]{1,0:T(8,128)(2,1)} %get-tuple-element.36.normed.left, bf16[3360,1152]{1,0:T(8,128)(2,1)} %bitcast.29, bf16[192,312,256]{2,1,0:T(8,128)(2,1)} %weight_grads.1.refs_0_), custom_call_target="tpu_custom_call", output_to_operand_aliasing={{}: (3, {})} | custom-call | flops 8670412800 | bytes 17848320 | tf_op jit(solution)/shard_map/grad_three/pallas_call | solution.py:970
  344.2 140.3 %reduce_slots.1 = (f32[12,312,256]{2,1,0:T(8,128)}, f32[1120,1024]{1,0:T(8,128)}, f32[8,1120]{1,0:T(8,128)}) custom-call(bf16[192,312,256]{2,1,0:T(8,128)(2,1)} %grad_three.1.grads, bf16[3,1120,1120]{2,1,0:T(8,128)(2,1)} %get-tuple-element.47.w_three, bf16[3,1120,1152]{2,1,0:T(8,128)(2,1)} %attention_back.1.grad_three, bf16[1120,1024]{1,0:T(8,128)(2,1)} %bitcast.32, ...), custom_call_target="tpu_custom_call" | custom-call | tf_op jit(solution)/shard_map/reduce_slots/pallas_call | solution.py:682
  484.6 31.6 %optimizer.1 = (f32[12,280,280]{2,1,0:T(8,128)}, f32[12,280,280]{2,1,0:T(8,128)}, f32[12,280,280]{2,1,0:T(8,128)}, f32[12,280,280]{2,1,0:T(8,128)}, bf16[12,280,...) custom-call(f32[12,312,256]{2,1,0:T(8,128)} %get-tuple-element.50.pa, ...), custom_call_target="tpu_custom_call" | custom-call | tf_op jit(solution)/shard_map/optimizer/pallas_call | solution.py:1345
  (13 shorter events, 0.1 us)
